TPU v7x, 32 devices: a whole 2x2x4 slice. The times are simulated.
32 devices in a mesh: parts: 2 (over y), src: 4 (over x, core), space: 4 (over z).
Axes of the slice: x: 2, y: 2, z: 4, core: 2. Of those that a mesh axis runs over, the one named last changes fastest.
Arguments:
- fields: float32 [8, 4, 16, 128, 128], P(('parts', 'src'), None, 'space'), parts along dimension 0, may hold values from -6 to 6
- velocity: float32 [32, 128, 128], P(('parts', 'space')), parts along dimension 0, may hold values from 0.5 to 1
- conductivity: float32 [32, 128, 128], P(('parts', 'space')), parts along dimension 0, may hold values from 1 to 4
- labels: int32 [8], P(('parts', 'src')), parts along dimension 0, may hold values from 0 to 1, as said below
Outputs:
- fields_out: float32 [8, 2, 16, 128, 128], P(('parts', 'src'), None, 'space'), parts along dimension 0
- models_out: float32 [2, 32, 128, 128], P(None, ('parts', 'space')), parts along dimension 1
There are 2 independent parts, one for each index of `parts`. A program takes and returns all parts, laid end to end along the dimension named above; each array names one. Nothing has to cross between parts.
Inputs may be any that keep to these rules, and one draw needn't show every extreme that they name: `labels`: at least one group has label 0 and at least one has label 1; the rest are drawn.
All inputs are finite; a program needn't handle non-finite values.
Results may differ from a plain program's by a relative error of at most 0.00002.
Values sent between devices are 32-bit elements; how exact they have to be, the bound alone decides.
No kernel may reach another device: no remote copies, remote signals or barrier semaphores. Data moves between devices by JAX's collectives and lax.ppermute only.
A program may use at most 64 MiB of HBM per device.

v0:
```python
import jax
import jax.numpy as jnp
from jax import lax
from jax.sharding import PartitionSpec as P

STEPS = 3


speed_gain = 0.25
diffuse_gain = 0.15
step_size = 0.1
penalty_gain = 50.0


def extended_2(block, sides, width):
    for axis, dim in sides:
        count = lax.axis_size(axis)
        forward = [(i, i + 1) for i in range(count - 1)]
        backward = [(target, source) for source, target in forward]
        low = lax.ppermute(
            lax.slice_in_dim(block, block.shape[dim] - width, None, axis=dim), axis, forward
        )
        high = lax.ppermute(lax.slice_in_dim(block, 0, width, axis=dim), axis, backward)
        block = jnp.concatenate([low, block, high], axis=dim)
    return block


def neighbours(padded):
    middle = padded[..., 1:-1, :, :]
    total = padded[..., 2:, :, :] + padded[..., :-2, :, :]
    zero_y = jnp.zeros_like(middle[..., :1, :])
    total = (
        total
        + jnp.concatenate([middle[..., 1:, :], zero_y], -2)
        + jnp.concatenate([zero_y, middle[..., :-1, :]], -2)
    )
    zero_z = jnp.zeros_like(middle[..., :1])
    total = (
        total
        + jnp.concatenate([middle[..., 1:], zero_z], -1)
        + jnp.concatenate([zero_z, middle[..., :-1]], -1)
    )
    return total - 6.0 * middle


def coefficient(weight, velocity, conductivity):
    return weight * speed_gain * velocity**2 + (1.0 - weight) * diffuse_gain / conductivity


def advance_thin(state, coef, weight):
    upper, upper_prev, lower, lower_prev = state
    accum = jnp.zeros_like(upper)
    for step in range(STEPS):
        padded = extended_2(jnp.stack([upper, lower], 1), (("space", 2),), 1)
        laps = neighbours(padded)
        lap_upper = laps[:, 0]
        lap_lower = laps[:, 1]
        accum = accum + lower * lap_upper
        upper_next = weight * (2.0 * upper - upper_prev) + (1.0 - weight) * upper + coef * lap_upper
        lower_next = weight * (2.0 * lower - lower_prev) + (1.0 - weight) * lower + coef * lap_lower
        upper_prev, upper = (upper, upper_next)
        lower_prev, lower = (lower, lower_next)
    return ((upper, upper_prev, lower, lower_prev), accum)


def advance(state, coef, weight):
    return advance_thin(state, coef, weight)


def penalty_term(velocity, conductivity):
    models = jnp.stack([velocity, jnp.log(conductivity)], 0)
    padded = extended_2(models, (("space", 1),), 1)
    middle = padded[:, 1:-1]
    first_idx = lax.axis_index("space")
    count = lax.axis_size("space")
    below = jnp.where(first_idx == 0, middle[:, :1], padded[:, :1])
    above = jnp.where(first_idx == count - 1, middle[:, -1:], padded[:, -1:])
    extended = jnp.concatenate([below, middle, above], 1)
    along_x = (extended[:, 2:] - extended[:, :-2]) * 0.5
    side = jnp.pad(middle, ((0, 0), (0, 0), (1, 1), (1, 1)), mode="edge")
    along_y = (side[:, :, 2:, 1:-1] - side[:, :, :-2, 1:-1]) * 0.5
    along_z = (side[:, :, 1:-1, 2:] - side[:, :, 1:-1, :-2]) * 0.5
    vx, lx = (along_x[0], along_x[1])
    vy, ly = (along_y[0], along_y[1])
    vz, lz = (along_z[0], along_z[1])
    cross_a = vy * lz - vz * ly
    cross_b = vz * lx - vx * lz
    cross_c = vx * ly - vy * lx
    return penalty_gain * (cross_a * cross_a + cross_b * cross_b + cross_c * cross_c)


def renew(velocity, conductivity, gradient, penalty):
    new_velocity = velocity * jnp.exp(-step_size * jnp.tanh(gradient[0] + penalty))
    new_conductivity = conductivity * jnp.exp(-step_size * jnp.tanh(gradient[1] + penalty))
    return jnp.stack([new_velocity, new_conductivity], 0)


def shards(fields, velocity, conductivity, labels):
    weight = labels.astype(jnp.float32).reshape(-1, 1, 1, 1)
    coef = coefficient(weight, velocity, conductivity)
    state = (fields[:, 0], fields[:, 1], fields[:, 2], fields[:, 3])
    state, accum = advance(state, coef, weight)
    penalty = penalty_term(velocity, conductivity)
    partial_sum = jnp.stack([jnp.sum(weight * accum, 0), jnp.sum((1.0 - weight) * accum, 0)], 0)
    groups_all = labels.shape[0] * lax.axis_size("src")
    scale = 1.0 / (20.0 * jnp.sqrt(jnp.float32(groups_all)))
    share = lax.psum_scatter(partial_sum, "src", scatter_dimension=2, tiled=True)
    band = share.shape[2]
    offset = lax.axis_index("src") * band
    vel_band = lax.dynamic_slice_in_dim(velocity, offset, band, 1)
    cond_band = lax.dynamic_slice_in_dim(conductivity, offset, band, 1)
    pen_band = lax.dynamic_slice_in_dim(penalty, offset, band, 1)
    fresh = renew(vel_band, cond_band, scale * share, pen_band)
    updated = lax.all_gather(fresh, "src", axis=2, tiled=True)
    coef_next = coefficient(weight, updated[0], updated[1])
    final, unused = advance(state, coef_next, weight)
    return (jnp.stack([final[0], final[2]], 1), updated)


def solution(mesh):
    in_specs = (
        P(("parts", "src"), None, "space", None, None),
        P(("parts", "space"), None, None),
        P(("parts", "space"), None, None),
        P(("parts", "src")),
    )
    out_specs = (
        P(("parts", "src"), None, "space", None, None),
        P(None, ("parts", "space"), None, None),
    )
    return jax.shard_map(shards, mesh=mesh, in_specs=in_specs, out_specs=out_specs, check_vma=False)
```

profile of v0, /device:TPU:0, one launch (start us, length us, event | category | flops | bytes accessed | tf_op | source)
XLA Modules:
  0.0 106.2 jit_solution(3605257124550417940)
XLA Ops:
  7.2 1.1 %fusion.140 = (f32[1,1,4,128,128]{4,3,2,1,0:T(8,128)S(1)}, f32[1,1,4,128,128]{4,3,2,1,0:T(8,128)S(1)}) fusion(f32[1,4,4,128,128]{4,3,2,1,0:T(8,128)} %param.4), kind=kLoop, calls=%fused_computation.300 | loop fusion | bytes 1048576 | tf_op jit(solution)/shard_map/slice | solution.py:101
  8.3 5.0 %collective-permute-start.1 = (f32[1,2,1,128,128]{4,3,2,1,0:T(8,128)S(1)}, f32[1,2,1,128,128]{4,3,2,1,0:T(8,128)S(1)}, u32[]{:S(2)}, u32[]{:S(2)}) collective-permute-start(f32[1,2,1,128,128]{4,3,2,1,0:T(8,128)S(1)} %get-tuple-element.69), channel_id=1, source_target_pairs={{0,1},{1,2},{2,3},{4,5},{5,6},{6,7},{8,9},{9,10},{10,11},{12,13},{... | collective-permute-start | bytes 393224 | tf_op jit(solution)/shard_map/ppermute | solution.py:20
  13.3 1.3 %collective-permute-start = (f32[1,2,1,128,128]{4,3,2,1,0:T(8,128)S(1)}, f32[1,2,1,128,128]{4,3,2,1,0:T(8,128)S(1)}, u32[]{:S(2)}, u32[]{:S(2)}) collective-permute-start(f32[1,2,1,128,128]{4,3,2,1,0:T(8,128)S(1)} %get-tuple-element.68), channel_id=1, source_target_pairs={{1,0},{2,1},{3,2},{5,4},{6,5},{7,6},{9,8},{10,9},{11,10},{13,12},{... | collective-permute-start | bytes 393224 | tf_op jit(solution)/shard_map/ppermute | solution.py:23
  15.5 0.5 collective-permute-done.1
  16.0 4.1 %collective-permute-done = f32[1,2,1,128,128]{4,3,2,1,0:T(8,128)S(1)} collective-permute-done((f32[1,2,1,128,128]{4,3,2,1,0:T(8,128)S(1)}, f32[1,2,1,128,128]{4,3,2,1,0:T(8,128)S(1)}, u32[]{:S(2)}, u32[]{:S(2)}) %collective-permute-start) | collective-permute-done | bytes 131104 | tf_op jit(solution)/shard_map/ppermute | solution.py:23
  20.1 0.3 fusion.35
  20.5 0.6 copy-done
  21.1 0.4 copy-done.1
  22.0 3.5 %collective-permute-start.3 = (f32[1,2,1,128,128]{4,3,2,1,0:T(8,128)S(1)}, f32[1,2,1,128,128]{4,3,2,1,0:T(8,128)S(1)}, u32[]{:S(2)}, u32[]{:S(2)}) collective-permute-start(f32[1,2,1,128,128]{4,3,2,1,0:T(8,128)S(1)} %get-tuple-element.63), channel_id=1, source_target_pairs={{0,1},{1,2},{2,3},{4,5},{5,6},{6,7},{8,9},{9,10},{10,11},{12,13},{... | collective-permute-start | bytes 393224 | tf_op jit(solution)/shard_map/ppermute | solution.py:20
  25.5 1.3 %collective-permute-start.2 = (f32[1,2,1,128,128]{4,3,2,1,0:T(8,128)S(1)}, f32[1,2,1,128,128]{4,3,2,1,0:T(8,128)S(1)}, u32[]{:S(2)}, u32[]{:S(2)}) collective-permute-start(f32[1,2,1,128,128]{4,3,2,1,0:T(8,128)S(1)} %get-tuple-element.62), channel_id=1, source_target_pairs={{1,0},{2,1},{3,2},{5,4},{6,5},{7,6},{9,8},{10,9},{11,10},{13,12},{... | collective-permute-start | bytes 393224 | tf_op jit(solution)/shard_map/ppermute | solution.py:23
  26.8 1.3 %collective-permute-start.6 = (f32[2,1,128,128]{3,2,1,0:T(8,128)S(1)}, f32[2,1,128,128]{3,2,1,0:T(8,128)S(1)}, u32[]{:S(2)}, u32[]{:S(2)}) collective-permute-start(f32[2,1,128,128]{3,2,1,0:T(8,128)S(1)} %pad_maximum_fusion.49), channel_id=1, source_target_pairs={{1,0},{2,1},{3,2},{5,4},{6,5},{7,6},{9,8},{10,9},{11,10},{13,12},{... | collective-permute-start | bytes 393224 | tf_op jit(solution)/shard_map/ppermute | solution.py:23
  28.1 0.2 fusion.141
  28.3 0.5 fusion.54
  28.9 0.8 fusion.142
  29.8 3.0 %collective-permute-done.2 = f32[1,2,1,128,128]{4,3,2,1,0:T(8,128)S(1)} collective-permute-done((f32[1,2,1,128,128]{4,3,2,1,0:T(8,128)S(1)}, f32[1,2,1,128,128]{4,3,2,1,0:T(8,128)S(1)}, u32[]{:S(2)}, u32[]{:S(2)}) %collective-permute-start.2) | collective-permute-done | bytes 131104 | tf_op jit(solution)/shard_map/ppermute | solution.py:23
  32.8 0.3 fusion.29
  33.3 3.6 %collective-permute-start.5 = (f32[1,2,1,128,128]{4,3,2,1,0:T(8,128)S(1)}, f32[1,2,1,128,128]{4,3,2,1,0:T(8,128)S(1)}, u32[]{:S(2)}, u32[]{:S(2)}) collective-permute-start(f32[1,2,1,128,128]{4,3,2,1,0:T(8,128)S(1)} %get-tuple-element.57), channel_id=1, source_target_pairs={{0,1},{1,2},{2,3},{4,5},{5,6},{6,7},{8,9},{9,10},{10,11},{12,13},{... | collective-permute-start | bytes 393224 | tf_op jit(solution)/shard_map/ppermute | solution.py:20
  37.0 1.3 %collective-permute-start.4 = (f32[1,2,1,128,128]{4,3,2,1,0:T(8,128)S(1)}, f32[1,2,1,128,128]{4,3,2,1,0:T(8,128)S(1)}, u32[]{:S(2)}, u32[]{:S(2)}) collective-permute-start(f32[1,2,1,128,128]{4,3,2,1,0:T(8,128)S(1)} %get-tuple-element.56), channel_id=1, source_target_pairs={{1,0},{2,1},{3,2},{5,4},{6,5},{7,6},{9,8},{10,9},{11,10},{13,12},{... | collective-permute-start | bytes 393224 | tf_op jit(solution)/shard_map/ppermute | solution.py:23
  38.5 4.6 %collective-permute-start.7 = (f32[2,1,128,128]{3,2,1,0:T(8,128)S(1)}, f32[2,1,128,128]{3,2,1,0:T(8,128)S(1)}, u32[]{:S(2)}, u32[]{:S(2)}) collective-permute-start(f32[2,1,128,128]{3,2,1,0:T(8,128)S(1)} %get-tuple-element.11), channel_id=1, source_target_pairs={{0,1},{1,2},{2,3},{4,5},{5,6},{6,7},{8,9},{9,10},{10,11},{12,13},{... | collective-permute-start | bytes 393224 | tf_op jit(solution)/shard_map/ppermute | solution.py:20
  43.2 0.7 collective-permute-done.4
  43.8 0.3 fusion.23
  44.2 0.2 multiply_bitcast_fusion.1
  44.4 0.8 pad_maximum_fusion.47
  45.3 2.4 %collective-permute-start.9 = (f32[1,2,1,128,128]{4,3,2,1,0:T(8,128)S(1)}, f32[1,2,1,128,128]{4,3,2,1,0:T(8,128)S(1)}, u32[]{:S(2)}, u32[]{:S(2)}) collective-permute-start(f32[1,2,1,128,128]{4,3,2,1,0:T(8,128)S(1)} %get-tuple-element.51), channel_id=1, source_target_pairs={{0,1},{1,2},{2,3},{4,5},{5,6},{6,7},{8,9},{9,10},{10,11},{12,13},{... | collective-permute-start | bytes 393224 | tf_op jit(solution)/shard_map/ppermute | solution.py:20
  47.7 1.3 %collective-permute-start.8 = (f32[1,2,1,128,128]{4,3,2,1,0:T(8,128)S(1)}, f32[1,2,1,128,128]{4,3,2,1,0:T(8,128)S(1)}, u32[]{:S(2)}, u32[]{:S(2)}) collective-permute-start(f32[1,2,1,128,128]{4,3,2,1,0:T(8,128)S(1)} %get-tuple-element.50), channel_id=1, source_target_pairs={{1,0},{2,1},{3,2},{5,4},{6,5},{7,6},{9,8},{10,9},{11,10},{13,12},{... | collective-permute-start | bytes 393224 | tf_op jit(solution)/shard_map/ppermute | solution.py:23
  49.5 0.8 collective-permute-done.9
  50.2 4.4 %collective-permute-done.8 = f32[1,2,1,128,128]{4,3,2,1,0:T(8,128)S(1)} collective-permute-done((f32[1,2,1,128,128]{4,3,2,1,0:T(8,128)S(1)}, f32[1,2,1,128,128]{4,3,2,1,0:T(8,128)S(1)}, u32[]{:S(2)}, u32[]{:S(2)}) %collective-permute-start.8) | collective-permute-done | bytes 131104 | tf_op jit(solution)/shard_map/ppermute | solution.py:23
  54.6 0.3 fusion.17
  54.9 11.3 %reduce-scatter.2.cloned.1.call-done = f32[2,4,32,128]{3,2,1,0:T(8,128)} async-done(((f32[2,4,128,128]{3,2,1,0:T(8,128)}), f32[2,4,32,128]{3,2,1,0:T(8,128)}) %reduce-scatter.2.cloned.1.call-update) | async-done | bytes 131088 | tf_op jit(solution)/shard_map/reduce_scatter | solution.py:107
  66.3 0.9 broadcast_multiply_fusion
  67.2 0.9 fusion.133
  68.2 6.6 %all_gather.3 = f32[2,4,128,128]{3,2,1,0:T(8,128)S(1)} all-gather(f32[2,4,32,128]{3,2,1,0:T(8,128)S(1)} %pad_maximum_fusion.51), channel_id=1, replica_groups=mesh['parts'=2,'src'=4,'space'=4] {'src'}, dimensions={2}, use_global_device_ids=true | all-gather | bytes 655360 | tf_op jit(solution)/shard_map/all_gather | solution.py:114
  75.0 0.2 fusion.8
  75.2 3.4 %collective-permute-start.11 = (f32[1,2,1,128,128]{4,3,2,1,0:T(8,128)S(1)}, f32[1,2,1,128,128]{4,3,2,1,0:T(8,128)S(1)}, u32[]{:S(2)}, u32[]{:S(2)}) collective-permute-start(f32[1,2,1,128,128]{4,3,2,1,0:T(8,128)S(1)} %get-tuple-element.37), channel_id=1, source_target_pairs={{0,1},{1,2},{2,3},{4,5},{5,6},{6,7},{8,9},{9,10},{10,11},{12,13},{... | collective-permute-start | bytes 393224 | tf_op jit(solution)/shard_map/ppermute | solution.py:20
  78.6 1.3 %collective-permute-start.10 = (f32[1,2,1,128,128]{4,3,2,1,0:T(8,128)S(1)}, f32[1,2,1,128,128]{4,3,2,1,0:T(8,128)S(1)}, u32[]{:S(2)}, u32[]{:S(2)}) collective-permute-start(f32[1,2,1,128,128]{4,3,2,1,0:T(8,128)S(1)} %get-tuple-element.36), channel_id=1, source_target_pairs={{1,0},{2,1},{3,2},{5,4},{6,5},{7,6},{9,8},{10,9},{11,10},{13,12},{... | collective-permute-start | bytes 393224 | tf_op jit(solution)/shard_map/ppermute | solution.py:23
  80.0 1.9 %collective-permute-done.11 = f32[1,2,1,128,128]{4,3,2,1,0:T(8,128)S(1)} collective-permute-done((f32[1,2,1,128,128]{4,3,2,1,0:T(8,128)S(1)}, f32[1,2,1,128,128]{4,3,2,1,0:T(8,128)S(1)}, u32[]{:S(2)}, u32[]{:S(2)}) %collective-permute-start.11) | collective-permute-done | bytes 131104 | tf_op jit(solution)/shard_map/ppermute | solution.py:20
  81.9 4.1 %collective-permute-done.10 = f32[1,2,1,128,128]{4,3,2,1,0:T(8,128)S(1)} collective-permute-done((f32[1,2,1,128,128]{4,3,2,1,0:T(8,128)S(1)}, f32[1,2,1,128,128]{4,3,2,1,0:T(8,128)S(1)}, u32[]{:S(2)}, u32[]{:S(2)}) %collective-permute-start.10) | collective-permute-done | bytes 131104 | tf_op jit(solution)/shard_map/ppermute | solution.py:23
  86.0 0.3 fusion.11
  86.3 0.3 fusion.134
  86.6 0.2 fusion.2
  86.8 3.4 %collective-permute-start.13 = (f32[1,2,1,128,128]{4,3,2,1,0:T(8,128)S(1)}, f32[1,2,1,128,128]{4,3,2,1,0:T(8,128)S(1)}, u32[]{:S(2)}, u32[]{:S(2)}) collective-permute-start(f32[1,2,1,128,128]{4,3,2,1,0:T(8,128)S(1)} %get-tuple-element.31), channel_id=1, source_target_pairs={{0,1},{1,2},{2,3},{4,5},{5,6},{6,7},{8,9},{9,10},{10,11},{12,13},{... | collective-permute-start | bytes 393224 | tf_op jit(solution)/shard_map/ppermute | solution.py:20
  90.2 1.3 %collective-permute-start.12 = (f32[1,2,1,128,128]{4,3,2,1,0:T(8,128)S(1)}, f32[1,2,1,128,128]{4,3,2,1,0:T(8,128)S(1)}, u32[]{:S(2)}, u32[]{:S(2)}) collective-permute-start(f32[1,2,1,128,128]{4,3,2,1,0:T(8,128)S(1)} %get-tuple-element.30), channel_id=1, source_target_pairs={{1,0},{2,1},{3,2},{5,4},{6,5},{7,6},{9,8},{10,9},{11,10},{13,12},{... | collective-permute-start | bytes 393224 | tf_op jit(solution)/shard_map/ppermute | solution.py:23
  91.6 1.1 %collective-permute-done.13 = f32[1,2,1,128,128]{4,3,2,1,0:T(8,128)S(1)} collective-permute-done((f32[1,2,1,128,128]{4,3,2,1,0:T(8,128)S(1)}, f32[1,2,1,128,128]{4,3,2,1,0:T(8,128)S(1)}, u32[]{:S(2)}, u32[]{:S(2)}) %collective-permute-start.13) | collective-permute-done | bytes 131104 | tf_op jit(solution)/shard_map/ppermute | solution.py:20
  92.7 4.4 %collective-permute-done.12 = f32[1,2,1,128,128]{4,3,2,1,0:T(8,128)S(1)} collective-permute-done((f32[1,2,1,128,128]{4,3,2,1,0:T(8,128)S(1)}, f32[1,2,1,128,128]{4,3,2,1,0:T(8,128)S(1)}, u32[]{:S(2)}, u32[]{:S(2)}) %collective-permute-start.12) | collective-permute-done | bytes 131104 | tf_op jit(solution)/shard_map/ppermute | solution.py:23
  97.1 0.3 fusion.5
  97.4 0.4 fusion.77
  97.8 0.8 pad_maximum_fusion.48
  98.6 0.8 copy.8
  (41 shorter events, 2.3 us)
Async XLA Ops:
  7.2 59.1 %reduce-scatter.2.cloned.1.call-start = ((), (), s32[]{:S(2)}) async-start(), calls=%async_computation.1 | async-start | bytes 655360 | tf_op jit(solution)/shard_map/reduce_scatter | solution.py:107
  8.3 7.7 %collective-permute-start.1 = (f32[1,2,1,128,128]{4,3,2,1,0:T(8,128)S(1)}, f32[1,2,1,128,128]{4,3,2,1,0:T(8,128)S(1)}, u32[]{:S(2)}, u32[]{:S(2)}) collective-permute-start(f32[1,2,1,128,128]{4,3,2,1,0:T(8,128)S(1)} %get-tuple-element.69), channel_id=1, source_target_pairs={{0,1},{1,2},{2,3},{4,5},{5,6},{6,7},{8,9},{9,10},{10,11},{12,13},{... | collective-permute-start | bytes 393224 | tf_op jit(solution)/shard_map/ppermute | solution.py:20
  13.3 6.9 %collective-permute-start = (f32[1,2,1,128,128]{4,3,2,1,0:T(8,128)S(1)}, f32[1,2,1,128,128]{4,3,2,1,0:T(8,128)S(1)}, u32[]{:S(2)}, u32[]{:S(2)}) collective-permute-start(f32[1,2,1,128,128]{4,3,2,1,0:T(8,128)S(1)} %get-tuple-element.68), channel_id=1, source_target_pairs={{1,0},{2,1},{3,2},{5,4},{6,5},{7,6},{9,8},{10,9},{11,10},{13,12},{... | collective-permute-start | bytes 393224 | tf_op jit(solution)/shard_map/ppermute | solution.py:23
  20.1 1.0 copy-start
  20.1 1.3 %copy-start.1 = (f32[1,4,4,128,128]{4,3,2,1,0:T(8,128)S(1)}, f32[1,4,4,128,128]{4,3,2,1,0:T(8,128)}, u32[]{:S(2)}) copy-start(f32[1,4,4,128,128]{4,3,2,1,0:T(8,128)} %param.4) | copy-start | bytes 3145732
  20.1 1.3 %copy-start.2 = (f32[4,128,128]{2,1,0:T(8,128)S(1)}, f32[4,128,128]{2,1,0:T(8,128)}, u32[]{:S(2)}) copy-start(f32[4,128,128]{2,1,0:T(8,128)} %param.6) | copy-start | bytes 786436
  22.0 7.8 %collective-permute-start.3 = (f32[1,2,1,128,128]{4,3,2,1,0:T(8,128)S(1)}, f32[1,2,1,128,128]{4,3,2,1,0:T(8,128)S(1)}, u32[]{:S(2)}, u32[]{:S(2)}) collective-permute-start(f32[1,2,1,128,128]{4,3,2,1,0:T(8,128)S(1)} %get-tuple-element.63), channel_id=1, source_target_pairs={{0,1},{1,2},{2,3},{4,5},{5,6},{6,7},{8,9},{9,10},{10,11},{12,13},{... | collective-permute-start | bytes 393224 | tf_op jit(solution)/shard_map/ppermute | solution.py:20
  25.5 7.3 %collective-permute-start.2 = (f32[1,2,1,128,128]{4,3,2,1,0:T(8,128)S(1)}, f32[1,2,1,128,128]{4,3,2,1,0:T(8,128)S(1)}, u32[]{:S(2)}, u32[]{:S(2)}) collective-permute-start(f32[1,2,1,128,128]{4,3,2,1,0:T(8,128)S(1)} %get-tuple-element.62), channel_id=1, source_target_pairs={{1,0},{2,1},{3,2},{5,4},{6,5},{7,6},{9,8},{10,9},{11,10},{13,12},{... | collective-permute-start | bytes 393224 | tf_op jit(solution)/shard_map/ppermute | solution.py:23
  26.8 11.7 %collective-permute-start.6 = (f32[2,1,128,128]{3,2,1,0:T(8,128)S(1)}, f32[2,1,128,128]{3,2,1,0:T(8,128)S(1)}, u32[]{:S(2)}, u32[]{:S(2)}) collective-permute-start(f32[2,1,128,128]{3,2,1,0:T(8,128)S(1)} %pad_maximum_fusion.49), channel_id=1, source_target_pairs={{1,0},{2,1},{3,2},{5,4},{6,5},{7,6},{9,8},{10,9},{11,10},{13,12},{... | collective-permute-start | bytes 393224 | tf_op jit(solution)/shard_map/ppermute | solution.py:23
  33.3 9.8 %collective-permute-start.5 = (f32[1,2,1,128,128]{4,3,2,1,0:T(8,128)S(1)}, f32[1,2,1,128,128]{4,3,2,1,0:T(8,128)S(1)}, u32[]{:S(2)}, u32[]{:S(2)}) collective-permute-start(f32[1,2,1,128,128]{4,3,2,1,0:T(8,128)S(1)} %get-tuple-element.57), channel_id=1, source_target_pairs={{0,1},{1,2},{2,3},{4,5},{5,6},{6,7},{8,9},{9,10},{10,11},{12,13},{... | collective-permute-start | bytes 393224 | tf_op jit(solution)/shard_map/ppermute | solution.py:20
  37.0 6.9 %collective-permute-start.4 = (f32[1,2,1,128,128]{4,3,2,1,0:T(8,128)S(1)}, f32[1,2,1,128,128]{4,3,2,1,0:T(8,128)S(1)}, u32[]{:S(2)}, u32[]{:S(2)}) collective-permute-start(f32[1,2,1,128,128]{4,3,2,1,0:T(8,128)S(1)} %get-tuple-element.56), channel_id=1, source_target_pairs={{1,0},{2,1},{3,2},{5,4},{6,5},{7,6},{9,8},{10,9},{11,10},{13,12},{... | collective-permute-start | bytes 393224 | tf_op jit(solution)/shard_map/ppermute | solution.py:23
  38.5 10.5 %collective-permute-start.7 = (f32[2,1,128,128]{3,2,1,0:T(8,128)S(1)}, f32[2,1,128,128]{3,2,1,0:T(8,128)S(1)}, u32[]{:S(2)}, u32[]{:S(2)}) collective-permute-start(f32[2,1,128,128]{3,2,1,0:T(8,128)S(1)} %get-tuple-element.11), channel_id=1, source_target_pairs={{0,1},{1,2},{2,3},{4,5},{5,6},{6,7},{8,9},{9,10},{10,11},{12,13},{... | collective-permute-start | bytes 393224 | tf_op jit(solution)/shard_map/ppermute | solution.py:20
  45.3 4.9 %collective-permute-start.9 = (f32[1,2,1,128,128]{4,3,2,1,0:T(8,128)S(1)}, f32[1,2,1,128,128]{4,3,2,1,0:T(8,128)S(1)}, u32[]{:S(2)}, u32[]{:S(2)}) collective-permute-start(f32[1,2,1,128,128]{4,3,2,1,0:T(8,128)S(1)} %get-tuple-element.51), channel_id=1, source_target_pairs={{0,1},{1,2},{2,3},{4,5},{5,6},{6,7},{8,9},{9,10},{10,11},{12,13},{... | collective-permute-start | bytes 393224 | tf_op jit(solution)/shard_map/ppermute | solution.py:20
  47.7 6.9 %collective-permute-start.8 = (f32[1,2,1,128,128]{4,3,2,1,0:T(8,128)S(1)}, f32[1,2,1,128,128]{4,3,2,1,0:T(8,128)S(1)}, u32[]{:S(2)}, u32[]{:S(2)}) collective-permute-start(f32[1,2,1,128,128]{4,3,2,1,0:T(8,128)S(1)} %get-tuple-element.50), channel_id=1, source_target_pairs={{1,0},{2,1},{3,2},{5,4},{6,5},{7,6},{9,8},{10,9},{11,10},{13,12},{... | collective-permute-start | bytes 393224 | tf_op jit(solution)/shard_map/ppermute | solution.py:23
  75.2 6.7 %collective-permute-start.11 = (f32[1,2,1,128,128]{4,3,2,1,0:T(8,128)S(1)}, f32[1,2,1,128,128]{4,3,2,1,0:T(8,128)S(1)}, u32[]{:S(2)}, u32[]{:S(2)}) collective-permute-start(f32[1,2,1,128,128]{4,3,2,1,0:T(8,128)S(1)} %get-tuple-element.37), channel_id=1, source_target_pairs={{0,1},{1,2},{2,3},{4,5},{5,6},{6,7},{8,9},{9,10},{10,11},{12,13},{... | collective-permute-start | bytes 393224 | tf_op jit(solution)/shard_map/ppermute | solution.py:20
  78.6 7.4 %collective-permute-start.10 = (f32[1,2,1,128,128]{4,3,2,1,0:T(8,128)S(1)}, f32[1,2,1,128,128]{4,3,2,1,0:T(8,128)S(1)}, u32[]{:S(2)}, u32[]{:S(2)}) collective-permute-start(f32[1,2,1,128,128]{4,3,2,1,0:T(8,128)S(1)} %get-tuple-element.36), channel_id=1, source_target_pairs={{1,0},{2,1},{3,2},{5,4},{6,5},{7,6},{9,8},{10,9},{11,10},{13,12},{... | collective-permute-start | bytes 393224 | tf_op jit(solution)/shard_map/ppermute | solution.py:23
  86.8 5.9 %collective-permute-start.13 = (f32[1,2,1,128,128]{4,3,2,1,0:T(8,128)S(1)}, f32[1,2,1,128,128]{4,3,2,1,0:T(8,128)S(1)}, u32[]{:S(2)}, u32[]{:S(2)}) collective-permute-start(f32[1,2,1,128,128]{4,3,2,1,0:T(8,128)S(1)} %get-tuple-element.31), channel_id=1, source_target_pairs={{0,1},{1,2},{2,3},{4,5},{5,6},{6,7},{8,9},{9,10},{10,11},{12,13},{... | collective-permute-start | bytes 393224 | tf_op jit(solution)/shard_map/ppermute | solution.py:20
  90.2 6.9 %collective-permute-start.12 = (f32[1,2,1,128,128]{4,3,2,1,0:T(8,128)S(1)}, f32[1,2,1,128,128]{4,3,2,1,0:T(8,128)S(1)}, u32[]{:S(2)}, u32[]{:S(2)}) collective-permute-start(f32[1,2,1,128,128]{4,3,2,1,0:T(8,128)S(1)} %get-tuple-element.30), channel_id=1, source_target_pairs={{1,0},{2,1},{3,2},{5,4},{6,5},{7,6},{9,8},{10,9},{11,10},{13,12},{... | collective-permute-start | bytes 393224 | tf_op jit(solution)/shard_map/ppermute | solution.py:23
Sparse Core Ops, SparseCore 0:
  45.4 20.8 reduce-scatter.1
where the time goes:
time: 107 us; the launch traced here: 106 us
  waiting for transfers between devices  36.2 us (34%)
  starting transfers between devices  35 us (33%)
  between operations  15.1 us (14%)
  other arithmetic  9.47 us (9%)
  blocking collectives  6.59 us (6%)
  local copies, waits for them, and re-layouts  3.91 us (4%)
    ppermute x7, starting transfers between devices, extended_2(): lax.ppermute(lax.slice_in_dim(block, block.shape[dim] - width, None, axis...  25.9 us
    ppermute x7, waiting for transfers between devices, extended_2(): lax.ppermute(lax.slice_in_dim(block, 0, width, axis=dim), axis, backward)  20.7 us
    reduce_scatter x1, waiting for transfers between devices, shards(): lax.psum_scatter(partial_sum, 'src', scatter_dimension=2, tiled=True)  11.3 us
    ppermute x7, starting transfers between devices, extended_2(): lax.ppermute(lax.slice_in_dim(block, 0, width, axis=dim), axis, backward)  9.04 us
    all_gather x1, blocking collectives, shards(): updated = lax.all_gather(fresh, 'src', axis=2, tiled=True)  6.59 us
    ppermute x7, waiting for transfers between devices, extended_2(): lax.ppermute(lax.slice_in_dim(block, block.shape[dim] - width, None, axis...  4.21 us
    another operation x21, other arithmetic, advance_thin(): padded = extended_2(jnp.stack([upper, lower], 1), (('space', 2),), 1)  2.26 us
  transfers between devices with their start and end apart: 15, of which 11 were waited for; matrix products, arithmetic and copies ran while one was open for 5% of the time, Pallas kernels for 0%

commit v1 on v0

v1 whole, which is shorter than its diff:
```python
import math

import jax
import jax.numpy as jnp
from jax import lax
from jax.experimental import pallas as pl
from jax.experimental.pallas import tpu as pltpu
from jax.sharding import PartitionSpec as P

speed_gain = 0.25
diffuse_gain = 0.15
step_size = 0.1
penalty_gain = 50.0

VMEM = pl.BlockSpec(memory_space=pltpu.VMEM)
SMEM = pl.BlockSpec(memory_space=pltpu.SMEM)
F32 = jnp.float32


def call(kernel, outs, args, specs, name, scratch=()):
    size = sum(math.prod(o) for o in outs) + sum(a.size for a in args)
    return pl.pallas_call(
        kernel,
        out_shape=tuple(jax.ShapeDtypeStruct(o, F32) for o in outs),
        in_specs=specs,
        out_specs=tuple(VMEM for _ in outs),
        scratch_shapes=list(scratch),
        name=name,
        cost_estimate=pl.CostEstimate(flops=20 * size, bytes_accessed=4 * size, transcendentals=0),
    )(*args)


def plane_tools(shape):
    row = lax.broadcasted_iota(jnp.int32, shape, 0)
    col = lax.broadcasted_iota(jnp.int32, shape, 1)
    rows, cols = shape

    def shifts(p, edge):
        def fill(test, moved):
            return jnp.where(test, p if edge else 0.0, moved)

        return (
            fill(row == 0, pltpu.roll(p, 1, 0)),
            fill(row == rows - 1, pltpu.roll(p, rows - 1, 0)),
            fill(col == 0, pltpu.roll(p, 1, 1)),
            fill(col == cols - 1, pltpu.roll(p, cols - 1, 1)),
        )

    def flat(p):
        a, b, c, d = shifts(p, False)
        return ((a + b) + (c + d)) - 6.0 * p

    return shifts, flat


def coefficient(weight, velocity, conductivity):
    return weight * speed_gain * velocity**2 + (1.0 - weight) * diffuse_gain / conductivity


def isolated_kernel(meta, f_ref, v_ref, c_ref, e_ref, o_ref, coef_ref, s1, s2):
    a = meta[0].astype(F32)
    even = meta[1] == 0
    tile = f_ref.shape[2]
    _, flat = plane_tools(f_ref.shape[3:])
    for i in range(tile):
        coef_ref[i] = coefficient(a, v_ref[i], c_ref[i])

    def lap(ref, i):
        total = flat(ref[i])
        if i > 0:
            total = total + ref[i - 1]
        if i < tile - 1:
            total = total + ref[i + 1]
        return total

    for n in range(2):
        cur, prev = f_ref.at[0, 2 * n], f_ref.at[0, 2 * n + 1]
        for i in range(tile):
            s1[i] = (1.0 + a) * cur[i] - a * prev[i] + coef_ref[i] * lap(cur, i)
        for i in (0, tile - 1):
            s2[i] = (1.0 + a) * s1[i] - a * cur[i] + coef_ref[i] * lap(s1, i)
        for k, ref in enumerate((s1, s2)):
            low, high = ref[0], ref[tile - 1]
            e_ref[2 * n + k] = jnp.where(even, high, low)
            o_ref[2 * n + k] = jnp.where(even, low, high)


def sides(even, e_ref, o_ref, k):
    e, o = e_ref[k], o_ref[k]
    return jnp.where(even, o, e), jnp.where(even, e, o)


def model_halo(meta, pick):
    first = meta[4] == 0
    out = []
    for s in range(2):
        mine, other = pick[0][s], pick[1][s]
        has = meta[2 + s] == 1
        out.append(
            (
                jnp.where(has, jnp.where(first, mine, other), 1.0),
                jnp.where(has, jnp.where(first, other, mine), 1.0),
                has,
            )
        )
    return out


def first_kernel(
    meta, f_ref, coef_ref, e1, o1, m_e, m_o, e2, o2,
    acc_ref, st_ref, hb_ref, hc_ref, pe_ref, po_ref, one,
):
    a = meta[0].astype(F32)
    even = meta[1] == 0
    tile, ny = f_ref.shape[2], f_ref.shape[3]
    _, flat = plane_tools(f_ref.shape[3:])
    edge = (0, tile - 1)
    halo = model_halo(meta, (sides(even, e1, o1, 0), sides(even, m_e, m_o, 0)))
    for s in range(2):
        v, c, has = halo[s]
        hc_ref[s] = jnp.where(has, coefficient(a, v, c), 0.0)

    def lap(ref, i, h):
        below = ref[i - 1] if i > 0 else h[0]
        above = ref[i + 1] if i < tile - 1 else h[1]
        return flat(ref[i]) + (below + above)

    for n in (1, 0):
        cur, prev = f_ref.at[0, 2 * n], f_ref.at[0, 2 * n + 1]
        two, three = st_ref.at[n, 0], st_ref.at[n, 1]
        h0 = sides(even, e1, o1, 1 + n)
        h1 = sides(even, e2, o2, 2 * n)
        h2 = sides(even, e2, o2, 2 * n + 1)
        d = [hc_ref[s] * cur[edge[s]] for s in range(2)]
        h1 = [h1[s] + d[s] for s in range(2)]
        for i in range(tile):
            l = lap(cur, i, h0)
            if n == 0:
                acc_ref[i * ny:(i + 1) * ny] = f_ref[0, 2, i] * l
            one[n, i] = (1.0 + a) * cur[i] - a * prev[i] + coef_ref[i] * l
        h2 = [
            h2[s] + (1.0 + a) * d[s] + hc_ref[s] * (flat(d[s]) + one[n, edge[s]])
            for s in range(2)
        ]
        for i in range(tile):
            l = lap(one.at[n], i, h1)
            if n == 0:
                acc_ref[i * ny:(i + 1) * ny] += one[1, i] * l
            two[i] = (1.0 + a) * one[n, i] - a * cur[i] + coef_ref[i] * l
        for i in range(tile):
            l = lap(two, i, h2)
            if n == 0:
                acc_ref[i * ny:(i + 1) * ny] += st_ref[1, 0, i] * l
            three[i] = (1.0 + a) * two[i] - a * one[n, i] + coef_ref[i] * l
        for s in range(2):
            hb_ref[s, n, 0] = h2[s]
            hb_ref[s, n, 1] = (
                (1.0 + a) * h2[s] - a * h1[s] + hc_ref[s] * (flat(h2[s]) + two[edge[s]])
            )
        low = (two[1], three[1], three[2])
        high = (two[tile - 2], three[tile - 2], three[tile - 3])
        for k in range(3):
            pe_ref[3 * n + k] = jnp.where(even, high[k], low[k])
            po_ref[3 * n + k] = jnp.where(even, low[k], high[k])
    acc_ref[tile * ny:] = jnp.full((acc_ref.shape[0] - tile * ny, acc_ref.shape[1]), a, F32)


def penalty_kernel(meta, v_ref, c_ref, e1, o1, m_e, m_o, out_ref, logs):
    even = meta[1] == 0
    tile = v_ref.shape[0]
    shifts, _ = plane_tools(v_ref.shape[1:])
    halo = model_halo(meta, (sides(even, e1, o1, 0), sides(even, m_e, m_o, 0)))
    for i in range(tile):
        logs[i + 1] = jnp.log(c_ref[i])
    for s, at, own in ((0, 0, 1), (1, tile + 1, tile)):
        logs[at] = jnp.where(halo[s][2], jnp.log(halo[s][1]), logs[own])
    ends = (
        jnp.where(halo[0][2], halo[0][0], v_ref[0]),
        jnp.where(halo[1][2], halo[1][0], v_ref[tile - 1]),
    )
    for i in range(tile):
        below = v_ref[i - 1] if i > 0 else ends[0]
        above = v_ref[i + 1] if i < tile - 1 else ends[1]
        vx = (above - below) * 0.5
        lx = (logs[i + 2] - logs[i]) * 0.5
        p, q, r, t = shifts(v_ref[i], True)
        vy, vz = (q - p) * 0.5, (t - r) * 0.5
        p, q, r, t = shifts(logs[i + 1], True)
        ly, lz = (q - p) * 0.5, (t - r) * 0.5
        ca = vy * lz - vz * ly
        cb = vz * lx - vx * lz
        cc = vx * ly - vy * lx
        out_ref[i] = penalty_gain * (ca * ca + cb * cb + cc * cc)


def weigh_kernel(mine, other, out_ref):
    tile, ny = out_ref.shape[1:3]
    for ref in (mine, other):
        label = jnp.broadcast_to(ref[tile * ny:tile * ny + 1], out_ref.shape[2:])
        for i in range(tile):
            acc = ref[i * ny:(i + 1) * ny]
            if ref is mine:
                out_ref[0, i] = label * acc
                out_ref[1, i] = (1.0 - label) * acc
            else:
                out_ref[0, i] += label * acc
                out_ref[1, i] += (1.0 - label) * acc


def renew_kernel(scale, meta, p_ref, q_ref, pen_ref, v_ref, c_ref, m_ref, coef_ref, e_ref, o_ref):
    a = meta[0].astype(F32)
    even = meta[1] == 0
    tile = v_ref.shape[0]
    for i in range(tile):
        new = []
        for n, ref in enumerate((v_ref, c_ref)):
            grad = scale * (p_ref[n, i] + q_ref[n, i])
            new.append(ref[i] * jnp.exp(-step_size * jnp.tanh(grad + pen_ref[i])))
            m_ref[n, i] = new[n]
        coef_ref[i] = coefficient(a, *new)
    for k in range(2):
        low, high = coef_ref[k], coef_ref[tile - 2 + k]
        e_ref[k] = jnp.where(even, high, low)
        o_ref[k] = jnp.where(even, low, high)


def second_kernel(meta, st_ref, hb_ref, hc_ref, re, ro, coef_ref, ce, co, out_ref, s3, s4, s5):
    a = meta[0].astype(F32)
    even = meta[1] == 0
    tile = st_ref.shape[2]
    _, flat = plane_tools(st_ref.shape[3:])
    far, near = sides(even, ce, co, 0), sides(even, ce, co, 1)
    cn = {-2: far[0], -1: near[0], tile: far[1], tile + 1: near[1]}

    def coef(j):
        return coef_ref[j] if 0 <= j < tile else cn[j]

    def lap(ref, j, off):
        return flat(ref[j + off]) + (ref[j + off - 1] + ref[j + off + 1])

    for n in range(2):
        two = sides(even, re, ro, 3 * n)
        s3[2], s3[tile + 3] = (hb_ref[s, n, 1] + hc_ref[s] * two[s] for s in range(2))
        s3[1], s3[tile + 4] = sides(even, re, ro, 3 * n + 1)
        s3[0], s3[tile + 5] = sides(even, re, ro, 3 * n + 2)
        prev = {-2: two[0], -1: hb_ref[0, n, 0], tile: hb_ref[1, n, 0], tile + 1: two[1]}
        for i in range(tile):
            s3[i + 3] = st_ref[n, 1, i]
        for j in range(-2, tile + 2):
            before = st_ref[n, 0, j] if 0 <= j < tile else prev[j]
            s4[j + 2] = (1.0 + a) * s3[j + 3] - a * before + coef(j) * lap(s3, j, 3)
        for j in range(-1, tile + 1):
            s5[j + 1] = (1.0 + a) * s4[j + 2] - a * s3[j + 3] + coef(j) * lap(s4, j, 2)
        for j in range(tile):
            out_ref[0, n, j] = (1.0 + a) * s5[j + 1] - a * s4[j + 2] + coef(j) * lap(s5, j, 1)


def swap_pairs(even_block, odd_block):
    count = lax.axis_size("space")
    evens = [(i, i ^ 1) for i in range(count) if i ^ 1 < count]
    odds = [(i, ((i + 1) ^ 1) - 1) for i in range(count) if 0 <= ((i + 1) ^ 1) - 1 < count]
    return lax.ppermute(even_block, "space", evens), lax.ppermute(odd_block, "space", odds)


def across(block, mask):
    count = lax.axis_size("src")
    return lax.ppermute(block, "src", [(i, i ^ mask) for i in range(count)])


def shards(fields, velocity, conductivity, labels):
    tile, ny, nz = velocity.shape
    plane = (ny, nz)
    here, count = lax.axis_index("space"), lax.axis_size("space")
    core = lax.axis_index("src") % 2
    meta = jnp.stack(
        [
            labels[0],
            here % 2,
            (here > 0).astype(jnp.int32),
            (here < count - 1).astype(jnp.int32),
            core,
        ]
    )
    even = here % 2 == 0

    edges = []
    for at in (0, tile - 1):
        model = jnp.where(core == 0, velocity[at], conductivity[at])
        edges.append(jnp.stack([model, fields[0, 0, at], fields[0, 2, at]], 0))
    low, high = edges
    e1, o1 = swap_pairs(jnp.where(even, high, low), jnp.where(even, low, high))

    stack = pltpu.VMEM((tile, *plane), F32)
    e2, o2, coef = call(
        isolated_kernel,
        [(4, *plane), (4, *plane), (tile, *plane)],
        (meta, fields, velocity, conductivity),
        [SMEM, VMEM, VMEM, VMEM],
        "isolated",
        [stack, stack],
    )
    e2, o2 = swap_pairs(e2, o2)
    other = across(jnp.stack([e1[:1], o1[:1]]), 1)
    m_e, m_o = other[0], other[1]

    acc, state, halo, halo_coef, e3, o3 = call(
        first_kernel,
        [
            (tile * ny + 8, nz),
            (2, 2, tile, *plane),
            (2, 2, 2, *plane),
            (2, *plane),
            (6, *plane),
            (6, *plane),
        ],
        (meta, fields, coef, e1, o1, m_e, m_o, e2, o2),
        [SMEM] + [VMEM] * 8,
        "first",
        [pltpu.VMEM((2, tile, *plane), F32)],
    )

    groups = lax.axis_size("src")
    masks = [1 << k for k in reversed(range(groups.bit_length() - 1))]
    acc_other = across(acc, masks[0])
    e3, o3 = swap_pairs(e3, o3)
    (pen,) = call(
        penalty_kernel,
        [(tile, *plane)],
        (meta, velocity, conductivity, e1, o1, m_e, m_o),
        [SMEM] + [VMEM] * 6,
        "penalty",
        [pltpu.VMEM((tile + 2, *plane), F32)],
    )
    (part,) = call(weigh_kernel, [(2, tile, *plane)], (acc, acc_other), [VMEM] * 2, "weigh")
    for mask in masks[1:-1]:
        part = part + across(part, mask)
    rest = across(part, masks[-1])

    scale = 1.0 / (20.0 * math.sqrt(groups * labels.shape[0]))
    models, coef_next, e4, o4 = call(
        lambda *refs: renew_kernel(scale, *refs),
        [(2, tile, *plane), (tile, *plane), (2, *plane), (2, *plane)],
        (meta, part, rest, pen, velocity, conductivity),
        [SMEM] + [VMEM] * 5,
        "renew",
    )
    e4, o4 = swap_pairs(e4, o4)
    (final,) = call(
        second_kernel,
        [(1, 2, tile, *plane)],
        (meta, state, halo, halo_coef, e3, o3, coef_next, e4, o4),
        [SMEM] + [VMEM] * 8,
        "second",
        [
            pltpu.VMEM((tile + 6, *plane), F32),
            pltpu.VMEM((tile + 4, *plane), F32),
            pltpu.VMEM((tile + 2, *plane), F32),
        ],
    )
    return final, models


def solution(mesh):
    in_specs = (
        P(("parts", "src"), None, "space", None, None),
        P(("parts", "space"), None, None),
        P(("parts", "space"), None, None),
        P(("parts", "src")),
    )
    out_specs = (
        P(("parts", "src"), None, "space", None, None),
        P(None, ("parts", "space"), None, None),
    )
    return jax.shard_map(shards, mesh=mesh, in_specs=in_specs, out_specs=out_specs, check_vma=False)
```

time: 107 us -> 64.6 us (0.60)
  Pallas kernels: 0 us -> 18.4 us
  starting transfers between devices: 35 us -> 16.9 us
  waiting for transfers between devices: 36.2 us -> 20.9 us
  between operations: 15.1 us -> 1.45 us
  other arithmetic: 9.47 us -> 0.06 us
  blocking collectives: 6.59 us -> 0 us
  local copies, waits for them, and re-layouts: 3.91 us -> 6.08 us
    pallas_call x0 -> x6, Pallas kernels: none -> 18.4 us  [call(): pl.pallas_call(kernel, out_shape=tuple((jax.ShapeDtypeStruct(o, F32) for...]
    ppermute x14 -> x11, starting transfers between devices: 34.9 us -> 16.9 us  [the longest x4 12.6 us: swap_pairs(): lax.ppermute(even_block, 'space', evens)]
    reduce_scatter x1 -> x0, waiting for transfers between devices: 11.3 us -> none  [shards(): lax.psum_scatter(partial_sum, 'src', scatter_dimension=2, tiled=True)]
    all_gather x1 -> x0, blocking collectives: 6.59 us -> none  [shards(): updated = lax.all_gather(fresh, 'src', axis=2, tiled=True)]
    another operation x28 -> x1, other arithmetic: 5.28 us -> 0.01 us  [shards(): other = across(jnp.stack([e1[:1], o1[:1]]), 1)]
    ppermute x14 -> x11, waiting for transfers between devices: 24.9 us -> 20.9 us  [the longest x4 14.2 us: swap_pairs(): lax.ppermute(even_block, 'space', evens)]
    slice x4 -> x0, local copies, waits for them, and re-layouts: 2.1 us -> none  [the longest x1 1.07 us: shards(): state = (fields[:, 0], fields[:, 1], fields[:, 2], fields[:, 3])]
    sub x6 -> x0, other arithmetic: 1.97 us -> none  [neighbours(): return total - 6.0 * middle]
  transfers between devices with their start and end apart: 15 -> 11, of which waited for: 11 -> 5; matrix products, arithmetic and copies ran while one was open for 5% -> 2% of each run, Pallas kernels for 0% -> 12%
where the time goes in v1:
time: 64.6 us; the launch traced here: 63.7 us
  waiting for transfers between devices  20.9 us (32%)
  Pallas kernels  18.4 us (28%)
  starting transfers between devices  16.9 us (26%)
  local copies, waits for them, and re-layouts  6.08 us (9%)
  between operations  1.45 us (2%)
    pallas_call x6, Pallas kernels, call(): pl.pallas_call(kernel, out_shape=tuple((jax.ShapeDtypeStruct(o, F32) for...  18.4 us
    ppermute x4, waiting for transfers between devices, swap_pairs(): lax.ppermute(even_block, 'space', evens)  14.2 us
    ppermute x4, starting transfers between devices, swap_pairs(): lax.ppermute(even_block, 'space', evens)  12.6 us
    ppermute x3, waiting for transfers between devices, across(): return lax.ppermute(block, 'src', [(i, i ^ mask) for i in range(count)])  6.67 us
    unnamed x28, local copies, waits for them, and re-layouts  3.77 us
    ppermute x4, starting transfers between devices, swap_pairs(): lax.ppermute(odd_block, 'space', odds)  2.67 us
    ppermute x3, starting transfers between devices, across(): return lax.ppermute(block, 'src', [(i, i ^ mask) for i in range(count)])  1.56 us
  transfers between devices with their start and end apart: 11, of which 5 were waited for; matrix products, arithmetic and copies ran while one was open for 2% of the time, Pallas kernels for 12%

profile of v1, /device:TPU:0, one launch (start us, length us, event | category | flops | bytes accessed | tf_op | source)
XLA Modules:
  0.0 63.7 jit_solution(16672939222339187481)
XLA Ops:
  0.7 0.0 copy-start
  0.7 0.0 copy-start.1
  0.7 1.0 %slice_bitcast_fusion.7 = (f32[1,128,128]{2,1,0:T(8,128)S(1)}, f32[1,128,128]{2,1,0:T(8,128)S(1)}, f32[1,128,128]{2,1,0:T(8,128)S(1)}, f32[1,128,128]{2,1,0:T(8,128)S(1)}) fusion(f32[1,4,4,128,128]{4,3,2,1,0:T(8,128)} %f_ref.3), kind=kLoop, calls=%fused_computation.13 | loop fusion | bytes 524288 | tf_op jit(solution)/shard_map/stack;squeeze | solution.py:289
  1.7 0.0 copy-done
  1.7 0.1 copy-done.1
  1.9 0.7 %collective-permute-start.1 = (f32[3,128,128]{2,1,0:T(8,128)S(1)}, f32[3,128,128]{2,1,0:T(8,128)S(1)}, u32[]{:S(2)}, u32[]{:S(2)}) collective-permute-start(f32[3,128,128]{2,1,0:T(8,128)S(1)} %get-tuple-element.34), channel_id=1, source_target_pairs={{1,2},{2,1},{5,6},{6,5},{9,10},{10,9},{13,14},{14,13},{17,18},{18,... | collective-permute-start | bytes 589832 | tf_op jit(solution)/shard_map/ppermute | solution.py:262
  2.6 5.9 %collective-permute-start = (f32[3,128,128]{2,1,0:T(8,128)S(1)}, f32[3,128,128]{2,1,0:T(8,128)S(1)}, u32[]{:S(2)}, u32[]{:S(2)}) collective-permute-start(f32[3,128,128]{2,1,0:T(8,128)S(1)} %get-tuple-element.35), channel_id=1, source_target_pairs={{0,1},{1,0},{2,3},{3,2},{4,5},{5,4},{6,7},{7,6},{8,9},{9,8},{10,11... | collective-permute-start | bytes 589832 | tf_op jit(solution)/shard_map/ppermute | solution.py:262
  8.5 0.0 collective-permute-done.1.o1
  8.5 4.6 %collective-permute-done.e1 = f32[3,128,128]{2,1,0:T(8,128)S(1)} collective-permute-done((f32[3,128,128]{2,1,0:T(8,128)S(1)}, f32[3,128,128]{2,1,0:T(8,128)S(1)}, u32[]{:S(2)}, u32[]{:S(2)}) %collective-permute-start) | collective-permute-done | bytes 196640 | tf_op jit(solution)/shard_map/ppermute | solution.py:262
  13.1 0.0 copy-done.2
  13.1 0.6 %copy-done.3 = f32[3,128,128]{2,1,0:T(8,128)} copy-done((f32[3,128,128]{2,1,0:T(8,128)}, f32[3,128,128]{2,1,0:T(8,128)S(1)}, u32[]{:S(2)}) %copy-start.3) | copy-done | bytes 196632
  13.8 0.0 collective-permute-start.2
  14.4 0.6 stack.44.meta.refs_0_
  15.1 2.8 %isolated.1 = (f32[4,128,128]{2,1,0:T(8,128)}, f32[4,128,128]{2,1,0:T(8,128)}, f32[4,128,128]{2,1,0:T(8,128)}) custom-call(s32[5]{0:T(128)} %stack.44.meta.refs_0_, f32[1,4,4,128,128]{4,3,2,1,0:T(8,128)} %f_ref.3, f32[4,128,128]{2,1,0:T(8,128)} %refs_4_.1, f32[4,128,128]{2,1,0:T(8,128)} %refs_5_.1), custom_call_target="tpu_custom_call" | custom-call | flops 11796580 | bytes 2359316 | tf_op jit(solution)/shard_map/isolated/pallas_call | solution.py:22
  17.9 1.7 %collective-permute-start.3 = (f32[4,128,128]{2,1,0:T(8,128)}, f32[4,128,128]{2,1,0:T(8,128)S(1)}, u32[]{:S(2)}, u32[]{:S(2)}) collective-permute-start(f32[4,128,128]{2,1,0:T(8,128)} %get-tuple-element.16), channel_id=1, source_target_pairs={{0,1},{1,0},{2,3},{3,2},{4,5},{5,4},{6,7},{7,6},{8,9},{9,8},{10,11... | collective-permute-start | bytes 786440 | tf_op jit(solution)/shard_map/ppermute | solution.py:262
  19.6 0.7 %collective-permute-start.4 = (f32[4,128,128]{2,1,0:T(8,128)}, f32[4,128,128]{2,1,0:T(8,128)S(1)}, u32[]{:S(2)}, u32[]{:S(2)}) collective-permute-start(f32[4,128,128]{2,1,0:T(8,128)} %get-tuple-element.17), channel_id=1, source_target_pairs={{1,2},{2,1},{5,6},{6,5},{9,10},{10,9},{13,14},{14,13},{17,18},{18,... | collective-permute-start | bytes 786440 | tf_op jit(solution)/shard_map/ppermute | solution.py:262
  20.3 0.0 collective-permute-done.2
  20.3 0.7 %slice_bitcast_fusion = (f32[1,128,128]{2,1,0:T(8,128)}, f32[1,128,128]{2,1,0:T(8,128)}) fusion(f32[2,1,128,128]{3,2,1,0:T(8,128)S(1)} %collective-permute-done.2), kind=kLoop, calls=%fused_computation.5 | loop fusion | bytes 262144 | tf_op jit(solution)/shard_map/squeeze | solution.py:304
  21.0 5.9 %collective-permute-done.3.e2 = f32[4,128,128]{2,1,0:T(8,128)S(1)} collective-permute-done((f32[4,128,128]{2,1,0:T(8,128)}, f32[4,128,128]{2,1,0:T(8,128)S(1)}, u32[]{:S(2)}, u32[]{:S(2)}) %collective-permute-start.3) | collective-permute-done | bytes 262176 | tf_op jit(solution)/shard_map/ppermute | solution.py:262
  26.8 0.0 collective-permute-done.4.o2
  26.8 0.7 %copy-done.8 = f32[4,128,128]{2,1,0:T(8,128)} copy-done((f32[4,128,128]{2,1,0:T(8,128)}, f32[4,128,128]{2,1,0:T(8,128)S(1)}, u32[]{:S(2)}) %copy-start.8) | copy-done | bytes 262168
  27.5 0.1 copy-done.9
  27.6 4.6 %first.1 = (f32[520,128]{1,0:T(8,128)}, f32[2,2,4,128,128]{4,3,2,1,0:T(8,128)}, f32[2,2,2,128,128]{4,3,2,1,0:T(8,128)}, f32[2,128,128]{2,1,0:T(8,128)}, f32[6,128,128]{2,1,0:T(8,128)}, /*index=5*/f32[6,128,128]{2,1,0:T(8,128)}) custom-call(s32[5]{0:T(128)} %stack.44.meta.refs_0_, f32[1,4,4,128,128]{4,3,2,1,0:T(8,128)} %f_ref.3, ...), custom_call_target="tpu_custom_call" | custom-call | flops 25579620 | bytes 5115924 | tf_op jit(solution)/shard_map/first/pallas_call | solution.py:22
  32.2 0.0 copy-start.12
  32.2 1.6 %collective-permute-start.7 = (f32[520,128]{1,0:T(8,128)}, f32[520,128]{1,0:T(8,128)S(1)}, u32[]{:S(2)}, u32[]{:S(2)}) collective-permute-start(f32[520,128]{1,0:T(8,128)} %get-tuple-element.23.mine), channel_id=1, source_target_pairs={{0,8},{4,12},{8,0},{12,4},{1,9},{5,13},{9,1},{13,5},{2,10},{6,14},... | collective-permute-start | bytes 798728 | tf_op jit(solution)/shard_map/ppermute | solution.py:267
  33.7 6.7 %collective-permute-done.7.other = f32[520,128]{1,0:T(8,128)S(1)} collective-permute-done((f32[520,128]{1,0:T(8,128)}, f32[520,128]{1,0:T(8,128)S(1)}, u32[]{:S(2)}, u32[]{:S(2)}) %collective-permute-start.7) | collective-permute-done | bytes 266272 | tf_op jit(solution)/shard_map/ppermute | solution.py:267
  40.4 0.7 %copy-done.7 = f32[520,128]{1,0:T(8,128)} copy-done((f32[520,128]{1,0:T(8,128)}, f32[520,128]{1,0:T(8,128)S(1)}, u32[]{:S(2)}) %copy-start.7) | copy-done | bytes 266264
  41.1 1.9 %weigh.1.refs_1_ = f32[2,4,128,128]{3,2,1,0:T(8,128)} custom-call(f32[520,128]{1,0:T(8,128)} %get-tuple-element.23.mine, f32[520,128]{1,0:T(8,128)} %copy-done.7), custom_call_target="tpu_custom_call" | custom-call | flops 5283840 | bytes 1056768 | tf_op jit(solution)/shard_map/weigh/pallas_call | solution.py:22
  43.0 0.0 collective-permute-start.8
  43.0 0.0 copy-done.13
  43.0 3.3 %collective-permute-start.5 = (f32[6,128,128]{2,1,0:T(8,128)S(1)}, f32[6,128,128]{2,1,0:T(8,128)S(1)}, u32[]{:S(2)}, u32[]{:S(2)}) collective-permute-start(f32[6,128,128]{2,1,0:T(8,128)S(1)} %copy-done.13), channel_id=1, source_target_pairs={{0,1},{1,0},{2,3},{3,2},{4,5},{5,4},{6,7},{7,6},{8,9},{9,8},{10,11... | collective-permute-start | bytes 1179656 | tf_op jit(solution)/shard_map/ppermute | solution.py:262
  46.3 0.0 copy-done.12
  46.3 0.7 %collective-permute-start.6 = (f32[6,128,128]{2,1,0:T(8,128)S(1)}, f32[6,128,128]{2,1,0:T(8,128)S(1)}, u32[]{:S(2)}, u32[]{:S(2)}) collective-permute-start(f32[6,128,128]{2,1,0:T(8,128)S(1)} %copy-done.12), channel_id=1, source_target_pairs={{1,2},{2,1},{5,6},{6,5},{9,10},{10,9},{13,14},{14,13},{17,18},{18,... | collective-permute-start | bytes 1179656 | tf_op jit(solution)/shard_map/ppermute | solution.py:262
  47.0 2.4 %penalty.1.refs_3_ = f32[4,128,128]{2,1,0:T(8,128)} custom-call(s32[5]{0:T(128)} %stack.44.meta.refs_0_, f32[4,128,128]{2,1,0:T(8,128)} %refs_4_.1, f32[4,128,128]{2,1,0:T(8,128)} %refs_5_.1, f32[3,128,128]{2,1,0:T(8,128)} %copy-done.3, f32[3,128,128]{2,1,0:T(8,128)} %copy-done.2, f32[1,128,128]{2,1,0:T(8,128)} %get-tuple-element.37.m_e, ...), custom_call_target="tpu_custom_call" | custom-call | flops 6553700 | bytes 1310740 | tf_op jit(solution)/shard_map/penalty/pallas_call | solution.py:22
  49.4 0.0 collective-permute-done.8.refs_2_
  49.4 0.8 %copy-done.4 = f32[2,4,128,128]{3,2,1,0:T(8,128)} copy-done((f32[2,4,128,128]{3,2,1,0:T(8,128)}, f32[2,4,128,128]{3,2,1,0:T(8,128)S(1)}, u32[]{:S(2)}) %copy-start.4) | copy-done | bytes 524312
  50.2 2.6 %renew.1 = (f32[2,4,128,128]{3,2,1,0:T(8,128)}, f32[4,128,128]{2,1,0:T(8,128)}, f32[2,128,128]{2,1,0:T(8,128)}, f32[2,128,128]{2,1,0:T(8,128)}) custom-call(s32[5]{0:T(128)} %stack.44.meta.refs_0_, f32[2,4,128,128]{3,2,1,0:T(8,128)} %weigh.1.refs_1_, f32[2,4,128,128]{3,2,1,0:T(8,128)} %copy-done.4, f32[4,128,128]{2,1,0:T(8,128)} %penalty.1.refs_3_, ...), custom_call_target="tpu_custom_call" | custom-call | flops 14418020 | bytes 2883604 | tf_op jit(solution)/shard_map/renew/pallas_call | solution.py:22
  52.7 1.7 %collective-permute-start.9 = (f32[2,128,128]{2,1,0:T(8,128)}, f32[2,128,128]{2,1,0:T(8,128)S(1)}, u32[]{:S(2)}, u32[]{:S(2)}) collective-permute-start(f32[2,128,128]{2,1,0:T(8,128)} %get-tuple-element.25), channel_id=1, source_target_pairs={{0,1},{1,0},{2,3},{3,2},{4,5},{5,4},{6,7},{7,6},{8,9},{9,8},{10,11... | collective-permute-start | bytes 393224 | tf_op jit(solution)/shard_map/ppermute | solution.py:262
  54.4 0.7 %collective-permute-start.10 = (f32[2,128,128]{2,1,0:T(8,128)}, f32[2,128,128]{2,1,0:T(8,128)S(1)}, u32[]{:S(2)}, u32[]{:S(2)}) collective-permute-start(f32[2,128,128]{2,1,0:T(8,128)} %get-tuple-element.26), channel_id=1, source_target_pairs={{1,2},{2,1},{5,6},{6,5},{9,10},{10,9},{13,14},{14,13},{17,18},{18,... | collective-permute-start | bytes 393224 | tf_op jit(solution)/shard_map/ppermute | solution.py:262
  55.1 1.2 %collective-permute-done.5.re = f32[6,128,128]{2,1,0:T(8,128)S(1)} collective-permute-done((f32[6,128,128]{2,1,0:T(8,128)S(1)}, f32[6,128,128]{2,1,0:T(8,128)S(1)}, u32[]{:S(2)}, u32[]{:S(2)}) %collective-permute-start.5) | collective-permute-done | bytes 393248 | tf_op jit(solution)/shard_map/ppermute | solution.py:262
  56.2 0.0 collective-permute-done.6.ro
  56.3 2.6 %collective-permute-done.9.ce = f32[2,128,128]{2,1,0:T(8,128)S(1)} collective-permute-done((f32[2,128,128]{2,1,0:T(8,128)}, f32[2,128,128]{2,1,0:T(8,128)S(1)}, u32[]{:S(2)}, u32[]{:S(2)}) %collective-permute-start.9) | collective-permute-done | bytes 131104 | tf_op jit(solution)/shard_map/ppermute | solution.py:262
  58.9 0.0 collective-permute-done.10.co
  58.9 0.0 copy-done.5
  58.9 0.0 copy-done.6
  58.9 0.6 copy-done.10
  59.5 0.1 copy-done.11
  59.6 4.1 %second.1 = f32[1,2,4,128,128]{4,3,2,1,0:T(8,128)} custom-call(s32[5]{0:T(128)} %stack.44.meta.refs_0_, f32[2,2,4,128,128]{4,3,2,1,0:T(8,128)} %get-tuple-element.18.st_ref, f32[2,2,2,128,128]{4,3,2,1,0:T(8,128)} %get-tuple-element.19.hb_ref, f32[2,128,128]{2,1,0:T(8,128)} %get-tuple-element.20.hc_ref, f32[6,128,128]{2,1,0:T(8,128)} %copy-done.5, ...), custom_call_target="tpu_custom_call" | custom-call | flops 17694820 | bytes 3538964 | tf_op jit(solution)/shard_map/second/pallas_call | solution.py:22
  (16 shorter events, 0.1 us)
Async XLA Ops:
  0.7 1.0 %copy-start = (f32[4,128,128]{2,1,0:T(8,128)S(1)}, f32[4,128,128]{2,1,0:T(8,128)}, u32[]{:S(2)}) copy-start(f32[4,128,128]{2,1,0:T(8,128)} %refs_4_.1) | copy-start | bytes 786436
  0.7 1.1 %copy-start.1 = (f32[4,128,128]{2,1,0:T(8,128)S(1)}, f32[4,128,128]{2,1,0:T(8,128)}, u32[]{:S(2)}) copy-start(f32[4,128,128]{2,1,0:T(8,128)} %refs_5_.1) | copy-start | bytes 786436
  1.9 6.6 %collective-permute-start.1 = (f32[3,128,128]{2,1,0:T(8,128)S(1)}, f32[3,128,128]{2,1,0:T(8,128)S(1)}, u32[]{:S(2)}, u32[]{:S(2)}) collective-permute-start(f32[3,128,128]{2,1,0:T(8,128)S(1)} %get-tuple-element.34), channel_id=1, source_target_pairs={{1,2},{2,1},{5,6},{6,5},{9,10},{10,9},{13,14},{14,13},{17,18},{18,... | collective-permute-start | bytes 589832 | tf_op jit(solution)/shard_map/ppermute | solution.py:262
  2.6 10.6 %collective-permute-start = (f32[3,128,128]{2,1,0:T(8,128)S(1)}, f32[3,128,128]{2,1,0:T(8,128)S(1)}, u32[]{:S(2)}, u32[]{:S(2)}) collective-permute-start(f32[3,128,128]{2,1,0:T(8,128)S(1)} %get-tuple-element.35), channel_id=1, source_target_pairs={{0,1},{1,0},{2,3},{3,2},{4,5},{5,4},{6,7},{7,6},{8,9},{9,8},{10,11... | collective-permute-start | bytes 589832 | tf_op jit(solution)/shard_map/ppermute | solution.py:262
  8.5 4.7 %copy-start.2 = (f32[3,128,128]{2,1,0:T(8,128)}, f32[3,128,128]{2,1,0:T(8,128)S(1)}, u32[]{:S(2)}) copy-start(f32[3,128,128]{2,1,0:T(8,128)S(1)} %collective-permute-done.1.o1) | copy-start | bytes 589828
  13.1 0.7 %copy-start.3 = (f32[3,128,128]{2,1,0:T(8,128)}, f32[3,128,128]{2,1,0:T(8,128)S(1)}, u32[]{:S(2)}) copy-start(f32[3,128,128]{2,1,0:T(8,128)S(1)} %collective-permute-done.e1) | copy-start | bytes 589828
  13.8 6.5 %collective-permute-start.2 = (f32[2,1,128,128]{3,2,1,0:T(8,128)S(1)}, f32[2,1,128,128]{3,2,1,0:T(8,128)S(1)}, u32[]{:S(2)}, u32[]{:S(2)}) collective-permute-start(f32[2,1,128,128]{3,2,1,0:T(8,128)S(1)} %pad_maximum_fusion.2), channel_id=1, source_target_pairs={{0,4},{4,0},{8,12},{12,8},{1,5},{5,1},{9,13},{13,9},{2,6},{6,2},{1... | collective-permute-start | bytes 393224 | tf_op jit(solution)/shard_map/ppermute | solution.py:267
  17.9 8.9 %collective-permute-start.3 = (f32[4,128,128]{2,1,0:T(8,128)}, f32[4,128,128]{2,1,0:T(8,128)S(1)}, u32[]{:S(2)}, u32[]{:S(2)}) collective-permute-start(f32[4,128,128]{2,1,0:T(8,128)} %get-tuple-element.16), channel_id=1, source_target_pairs={{0,1},{1,0},{2,3},{3,2},{4,5},{5,4},{6,7},{7,6},{8,9},{9,8},{10,11... | collective-permute-start | bytes 786440 | tf_op jit(solution)/shard_map/ppermute | solution.py:262
  19.6 7.2 %collective-permute-start.4 = (f32[4,128,128]{2,1,0:T(8,128)}, f32[4,128,128]{2,1,0:T(8,128)S(1)}, u32[]{:S(2)}, u32[]{:S(2)}) collective-permute-start(f32[4,128,128]{2,1,0:T(8,128)} %get-tuple-element.17), channel_id=1, source_target_pairs={{1,2},{2,1},{5,6},{6,5},{9,10},{10,9},{13,14},{14,13},{17,18},{18,... | collective-permute-start | bytes 786440 | tf_op jit(solution)/shard_map/ppermute | solution.py:262
  26.8 0.7 %copy-start.8 = (f32[4,128,128]{2,1,0:T(8,128)}, f32[4,128,128]{2,1,0:T(8,128)S(1)}, u32[]{:S(2)}) copy-start(f32[4,128,128]{2,1,0:T(8,128)S(1)} %collective-permute-done.3.e2) | copy-start | bytes 786436
  26.8 0.8 %copy-start.9 = (f32[4,128,128]{2,1,0:T(8,128)}, f32[4,128,128]{2,1,0:T(8,128)S(1)}, u32[]{:S(2)}) copy-start(f32[4,128,128]{2,1,0:T(8,128)S(1)} %collective-permute-done.4.o2) | copy-start | bytes 786436
  32.2 10.8 %copy-start.13 = (f32[6,128,128]{2,1,0:T(8,128)S(1)}, f32[6,128,128]{2,1,0:T(8,128)}, u32[]{:S(2)}) copy-start(f32[6,128,128]{2,1,0:T(8,128)} %get-tuple-element.21) | copy-start | bytes 1179652
  32.2 14.1 %copy-start.12 = (f32[6,128,128]{2,1,0:T(8,128)S(1)}, f32[6,128,128]{2,1,0:T(8,128)}, u32[]{:S(2)}) copy-start(f32[6,128,128]{2,1,0:T(8,128)} %get-tuple-element.22) | copy-start | bytes 1179652
  32.2 8.2 %collective-permute-start.7 = (f32[520,128]{1,0:T(8,128)}, f32[520,128]{1,0:T(8,128)S(1)}, u32[]{:S(2)}, u32[]{:S(2)}) collective-permute-start(f32[520,128]{1,0:T(8,128)} %get-tuple-element.23.mine), channel_id=1, source_target_pairs={{0,8},{4,12},{8,0},{12,4},{1,9},{5,13},{9,1},{13,5},{2,10},{6,14},... | collective-permute-start | bytes 798728 | tf_op jit(solution)/shard_map/ppermute | solution.py:267
  40.4 0.7 %copy-start.7 = (f32[520,128]{1,0:T(8,128)}, f32[520,128]{1,0:T(8,128)S(1)}, u32[]{:S(2)}) copy-start(f32[520,128]{1,0:T(8,128)S(1)} %collective-permute-done.7.other) | copy-start | bytes 798724
  43.0 6.3 %collective-permute-start.8 = (f32[2,4,128,128]{3,2,1,0:T(8,128)}, f32[2,4,128,128]{3,2,1,0:T(8,128)S(1)}, u32[]{:S(2)}, u32[]{:S(2)}) collective-permute-start(f32[2,4,128,128]{3,2,1,0:T(8,128)} %weigh.1.refs_1_), channel_id=1, source_target_pairs={{0,4},{4,0},{8,12},{12,8},{1,5},{5,1},{9,13},{13,9},{2,6},{6,2},{1... | collective-permute-start | bytes 1572872 | tf_op jit(solution)/shard_map/ppermute | solution.py:267
  43.0 13.2 %collective-permute-start.5 = (f32[6,128,128]{2,1,0:T(8,128)S(1)}, f32[6,128,128]{2,1,0:T(8,128)S(1)}, u32[]{:S(2)}, u32[]{:S(2)}) collective-permute-start(f32[6,128,128]{2,1,0:T(8,128)S(1)} %copy-done.13), channel_id=1, source_target_pairs={{0,1},{1,0},{2,3},{3,2},{4,5},{5,4},{6,7},{7,6},{8,9},{9,8},{10,11... | collective-permute-start | bytes 1179656 | tf_op jit(solution)/shard_map/ppermute | solution.py:262
  46.3 10.0 %collective-permute-start.6 = (f32[6,128,128]{2,1,0:T(8,128)S(1)}, f32[6,128,128]{2,1,0:T(8,128)S(1)}, u32[]{:S(2)}, u32[]{:S(2)}) collective-permute-start(f32[6,128,128]{2,1,0:T(8,128)S(1)} %copy-done.12), channel_id=1, source_target_pairs={{1,2},{2,1},{5,6},{6,5},{9,10},{10,9},{13,14},{14,13},{17,18},{18,... | collective-permute-start | bytes 1179656 | tf_op jit(solution)/shard_map/ppermute | solution.py:262
  49.4 0.8 %copy-start.4 = (f32[2,4,128,128]{3,2,1,0:T(8,128)}, f32[2,4,128,128]{3,2,1,0:T(8,128)S(1)}, u32[]{:S(2)}) copy-start(f32[2,4,128,128]{3,2,1,0:T(8,128)S(1)} %collective-permute-done.8.refs_2_) | copy-start | bytes 1572868
  52.7 6.1 %collective-permute-start.9 = (f32[2,128,128]{2,1,0:T(8,128)}, f32[2,128,128]{2,1,0:T(8,128)S(1)}, u32[]{:S(2)}, u32[]{:S(2)}) collective-permute-start(f32[2,128,128]{2,1,0:T(8,128)} %get-tuple-element.25), channel_id=1, source_target_pairs={{0,1},{1,0},{2,3},{3,2},{4,5},{5,4},{6,7},{7,6},{8,9},{9,8},{10,11... | collective-permute-start | bytes 393224 | tf_op jit(solution)/shard_map/ppermute | solution.py:262
  54.4 4.5 %collective-permute-start.10 = (f32[2,128,128]{2,1,0:T(8,128)}, f32[2,128,128]{2,1,0:T(8,128)S(1)}, u32[]{:S(2)}, u32[]{:S(2)}) collective-permute-start(f32[2,128,128]{2,1,0:T(8,128)} %get-tuple-element.26), channel_id=1, source_target_pairs={{1,2},{2,1},{5,6},{6,5},{9,10},{10,9},{13,14},{14,13},{17,18},{18,... | collective-permute-start | bytes 393224 | tf_op jit(solution)/shard_map/ppermute | solution.py:262
  56.2 2.6 %copy-start.5 = (f32[6,128,128]{2,1,0:T(8,128)}, f32[6,128,128]{2,1,0:T(8,128)S(1)}, u32[]{:S(2)}) copy-start(f32[6,128,128]{2,1,0:T(8,128)S(1)} %collective-permute-done.5.re) | copy-start | bytes 1179652
  56.3 2.6 %copy-start.6 = (f32[6,128,128]{2,1,0:T(8,128)}, f32[6,128,128]{2,1,0:T(8,128)S(1)}, u32[]{:S(2)}) copy-start(f32[6,128,128]{2,1,0:T(8,128)S(1)} %collective-permute-done.6.ro) | copy-start | bytes 1179652
  58.9 0.6 %copy-start.10 = (f32[2,128,128]{2,1,0:T(8,128)}, f32[2,128,128]{2,1,0:T(8,128)S(1)}, u32[]{:S(2)}) copy-start(f32[2,128,128]{2,1,0:T(8,128)S(1)} %collective-permute-done.9.ce) | copy-start | bytes 393220
  58.9 0.7 %copy-start.11 = (f32[2,128,128]{2,1,0:T(8,128)}, f32[2,128,128]{2,1,0:T(8,128)S(1)}, u32[]{:S(2)}) copy-start(f32[2,128,128]{2,1,0:T(8,128)S(1)} %collective-permute-done.10.co) | copy-start | bytes 393220

commit v2 on v1

--- a/solution.py
+++ b/solution.py
@@ -7,6 +7,7 @@
 from jax.experimental.pallas import tpu as pltpu
 from jax.sharding import PartitionSpec as P
 
+
 speed_gain = 0.25
 diffuse_gain = 0.15
 step_size = 0.1
@@ -17,7 +18,7 @@
 F32 = jnp.float32
 
 
-def call(kernel, outs, args, specs, name, scratch=()):
+def call(kernel, outs, args, specs, scratch=()):
     size = sum(math.prod(o) for o in outs) + sum(a.size for a in args)
     return pl.pallas_call(
         kernel,
@@ -25,7 +26,7 @@
         in_specs=specs,
         out_specs=tuple(VMEM for _ in outs),
         scratch_shapes=list(scratch),
-        name=name,
+        compiler_params=pltpu.CompilerParams(vmem_limit_bytes=16 << 20),
         cost_estimate=pl.CostEstimate(flops=20 * size, bytes_accessed=4 * size, transcendentals=0),
     )(*args)
 
@@ -106,8 +107,13 @@
     return out
 
 
+def pick_kernel(e1, o1, out_ref):
+    out_ref[0] = e1[0]
+    out_ref[1] = o1[0]
+
+
 def first_kernel(
-    meta, f_ref, coef_ref, e1, o1, m_e, m_o, e2, o2,
+    meta, f_ref, coef_ref, e1, o1, m, e2, o2,
     acc_ref, st_ref, hb_ref, hc_ref, pe_ref, po_ref, one,
 ):
     a = meta[0].astype(F32)
@@ -115,7 +121,7 @@
     tile, ny = f_ref.shape[2], f_ref.shape[3]
     _, flat = plane_tools(f_ref.shape[3:])
     edge = (0, tile - 1)
-    halo = model_halo(meta, (sides(even, e1, o1, 0), sides(even, m_e, m_o, 0)))
+    halo = model_halo(meta, (sides(even, e1, o1, 0), sides(even, m.at[:1], m.at[1:], 0)))
     for s in range(2):
         v, c, has = halo[s]
         hc_ref[s] = jnp.where(has, coefficient(a, v, c), 0.0)
@@ -165,11 +171,11 @@
     acc_ref[tile * ny:] = jnp.full((acc_ref.shape[0] - tile * ny, acc_ref.shape[1]), a, F32)
 
 
-def penalty_kernel(meta, v_ref, c_ref, e1, o1, m_e, m_o, out_ref, logs):
+def penalty_kernel(meta, v_ref, c_ref, e1, o1, m, out_ref, logs):
     even = meta[1] == 0
     tile = v_ref.shape[0]
     shifts, _ = plane_tools(v_ref.shape[1:])
-    halo = model_halo(meta, (sides(even, e1, o1, 0), sides(even, m_e, m_o, 0)))
+    halo = model_halo(meta, (sides(even, e1, o1, 0), sides(even, m.at[:1], m.at[1:], 0)))
     for i in range(tile):
         logs[i + 1] = jnp.log(c_ref[i])
     for s, at, own in ((0, 0, 1), (1, tile + 1, tile)):
@@ -267,7 +273,7 @@
     return lax.ppermute(block, "src", [(i, i ^ mask) for i in range(count)])
 
 
-def shards(fields, velocity, conductivity, labels):
+def block_step(fields, velocity, conductivity, labels):
     tile, ny, nz = velocity.shape
     plane = (ny, nz)
     here, count = lax.axis_index("space"), lax.axis_size("space")
@@ -296,12 +302,11 @@
         [(4, *plane), (4, *plane), (tile, *plane)],
         (meta, fields, velocity, conductivity),
         [SMEM, VMEM, VMEM, VMEM],
-        "isolated",
         [stack, stack],
     )
     e2, o2 = swap_pairs(e2, o2)
-    other = across(jnp.stack([e1[:1], o1[:1]]), 1)
-    m_e, m_o = other[0], other[1]
+    (other,) = call(pick_kernel, [(2, *plane)], (e1, o1), [VMEM] * 2)
+    other = across(other, 1)
 
     acc, state, halo, halo_coef, e3, o3 = call(
         first_kernel,
@@ -313,9 +318,8 @@
             (6, *plane),
             (6, *plane),
         ],
-        (meta, fields, coef, e1, o1, m_e, m_o, e2, o2),
-        [SMEM] + [VMEM] * 8,
-        "first",
+        (meta, fields, coef, e1, o1, other, e2, o2),
+        [SMEM] + [VMEM] * 7,
         [pltpu.VMEM((2, tile, *plane), F32)],
     )
 
@@ -326,12 +330,11 @@
     (pen,) = call(
         penalty_kernel,
         [(tile, *plane)],
-        (meta, velocity, conductivity, e1, o1, m_e, m_o),
-        [SMEM] + [VMEM] * 6,
-        "penalty",
+        (meta, velocity, conductivity, e1, o1, other),
+        [SMEM] + [VMEM] * 5,
         [pltpu.VMEM((tile + 2, *plane), F32)],
     )
-    (part,) = call(weigh_kernel, [(2, tile, *plane)], (acc, acc_other), [VMEM] * 2, "weigh")
+    (part,) = call(weigh_kernel, [(2, tile, *plane)], (acc, acc_other), [VMEM] * 2)
     for mask in masks[1:-1]:
         part = part + across(part, mask)
     rest = across(part, masks[-1])
@@ -342,7 +345,6 @@
         [(2, tile, *plane), (tile, *plane), (2, *plane), (2, *plane)],
         (meta, part, rest, pen, velocity, conductivity),
         [SMEM] + [VMEM] * 5,
-        "renew",
     )
     e4, o4 = swap_pairs(e4, o4)
     (final,) = call(
@@ -350,7 +352,6 @@
         [(1, 2, tile, *plane)],
         (meta, state, halo, halo_coef, e3, o3, coef_next, e4, o4),
         [SMEM] + [VMEM] * 8,
-        "second",
         [
             pltpu.VMEM((tile + 6, *plane), F32),
             pltpu.VMEM((tile + 4, *plane), F32),
@@ -371,4 +372,6 @@
         P(("parts", "src"), None, "space", None, None),
         P(None, ("parts", "space"), None, None),
     )
-    return jax.shard_map(shards, mesh=mesh, in_specs=in_specs, out_specs=out_specs, check_vma=False)
+    return jax.shard_map(
+        block_step, mesh=mesh, in_specs=in_specs, out_specs=out_specs, check_vma=False
+    )

time: 64.6 us -> 48 us (0.74)
  Pallas kernels: 18.4 us -> 9.16 us
  local copies, waits for them, and re-layouts: 6.08 us -> 1.14 us
  starting transfers between devices: 16.9 us -> 14.3 us
  other arithmetic: 0.06 us -> 0.99 us
  waiting for transfers between devices: 20.9 us -> 20.1 us
    pallas_call x6 -> x7, Pallas kernels: 18.4 us -> 9.16 us  [call(): pl.pallas_call(kernel, out_shape=tuple((jax.ShapeDtypeStruct(o, F32) for...]
    unnamed x28 -> x6, local copies, waits for them, and re-layouts: 3.77 us -> 0.02 us
    ppermute x4, starting transfers between devices: 12.6 us -> 9.77 us  [swap_pairs(): lax.ppermute(even_block, 'space', evens)]
    select_n x2, other arithmetic: 0.05 us -> 0.99 us  [the longest x1 0.96 us: block_step(): model = jnp.where(core == 0, velocity[at], conductivity[at])]
    ppermute x3, waiting for transfers between devices: 6.67 us -> 6.02 us  [across(): return lax.ppermute(block, 'src', [(i, i ^ mask) for i in range(count)])]
    squeeze x1 -> x0, local copies, waits for them, and re-layouts: 0.65 us -> none  [shards(): m_e, m_o = (other[0], other[1])]
    another operation x4 -> x2, local copies, waits for them, and re-layouts: 1.66 us -> 1.12 us  [the longest x1 1.04 us: block_step(): edges.append(jnp.stack([model, fields[0, 0, at], fields[0, 2, at]], 0))]
  transfers between devices with their start and end apart: 11 -> 11, of which waited for: 5 -> 5; matrix products, arithmetic and copies ran while one was open for 2% -> 0% of each run, Pallas kernels for 12% -> 8%
where the time goes in v2:
time: 48 us; the launch traced here: 47.2 us
  waiting for transfers between devices  20.1 us (42%)
  starting transfers between devices  14.3 us (30%)
  Pallas kernels  9.16 us (19%)
  between operations  1.44 us (3%)
  local copies, waits for them, and re-layouts  1.14 us (2%)
  other arithmetic  0.99 us (2%)
    ppermute x4, waiting for transfers between devices, swap_pairs(): lax.ppermute(even_block, 'space', evens)  14.1 us
    ppermute x4, starting transfers between devices, swap_pairs(): lax.ppermute(even_block, 'space', evens)  9.77 us
    pallas_call x7, Pallas kernels, call(): pl.pallas_call(kernel, out_shape=tuple((jax.ShapeDtypeStruct(o, F32) for...  9.16 us
    ppermute x3, waiting for transfers between devices, across(): return lax.ppermute(block, 'src', [(i, i ^ mask) for i in range(count)])  6.02 us
    ppermute x4, starting transfers between devices, swap_pairs(): lax.ppermute(odd_block, 'space', odds)  2.81 us
    ppermute x3, starting transfers between devices, across(): return lax.ppermute(block, 'src', [(i, i ^ mask) for i in range(count)])  1.7 us
    another operation x1, local copies, waits for them, and re-layouts, block_step(): edges.append(jnp.stack([model, fields[0, 0, at], fields[0, 2, at]], 0))  1.04 us
  transfers between devices with their start and end apart: 11, of which 5 were waited for; matrix products, arithmetic and copies ran while one was open for 0% of the time, Pallas kernels for 8%

profile of v2, /device:TPU:0, one launch (start us, length us, event | category | flops | bytes accessed | tf_op | source)
XLA Modules:
  0.0 47.2 jit_solution(762411133495572666)
XLA Ops:
  0.6 0.0 copy-start
  0.7 1.0 %slice_bitcast_fusion.3 = (f32[1,128,128]{2,1,0:T(8,128)S(1)}, f32[1,128,128]{2,1,0:T(8,128)S(1)}, f32[1,128,128]{2,1,0:T(8,128)S(1)}, f32[1,128,128]{2,1,0:T(8,128)S(1)}) fusion(f32[1,4,4,128,128]{4,3,2,1,0:T(8,128)} %f_ref.3), kind=kLoop, calls=%fused_computation.8 | loop fusion | bytes 524288 | tf_op jit(solution)/shard_map/stack;squeeze | solution.py:295
  1.7 1.0 %slice_select_fusion.1 = (f32[1,128,128]{2,1,0:T(8,128)S(1)}, f32[1,128,128]{2,1,0:T(8,128)S(1)}) fusion(f32[4,128,128]{2,1,0:T(8,128)} %refs_5_.1, f32[4,128,128]{2,1,0:T(8,128)} %refs_4_.1, pred[]{:T(512)S(6)} %eq.12), kind=kLoop, calls=%fused_computation.9 | loop fusion | flops 32768 | bytes 393217 | tf_op jit(solution)/shard_map/jit(_where)/select_n | solution.py:294
  2.7 0.0 copy-start.1
  2.7 0.0 copy-start.2
  2.7 0.8 %collective-permute-start.1 = (f32[3,128,128]{2,1,0:T(8,128)S(1)}, f32[3,128,128]{2,1,0:T(8,128)S(1)}, u32[]{:S(2)}, u32[]{:S(2)}) collective-permute-start(f32[3,128,128]{2,1,0:T(8,128)S(1)} %get-tuple-element.34), channel_id=1, source_target_pairs={{1,2},{2,1},{5,6},{6,5},{9,10},{10,9},{13,14},{14,13},{17,18},{18,... | collective-permute-start | bytes 589832 | tf_op jit(solution)/shard_map/ppermute | solution.py:268
  3.5 5.9 %collective-permute-start = (f32[3,128,128]{2,1,0:T(8,128)S(1)}, f32[3,128,128]{2,1,0:T(8,128)S(1)}, u32[]{:S(2)}, u32[]{:S(2)}) collective-permute-start(f32[3,128,128]{2,1,0:T(8,128)S(1)} %get-tuple-element.35), channel_id=1, source_target_pairs={{0,1},{1,0},{2,3},{3,2},{4,5},{5,4},{6,7},{7,6},{8,9},{9,8},{10,11... | collective-permute-start | bytes 589832 | tf_op jit(solution)/shard_map/ppermute | solution.py:268
  10.1 0.1 stack.35.meta.refs_0_
  10.2 0.0 copy-done
  10.2 0.0 copy-done.1
  10.2 0.0 copy-done.2
  10.2 1.1 %shard_map.59 = (f32[4,128,128]{2,1,0:T(8,128)S(1)}, f32[4,128,128]{2,1,0:T(8,128)S(1)}, f32[4,128,128]{2,1,0:T(8,128)S(1)}) custom-call(s32[5]{0:T(128)S(1)} %stack.35.meta.refs_0_, f32[1,4,4,128,128]{4,3,2,1,0:T(8,128)S(1)} %copy-done, f32[4,128,128]{2,1,0:T(8,128)S(1)} %copy-done.1, f32[4,128,128]{2,1,0:T(8,128)S(1)} %copy-done.2), custom_call_target="tpu_custom_call" | custom-call | flops 11796580 | bytes 2359316 | tf_op jit(solution)/shard_map/pallas_call | solution.py:23
  11.4 0.1 collective-permute-start.3
  11.4 0.7 %collective-permute-start.4 = (f32[4,128,128]{2,1,0:T(8,128)S(1)}, f32[4,128,128]{2,1,0:T(8,128)S(1)}, u32[]{:S(2)}, u32[]{:S(2)}) collective-permute-start(f32[4,128,128]{2,1,0:T(8,128)S(1)} %get-tuple-element.17), channel_id=1, source_target_pairs={{1,2},{2,1},{5,6},{6,5},{9,10},{10,9},{13,14},{14,13},{17,18},{18,... | collective-permute-start | bytes 786440 | tf_op jit(solution)/shard_map/ppermute | solution.py:268
  12.1 0.0 collective-permute-done.1.o1
  12.1 2.7 %collective-permute-done.e1 = f32[3,128,128]{2,1,0:T(8,128)S(1)} collective-permute-done((f32[3,128,128]{2,1,0:T(8,128)S(1)}, f32[3,128,128]{2,1,0:T(8,128)S(1)}, u32[]{:S(2)}, u32[]{:S(2)}) %collective-permute-start) | collective-permute-done | bytes 196640 | tf_op jit(solution)/shard_map/ppermute | solution.py:268
  14.9 0.1 collective-permute-start.2
  15.0 4.7 %collective-permute-done.3.e2 = f32[4,128,128]{2,1,0:T(8,128)S(1)} collective-permute-done((f32[4,128,128]{2,1,0:T(8,128)S(1)}, f32[4,128,128]{2,1,0:T(8,128)S(1)}, u32[]{:S(2)}, u32[]{:S(2)}) %collective-permute-start.3) | collective-permute-done | bytes 262176 | tf_op jit(solution)/shard_map/ppermute | solution.py:268
  19.7 0.0 collective-permute-done.4.o2
  19.7 0.0 collective-permute-done.2.m
  19.7 2.3 %shard_map.61 = (f32[520,128]{1,0:T(8,128)S(1)}, f32[2,2,4,128,128]{4,3,2,1,0:T(8,128)S(1)}, f32[2,2,2,128,128]{4,3,2,1,0:T(8,128)S(1)}, f32[2,128,128]{2,1,0:T(...) custom-call(s32[5]{0:T(128)S(1)} %stack.35.meta.refs_0_, f32[1,4,4,128,128]{4,3,2,1,0:T(8,128)S(1)} %copy-done, ...), custom_call_target="tpu_custom_call" | custom-call | flops 25579620 | bytes 5115924 | tf_op jit(solution)/shard_map/pallas_call | solution.py:23
  22.0 1.6 %collective-permute-start.7 = (f32[520,128]{1,0:T(8,128)S(1)}, f32[520,128]{1,0:T(8,128)S(1)}, u32[]{:S(2)}, u32[]{:S(2)}) collective-permute-start(f32[520,128]{1,0:T(8,128)S(1)} %get-tuple-element.23.mine), channel_id=1, source_target_pairs={{0,8},{4,12},{8,0},{12,4},{1,9},{5,13},{9,1},{13,5},{2,10},{6,14},... | collective-permute-start | bytes 798728 | tf_op jit(solution)/shard_map/ppermute | solution.py:273
  23.6 6.0 %collective-permute-done.7.other = f32[520,128]{1,0:T(8,128)S(1)} collective-permute-done((f32[520,128]{1,0:T(8,128)S(1)}, f32[520,128]{1,0:T(8,128)S(1)}, u32[]{:S(2)}, u32[]{:S(2)}) %collective-permute-start.7) | collective-permute-done | bytes 266272 | tf_op jit(solution)/shard_map/ppermute | solution.py:273
  29.6 0.1 shard_map.62.refs_1_
  29.7 0.1 collective-permute-start.8
  29.7 1.8 %collective-permute-start.5 = (f32[6,128,128]{2,1,0:T(8,128)S(1)}, f32[6,128,128]{2,1,0:T(8,128)S(1)}, u32[]{:S(2)}, u32[]{:S(2)}) collective-permute-start(f32[6,128,128]{2,1,0:T(8,128)S(1)} %get-tuple-element.21), channel_id=1, source_target_pairs={{0,1},{1,0},{2,3},{3,2},{4,5},{5,4},{6,7},{7,6},{8,9},{9,8},{10,11... | collective-permute-start | bytes 1179656 | tf_op jit(solution)/shard_map/ppermute | solution.py:268
  31.6 0.7 %collective-permute-start.6 = (f32[6,128,128]{2,1,0:T(8,128)S(1)}, f32[6,128,128]{2,1,0:T(8,128)S(1)}, u32[]{:S(2)}, u32[]{:S(2)}) collective-permute-start(f32[6,128,128]{2,1,0:T(8,128)S(1)} %get-tuple-element.22), channel_id=1, source_target_pairs={{1,2},{2,1},{5,6},{6,5},{9,10},{10,9},{13,14},{14,13},{17,18},{18,... | collective-permute-start | bytes 1179656 | tf_op jit(solution)/shard_map/ppermute | solution.py:268
  32.2 1.0 %shard_map.63.refs_3_ = f32[4,128,128]{2,1,0:T(8,128)S(1)} custom-call(s32[5]{0:T(128)S(1)} %stack.35.meta.refs_0_, f32[4,128,128]{2,1,0:T(8,128)S(1)} %copy-done.1, f32[4,128,128]{2,1,0:T(8,128)S(1)} %copy-done.2, f32[3,128,128]{2,1,0:T(8,128)S(1)} %collective-permute-done.e1, f32[3,128,128]{2,1,0:T(8,128)S(1)} %collective-permute-done.1.o1, ...), custom_call_target="tpu_custom_call" | custom-call | flops 6553700 | bytes 1310740 | tf_op jit(solution)/shard_map/pallas_call | solution.py:23
  33.3 0.0 collective-permute-done.8.refs_2_
  33.3 1.5 %shard_map.64 = (f32[2,4,128,128]{3,2,1,0:T(8,128)}, f32[4,128,128]{2,1,0:T(8,128)S(1)}, f32[2,128,128]{2,1,0:T(8,128)S(1)}, f32[2,128,128]{2,1,0:T(8,128)S(1)}) custom-call(s32[5]{0:T(128)S(1)} %stack.35.meta.refs_0_, f32[2,4,128,128]{3,2,1,0:T(8,128)S(1)} %shard_map.62.refs_1_, f32[2,4,128,128]{3,2,1,0:T(8,128)S(1)} %collective-permute-done.8.refs_2_, ...), custom_call_target="tpu_custom_call" | custom-call | flops 14418020 | bytes 2883604 | tf_op jit(solution)/shard_map/pallas_call | solution.py:23
  34.8 1.9 %collective-permute-start.9 = (f32[2,128,128]{2,1,0:T(8,128)S(1)}, f32[2,128,128]{2,1,0:T(8,128)S(1)}, u32[]{:S(2)}, u32[]{:S(2)}) collective-permute-start(f32[2,128,128]{2,1,0:T(8,128)S(1)} %get-tuple-element.25), channel_id=1, source_target_pairs={{0,1},{1,0},{2,3},{3,2},{4,5},{5,4},{6,7},{7,6},{8,9},{9,8},{10,11... | collective-permute-start | bytes 393224 | tf_op jit(solution)/shard_map/ppermute | solution.py:268
  36.8 0.7 %collective-permute-start.10 = (f32[2,128,128]{2,1,0:T(8,128)S(1)}, f32[2,128,128]{2,1,0:T(8,128)S(1)}, u32[]{:S(2)}, u32[]{:S(2)}) collective-permute-start(f32[2,128,128]{2,1,0:T(8,128)S(1)} %get-tuple-element.26), channel_id=1, source_target_pairs={{1,2},{2,1},{5,6},{6,5},{9,10},{10,9},{13,14},{14,13},{17,18},{18,... | collective-permute-start | bytes 393224 | tf_op jit(solution)/shard_map/ppermute | solution.py:268
  37.4 4.4 %collective-permute-done.5.re = f32[6,128,128]{2,1,0:T(8,128)S(1)} collective-permute-done((f32[6,128,128]{2,1,0:T(8,128)S(1)}, f32[6,128,128]{2,1,0:T(8,128)S(1)}, u32[]{:S(2)}, u32[]{:S(2)}) %collective-permute-start.5) | collective-permute-done | bytes 393248 | tf_op jit(solution)/shard_map/ppermute | solution.py:268
  41.8 0.0 collective-permute-done.6.ro
  41.8 2.3 %collective-permute-done.9.ce = f32[2,128,128]{2,1,0:T(8,128)S(1)} collective-permute-done((f32[2,128,128]{2,1,0:T(8,128)S(1)}, f32[2,128,128]{2,1,0:T(8,128)S(1)}, u32[]{:S(2)}, u32[]{:S(2)}) %collective-permute-start.9) | collective-permute-done | bytes 131104 | tf_op jit(solution)/shard_map/ppermute | solution.py:268
  44.1 0.0 collective-permute-done.10.co
  44.1 3.1 %shard_map.65 = f32[1,2,4,128,128]{4,3,2,1,0:T(8,128)} custom-call(s32[5]{0:T(128)S(1)} %stack.35.meta.refs_0_, f32[2,2,4,128,128]{4,3,2,1,0:T(8,128)S(1)} %get-tuple-element.18.st_ref, f32[2,2,2,128,128]{4,3,2,1,0:T(8,128)S(1)} %get-tuple-element.19.hb_ref, f32[2,128,128]{2,1,0:T(8,128)S(1)} %get-tuple-element.20.hc_ref, ...), custom_call_target="tpu_custom_call" | custom-call | flops 17694820 | bytes 3538964 | tf_op jit(solution)/shard_map/pallas_call | solution.py:23
  (2 shorter events, 0.0 us)
Async XLA Ops:
  0.6 9.6 %copy-start = (f32[1,4,4,128,128]{4,3,2,1,0:T(8,128)S(1)}, f32[1,4,4,128,128]{4,3,2,1,0:T(8,128)}, u32[]{:S(2)}) copy-start(f32[1,4,4,128,128]{4,3,2,1,0:T(8,128)} %f_ref.3) | copy-start | bytes 3145732
  2.7 7.5 %copy-start.1 = (f32[4,128,128]{2,1,0:T(8,128)S(1)}, f32[4,128,128]{2,1,0:T(8,128)}, u32[]{:S(2)}) copy-start(f32[4,128,128]{2,1,0:T(8,128)} %refs_4_.1) | copy-start | bytes 786436
  2.7 7.5 %copy-start.2 = (f32[4,128,128]{2,1,0:T(8,128)S(1)}, f32[4,128,128]{2,1,0:T(8,128)}, u32[]{:S(2)}) copy-start(f32[4,128,128]{2,1,0:T(8,128)} %refs_5_.1) | copy-start | bytes 786436
  2.7 9.4 %collective-permute-start.1 = (f32[3,128,128]{2,1,0:T(8,128)S(1)}, f32[3,128,128]{2,1,0:T(8,128)S(1)}, u32[]{:S(2)}, u32[]{:S(2)}) collective-permute-start(f32[3,128,128]{2,1,0:T(8,128)S(1)} %get-tuple-element.34), channel_id=1, source_target_pairs={{1,2},{2,1},{5,6},{6,5},{9,10},{10,9},{13,14},{14,13},{17,18},{18,... | collective-permute-start | bytes 589832 | tf_op jit(solution)/shard_map/ppermute | solution.py:268
  3.5 11.3 %collective-permute-start = (f32[3,128,128]{2,1,0:T(8,128)S(1)}, f32[3,128,128]{2,1,0:T(8,128)S(1)}, u32[]{:S(2)}, u32[]{:S(2)}) collective-permute-start(f32[3,128,128]{2,1,0:T(8,128)S(1)} %get-tuple-element.35), channel_id=1, source_target_pairs={{0,1},{1,0},{2,3},{3,2},{4,5},{5,4},{6,7},{7,6},{8,9},{9,8},{10,11... | collective-permute-start | bytes 589832 | tf_op jit(solution)/shard_map/ppermute | solution.py:268
  11.4 8.3 %collective-permute-start.3 = (f32[4,128,128]{2,1,0:T(8,128)S(1)}, f32[4,128,128]{2,1,0:T(8,128)S(1)}, u32[]{:S(2)}, u32[]{:S(2)}) collective-permute-start(f32[4,128,128]{2,1,0:T(8,128)S(1)} %get-tuple-element.16), channel_id=1, source_target_pairs={{0,1},{1,0},{2,3},{3,2},{4,5},{5,4},{6,7},{7,6},{8,9},{9,8},{10,11... | collective-permute-start | bytes 786440 | tf_op jit(solution)/shard_map/ppermute | solution.py:268
  11.4 8.3 %collective-permute-start.4 = (f32[4,128,128]{2,1,0:T(8,128)S(1)}, f32[4,128,128]{2,1,0:T(8,128)S(1)}, u32[]{:S(2)}, u32[]{:S(2)}) collective-permute-start(f32[4,128,128]{2,1,0:T(8,128)S(1)} %get-tuple-element.17), channel_id=1, source_target_pairs={{1,2},{2,1},{5,6},{6,5},{9,10},{10,9},{13,14},{14,13},{17,18},{18,... | collective-permute-start | bytes 786440 | tf_op jit(solution)/shard_map/ppermute | solution.py:268
  14.9 4.8 %collective-permute-start.2 = (f32[2,128,128]{2,1,0:T(8,128)S(1)}, f32[2,128,128]{2,1,0:T(8,128)S(1)}, u32[]{:S(2)}, u32[]{:S(2)}) collective-permute-start(f32[2,128,128]{2,1,0:T(8,128)S(1)} %shard_map.60), channel_id=1, source_target_pairs={{0,4},{4,0},{8,12},{12,8},{1,5},{5,1},{9,13},{13,9},{2,6},{6,2},{1... | collective-permute-start | bytes 393224 | tf_op jit(solution)/shard_map/ppermute | solution.py:273
  22.0 7.6 %collective-permute-start.7 = (f32[520,128]{1,0:T(8,128)S(1)}, f32[520,128]{1,0:T(8,128)S(1)}, u32[]{:S(2)}, u32[]{:S(2)}) collective-permute-start(f32[520,128]{1,0:T(8,128)S(1)} %get-tuple-element.23.mine), channel_id=1, source_target_pairs={{0,8},{4,12},{8,0},{12,4},{1,9},{5,13},{9,1},{13,5},{2,10},{6,14},... | collective-permute-start | bytes 798728 | tf_op jit(solution)/shard_map/ppermute | solution.py:273
  29.7 3.6 %collective-permute-start.8 = (f32[2,4,128,128]{3,2,1,0:T(8,128)S(1)}, f32[2,4,128,128]{3,2,1,0:T(8,128)S(1)}, u32[]{:S(2)}, u32[]{:S(2)}) collective-permute-start(f32[2,4,128,128]{3,2,1,0:T(8,128)S(1)} %shard_map.62.refs_1_), channel_id=1, source_target_pairs={{0,4},{4,0},{8,12},{12,8},{1,5},{5,1},{9,13},{13,9},{2,6},{6,2},{1... | collective-permute-start | bytes 1572872 | tf_op jit(solution)/shard_map/ppermute | solution.py:273
  29.7 12.1 %collective-permute-start.5 = (f32[6,128,128]{2,1,0:T(8,128)S(1)}, f32[6,128,128]{2,1,0:T(8,128)S(1)}, u32[]{:S(2)}, u32[]{:S(2)}) collective-permute-start(f32[6,128,128]{2,1,0:T(8,128)S(1)} %get-tuple-element.21), channel_id=1, source_target_pairs={{0,1},{1,0},{2,3},{3,2},{4,5},{5,4},{6,7},{7,6},{8,9},{9,8},{10,11... | collective-permute-start | bytes 1179656 | tf_op jit(solution)/shard_map/ppermute | solution.py:268
  31.6 10.2 %collective-permute-start.6 = (f32[6,128,128]{2,1,0:T(8,128)S(1)}, f32[6,128,128]{2,1,0:T(8,128)S(1)}, u32[]{:S(2)}, u32[]{:S(2)}) collective-permute-start(f32[6,128,128]{2,1,0:T(8,128)S(1)} %get-tuple-element.22), channel_id=1, source_target_pairs={{1,2},{2,1},{5,6},{6,5},{9,10},{10,9},{13,14},{14,13},{17,18},{18,... | collective-permute-start | bytes 1179656 | tf_op jit(solution)/shard_map/ppermute | solution.py:268
  34.8 9.2 %collective-permute-start.9 = (f32[2,128,128]{2,1,0:T(8,128)S(1)}, f32[2,128,128]{2,1,0:T(8,128)S(1)}, u32[]{:S(2)}, u32[]{:S(2)}) collective-permute-start(f32[2,128,128]{2,1,0:T(8,128)S(1)} %get-tuple-element.25), channel_id=1, source_target_pairs={{0,1},{1,0},{2,3},{3,2},{4,5},{5,4},{6,7},{7,6},{8,9},{9,8},{10,11... | collective-permute-start | bytes 393224 | tf_op jit(solution)/shard_map/ppermute | solution.py:268
  36.8 7.3 %collective-permute-start.10 = (f32[2,128,128]{2,1,0:T(8,128)S(1)}, f32[2,128,128]{2,1,0:T(8,128)S(1)}, u32[]{:S(2)}, u32[]{:S(2)}) collective-permute-start(f32[2,128,128]{2,1,0:T(8,128)S(1)} %get-tuple-element.26), channel_id=1, source_target_pairs={{1,2},{2,1},{5,6},{6,5},{9,10},{10,9},{13,14},{14,13},{17,18},{18,... | collective-permute-start | bytes 393224 | tf_op jit(solution)/shard_map/ppermute | solution.py:268

commit v3 on v0

v3 whole, which is shorter than its diff:
```python
import math

import jax
import jax.numpy as jnp
from jax import lax
from jax.experimental import pallas as pl
from jax.experimental.pallas import tpu as pltpu
from jax.sharding import PartitionSpec as P


speed_gain = 0.25
diffuse_gain = 0.15
step_size = 0.1
penalty_gain = 50.0

VMEM = pl.BlockSpec(memory_space=pltpu.VMEM)
F32 = jnp.float32


def call(kernel, outs, args, scratch=(), specs=None, extra=()):
    size = sum(math.prod(o) for o in outs) + sum(a.size for a in args)
    return pl.pallas_call(
        kernel,
        out_shape=tuple(jax.ShapeDtypeStruct(o, F32) for o in outs),
        in_specs=specs or [VMEM for _ in args],
        out_specs=tuple(VMEM for _ in outs),
        scratch_shapes=[pltpu.VMEM(s, F32) for s in scratch] + list(extra),
        compiler_params=pltpu.CompilerParams(vmem_limit_bytes=16 << 20),
        cost_estimate=pl.CostEstimate(flops=20 * size, bytes_accessed=4 * size, transcendentals=0),
    )(*args)


class Plane:
    def __init__(self, ref, *at, base=0):
        self.ref, self.at, self.base = ref, at, base

    def _rows(self, r, n):
        return (*self.at, slice(self.base + r, self.base + r + n))

    def get(self, r, n):
        return self.ref[self._rows(r, n)]

    def put(self, r, n, value):
        self.ref[self._rows(r, n)] = value


class Work:
    def __init__(self, weight_ref, ny, nz):
        self.ny, self.n = ny, 32 if ny % 32 == 0 else ny
        shape = (self.n, nz)
        row = lax.broadcasted_iota(jnp.int32, shape, 0)
        col = lax.broadcasted_iota(jnp.int32, shape, 1)
        self.top, self.bottom = row == 0, row == self.n - 1
        self.left, self.right = col == 0, col == nz - 1
        self.nz = nz
        if weight_ref is not None:
            self.a = jnp.broadcast_to(weight_ref[0:1], shape)
        here = lax.axis_index("space")
        self.even = here % 2 == 0
        self.has = (here > 0, here < lax.axis_size("space") - 1)
        self.first_core = lax.axis_index("src") % 2 == 0

    def blocks(self):
        return range(0, self.ny, self.n)

    def get(self, plane, r):
        return plane.get(r, self.n)

    def put(self, plane, r, value):
        plane.put(r, self.n, value)

    def shifts(self, plane, r, edge):
        n, v = self.n, plane.get(r, self.n)

        def fill(test, moved):
            return jnp.where(test, v if edge else 0.0, moved)

        up = plane.get(r - 1, n) if r > 0 else fill(self.top, pltpu.roll(v, 1, 0))
        last = r + n == self.ny
        down = fill(self.bottom, pltpu.roll(v, n - 1, 0)) if last else plane.get(r + 1, n)
        left = fill(self.left, pltpu.roll(v, 1, 1))
        right = fill(self.right, pltpu.roll(v, self.nz - 1, 1))
        return v, up, down, left, right

    def flat(self, plane, r):
        v, up, down, left, right = self.shifts(plane, r, False)
        return v, ((up + down) + (left + right)) - 6.0 * v

    def lap(self, plane, below, above, r):
        v, total = self.flat(plane, r)
        for other in (below, above):
            if other is not None:
                total = total + self.get(other, r)
        return v, total

    def ahead(self, v, before):
        return (1.0 + self.a) * v - self.a * before

    def step(self, out, now, before, coef, below, above, each=None):
        for r in self.blocks():
            v, total = self.lap(now, below, above, r)
            value = self.ahead(v, self.get(before, r)) + self.get(coef, r) * total
            if out is not None:
                self.put(out, r, value)
            if each is not None:
                each(r, v, total, value)

    def coefficient(self, v, c):
        return self.a * speed_gain * v**2 + (1.0 - self.a) * diffuse_gain / c

    def pack(self, even_ref, odd_ref, lows, highs):
        for k, (low, high) in enumerate(zip(lows, highs)):
            for r in self.blocks():
                lo, hi = self.get(low, r), self.get(high, r)
                self.put(Plane(even_ref, k), r, jnp.where(self.even, hi, lo))
                self.put(Plane(odd_ref, k), r, jnp.where(self.even, lo, hi))

    def unpack(self, even_ref, odd_ref, k, r):
        e, o = self.get(Plane(even_ref, k), r), self.get(Plane(odd_ref, k), r)
        return jnp.where(self.even, o, e), jnp.where(self.even, e, o)


def near(make, i, tile, ends=(None, None)):
    return (make(i - 1) if i > 0 else ends[0]), (make(i + 1) if i < tile - 1 else ends[1])


def isolated_kernel(
    labels, f_in, v_in, c_in,
    ae, ao, be, bo, ce, co, coef, one, acc, w, f, v, c, two, label, sems,
):
    copies = [
        pltpu.make_async_copy(src, dst, sems.at[n])
        for n, (src, dst) in enumerate(((labels, label), (v_in, v), (c_in, c), (f_in, f)))
    ]
    for copy in copies:
        copy.start()
    tile, ny, nz = v.shape
    copies[0].wait()
    w[...] = jnp.full(w.shape, label[0].astype(F32), F32)
    k = Work(w, ny, nz)
    copies[1].wait()
    copies[2].wait()
    edge = (0, tile - 1)
    for i in range(tile):
        for r in k.blocks():
            k.put(Plane(coef, i), r, k.coefficient(v[i, r:r + k.n], c[i, r:r + k.n]))
    copies[3].wait()
    for n in range(2):
        for i in range(tile):

            def each(r, value, total, out, i=i):
                k.put(Plane(acc, i), r, f[0, 2, i, r:r + k.n] * total)

            k.step(
                Plane(one, n, i), Plane(f, 0, 2 * n, i), Plane(f, 0, 2 * n + 1, i), Plane(coef, i),
                *near(lambda j: Plane(f, 0, 2 * n, j), i, tile), each if n == 0 else None,
            )
        for s, i in enumerate(edge):
            k.step(
                Plane(two, n, s), Plane(one, n, i), Plane(f, 0, 2 * n, i), Plane(coef, i),
                *near(lambda j: Plane(one, n, j), i, tile),
            )
    sides = [
        [Plane(coef, i), Plane(f, 0, 0, i), Plane(f, 0, 2, i), Plane(one, 0, i)] for i in edge
    ]
    k.pack(ae, ao, *sides)
    k.pack(be, bo, *([Plane(two, 0, s), Plane(one, 1, i)] for s, i in enumerate(edge)))
    for r in k.blocks():
        lo, hi = (
            jnp.where(k.first_core, v[i, r:r + k.n], c[i, r:r + k.n]) for i in edge
        )
        k.put(Plane(ce, 0), r, jnp.where(k.even, hi, lo))
        k.put(Plane(co, 0), r, jnp.where(k.even, lo, hi))
    k.pack(ce.at[1:], co.at[1:], [Plane(two, 1, 0)], [Plane(two, 1, 1)])


def inner_kernel(w, f, coef, one, acc, ae, ao, acc1, rim, ends, two, three, halo, zero):
    tile, ny, nz = coef.shape
    k = Work(w, ny, nz)
    edge = (0, tile - 1)
    for r in k.blocks():
        parts = [k.unpack(ae, ao, m, r) for m in range(4)]
        for s, i in enumerate(edge):
            h = [p[s] for p in parts]
            cf, w0, u0 = coef[i, r:r + k.n], f[0, 2, i, r:r + k.n], f[0, 0, i, r:r + k.n]
            k.put(Plane(halo, s, 0), r, h[0])
            k.put(Plane(halo, s, 1), r, h[3] + h[0] * u0)
            k.put(Plane(ends, 0, s), r, one[0, i, r:r + k.n] + cf * h[1])
            k.put(Plane(ends, 1, s), r, one[1, i, r:r + k.n] + cf * h[2])
            k.put(Plane(zero, s), r, acc[i, r:r + k.n] + w0 * h[1])

    def first(n, i):
        return Plane(ends, n, edge.index(i)) if i in edge else Plane(one, n, i)

    def inside(i):
        return Plane(acc1, base=(i - 1) * ny)

    outside = (Plane(halo, 0, 1), Plane(halo, 1, 1))
    for i in range(tile):

        def each(r, value, total, out, i=i):
            term = k.get(first(1, i), r) * total
            if i in edge:
                s = edge.index(i)
                k.put(Plane(rim, s), r, zero[s, r:r + k.n] + term)
            else:
                k.put(inside(i), r, acc[i, r:r + k.n] + term)

        k.step(
            Plane(two, 0, i), first(0, i), Plane(f, 0, 0, i), Plane(coef, i),
            *near(lambda j: first(0, j), i, tile, outside), each,
        )
    for i in range(1, tile - 1):
        k.step(
            Plane(two, 1, i), first(1, i), Plane(f, 0, 2, i), Plane(coef, i),
            *near(lambda j: first(1, j), i, tile),
        )
    for i in range(1, tile - 1):

        def each(r, value, total, out, i=i):
            k.put(inside(i), r, k.get(inside(i), r) + two[1, i, r:r + k.n] * total)

        k.step(
            Plane(three, i), Plane(two, 0, i), first(0, i), Plane(coef, i),
            *near(lambda j: Plane(two, 0, j), i, tile), each,
        )
    rows = (tile - 2) * ny
    acc1[rows:] = jnp.broadcast_to(w[0:1], (acc1.shape[0] - rows, nz))
    for i in edge:
        for r in k.blocks():
            k.put(Plane(two, 1, i), r, jnp.zeros((k.n, nz), F32))


def outer_kernel(w, f, coef, one, ends, two, halo, rim, be, bo, acc2, wtwo, uthree, beyond, d):
    tile, ny, nz = coef.shape
    k = Work(w, ny, nz)
    edge = (0, tile - 1)
    for s, i in enumerate(edge):
        for r in k.blocks():
            k.put(Plane(d, s), r, halo[s, 0, r:r + k.n] * f[0, 0, i, r:r + k.n])
    for r in k.blocks():
        u2, w1 = k.unpack(be, bo, 0, r), k.unpack(be, bo, 1, r)
        for s, i in enumerate(edge):
            h = halo[s, 0, r:r + k.n]
            dv, total = k.flat(Plane(d, s), r)
            total = total + ends[0, s, r:r + k.n]
            k.put(Plane(beyond, s, 0), r, u2[s] + (1.0 + k.a) * dv + h * total)
            k.put(Plane(beyond, s, 1), r, w1[s] + h * f[0, 2, i, r:r + k.n])

    def first(n, i):
        return Plane(ends, n, edge.index(i)) if i in edge else Plane(one, n, i)

    for s, i in enumerate(edge):
        k.step(
            Plane(wtwo, s), first(1, i), Plane(f, 0, 2, i), Plane(coef, i),
            *near(lambda j: first(1, j), i, tile, (Plane(beyond, 0, 1), Plane(beyond, 1, 1))),
        )

        def each(r, value, total, out, s=s):
            k.put(
                Plane(acc2, base=s * ny), r,
                rim[s, r:r + k.n] + wtwo[s, r:r + k.n] * total,
            )

        k.step(
            Plane(uthree, s), Plane(two, 0, i), first(0, i), Plane(coef, i),
            *near(lambda j: Plane(two, 0, j), i, tile, (Plane(beyond, 0, 0), Plane(beyond, 1, 0))),
            each,
        )


def early_kernel(w, coef, one, ends, two, wtwo, three, uthree, pe, po, wthree):
    tile, ny, nz = coef.shape
    k = Work(w, ny, nz)
    edge = (0, tile - 1)

    def second(i):
        return Plane(wtwo, edge.index(i)) if i in edge else Plane(two, 1, i)

    for i in range(1, tile - 1):
        k.step(
            Plane(wthree, i - 1), second(i), Plane(one, 1, i), Plane(coef, i),
            *near(second, i, tile),
        )

    def planes(i, j):
        return [
            Plane(two, 0, i), Plane(three, i), Plane(three, j),
            Plane(two, 1, i), Plane(wthree, i - 1), Plane(wthree, j - 1),
        ]

    k.pack(pe, po, planes(1, 2), planes(tile - 2, tile - 3))


def pick_kernel(ce, co, out):
    out[0], out[1] = ce[0], co[0]


def late_kernel(
    w, v, c, f, coef, ends, two, wtwo, halo, beyond, ce, co, other,
    pen, wthree, base, last, logs, rims, d,
):
    tile, ny, nz = coef.shape
    k = Work(w, ny, nz)
    edge = (0, tile - 1)
    for i in range(tile):
        for r in k.blocks():
            k.put(Plane(logs, i + 1), r, jnp.log(c[i, r:r + k.n]))
    for r in k.blocks():
        mine = k.unpack(ce, co, 0, r)
        theirs = k.unpack(other.at[0:1], other.at[1:2], 0, r)
        w2 = k.unpack(ce, co, 1, r)
        for s, i in enumerate(edge):
            vel = jnp.where(k.first_core, mine[s], theirs[s])
            con = jnp.where(k.first_core, theirs[s], mine[s])
            con = jnp.where(k.has[s], con, 1.0)
            k.put(Plane(rims, s), r, jnp.where(k.has[s], vel, v[i, r:r + k.n]))
            k.put(
                Plane(logs, (0, tile + 1)[s]), r,
                jnp.where(k.has[s], jnp.log(con), logs[i + 1, r:r + k.n]),
            )
            k.put(Plane(d, s), r, halo[s, 0, r:r + k.n] * f[0, 2, i, r:r + k.n])
            k.put(Plane(last, s), r, w2[s])
    for s, i in enumerate(edge):
        for r in k.blocks():
            dv, total = k.flat(Plane(d, s), r)
            total = total + ends[1, s, r:r + k.n]
            k.put(
                Plane(last, s), r,
                last[s, r:r + k.n] + (1.0 + k.a) * dv + halo[s, 0, r:r + k.n] * total,
            )

    def second(i):
        return Plane(wtwo, edge.index(i)) if i in edge else Plane(two, 1, i)

    for s, i in enumerate(edge):
        k.step(
            Plane(wthree, s), second(i), Plane(ends, 1, s), Plane(coef, i),
            *near(second, i, tile, (Plane(last, 0), Plane(last, 1))),
        )
        k.step(
            Plane(base, s, 0), Plane(beyond, s, 0), Plane(halo, s, 1), Plane(halo, s, 0),
            Plane(two, 0, i), None,
        )
        k.step(
            Plane(base, s, 1), Plane(last, s), Plane(beyond, s, 1), Plane(halo, s, 0),
            Plane(wtwo, s), None,
        )
    for i in range(tile):
        below, above = near(lambda j: Plane(v, j), i, tile, (Plane(rims, 0), Plane(rims, 1)))
        for r in k.blocks():
            vx = (k.get(above, r) - k.get(below, r)) * 0.5
            lx = (logs[i + 2, r:r + k.n] - logs[i, r:r + k.n]) * 0.5
            _, up, down, left, right = k.shifts(Plane(v, i), r, True)
            vy, vz = (down - up) * 0.5, (right - left) * 0.5
            _, up, down, left, right = k.shifts(Plane(logs, i + 1), r, True)
            ly, lz = (down - up) * 0.5, (right - left) * 0.5
            ca = vy * lz - vz * ly
            cb = vz * lx - vx * lz
            cc = vx * ly - vy * lx
            k.put(Plane(pen, i), r, penalty_gain * (ca * ca + cb * cb + cc * cc))


def weigh_kernel(acc1, acc2, far1, far2, out):
    _, tile, ny, nz = out.shape
    k = Work(None, ny, nz)
    rows = (tile - 2) * ny
    labels = [jnp.broadcast_to(ref[rows:rows + 1], (k.n, nz)) for ref in (acc1, far1)]
    for i in range(tile):
        for r in k.blocks():
            if i in (0, tile - 1):
                at = (0 if i == 0 else ny) + r
                mine, other = acc2[at:at + k.n], far2[at:at + k.n]
            else:
                at = (i - 1) * ny + r
                mine, other = acc1[at:at + k.n], far1[at:at + k.n]
            k.put(Plane(out, 0, i), r, labels[0] * mine + labels[1] * other)
            k.put(Plane(out, 1, i), r, (1.0 - labels[0]) * mine + (1.0 - labels[1]) * other)


def renew(scale, value, part, rest, pen):
    return value * jnp.exp(-step_size * jnp.tanh(scale * (part + rest) + pen))


def renew_kernel(scale, w, part, rest, pen, v, c, coef, e, o):
    tile, ny, nz = v.shape
    k = Work(w, ny, nz)
    sound = k.a == 1.0
    for i in range(tile):
        for r in k.blocks():
            at = slice(r, r + k.n)
            new = renew(
                scale,
                jnp.where(sound, v[i, at], c[i, at]),
                jnp.where(sound, part[0, i, at], part[1, i, at]),
                jnp.where(sound, rest[0, i, at], rest[1, i, at]),
                pen[i, at],
            )
            k.put(
                Plane(coef, i), r,
                jnp.where(sound, speed_gain * new**2, diffuse_gain / new),
            )
    k.pack(e, o, [Plane(coef, 0), Plane(coef, 1)], [Plane(coef, tile - 2), Plane(coef, tile - 1)])


def models_kernel(scale, part, rest, pen, v, c, out):
    tile, ny, nz = v.shape
    k = Work(None, ny, nz)
    for n, ref in enumerate((v, c)):
        for i in range(tile):
            for r in k.blocks():
                at = slice(r, r + k.n)
                out[n, i, at] = renew(scale, ref[i, at], part[n, i, at], rest[n, i, at], pen[i, at])


def before_kernel(
    w, coef, two, wtwo, three, uthree, winner, wthree, base, halo, beyond, last, pe, po,
    four, five, ring, lap, side, wide, prev,
):
    tile, ny, nz = coef.shape
    k = Work(w, ny, nz)
    edge = (0, tile - 1)
    for n in range(2):
        for r in k.blocks():
            at = slice(r, r + k.n)
            two_far = k.unpack(pe, po, 3 * n, r)
            three_far = k.unpack(pe, po, 3 * n + 1, r)
            three_end = k.unpack(pe, po, 3 * n + 2, r)
            for s in range(2):
                third = base[s, n, at] + halo[s, 0, at] * two_far[s]
                side[n, s, at] = third
                wide[(2, tile + 3)[s], at] = third
                wide[(1, tile + 4)[s], at] = three_far[s]
                wide[(0, tile + 5)[s], at] = three_end[s]
                prev[s, at] = two_far[s]

        def third_plane(i):
            if i in edge:
                return Plane(wthree if n else uthree, edge.index(i))
            return Plane(winner, i - 1) if n else Plane(three, i)

        for i in range(tile):
            for r in k.blocks():
                k.put(Plane(wide, i + 3), r, k.get(third_plane(i), r))

        def second(i):
            return Plane(wtwo, edge.index(i)) if n and i in edge else Plane(two, n, i)

        for i in range(tile):
            k.step(
                Plane(four, n, i), Plane(wide, i + 3), second(i), Plane(coef, i),
                Plane(wide, i + 2), Plane(wide, i + 4),
            )
        for s in range(2):
            for m, j in enumerate(((-2, -1), (tile + 1, tile))[s]):
                known = Plane(last, s) if n else Plane(beyond, s, 0)
                earlier = known if m else Plane(prev, s)
                for r in k.blocks():
                    value, total = k.lap(Plane(wide, j + 3), Plane(wide, j + 2), Plane(wide, j + 4), r)
                    k.put(Plane(ring, n, s, m), r, k.ahead(value, k.get(earlier, r)))
                    k.put(Plane(lap, n, s, m), r, total)
        for i in range(1, tile - 1):
            k.step(
                Plane(five, n, i - 1), Plane(four, n, i), third_plane(i), Plane(coef, i),
                Plane(four, n, i - 1), Plane(four, n, i + 1),
            )


def after_kernel(w, coef, four, five, ring, lap, side, uthree, wthree, e, o, out, cn, far, ends):
    tile, ny, nz = coef.shape
    k = Work(w, ny, nz)
    edge = (0, tile - 1)
    for r in k.blocks():
        parts = [k.unpack(e, o, m, r) for m in range(2)]
        for s in range(2):
            order = (0, 1) if s == 0 else (1, 0)
            for m in range(2):
                k.put(Plane(cn, s, m), r, parts[order[m]][s])
    for n in range(2):
        for s in range(2):
            for m in range(2):
                for r in k.blocks():
                    at = slice(r, r + k.n)
                    far[s, m, at] = ring[n, s, m, at] + cn[s, m, at] * lap[n, s, m, at]
        for s, i in enumerate(edge):
            k.step(
                Plane(ends, s, 0), Plane(far, s, 1), Plane(side, n, s), Plane(cn, s, 1),
                Plane(far, s, 0), Plane(four, n, i),
            )
            k.step(
                Plane(ends, s, 1), Plane(four, n, i), Plane(wthree if n else uthree, s),
                Plane(coef, i),
                *near(lambda j: Plane(four, n, j), i, tile, (Plane(far, 0, 1), Plane(far, 1, 1))),
            )

        def fifth(i):
            return Plane(ends, edge.index(i), 1) if i in edge else Plane(five, n, i - 1)

        for i in range(tile):
            k.step(
                Plane(out, 0, n, i), fifth(i), Plane(four, n, i), Plane(coef, i),
                *near(fifth, i, tile, (Plane(ends, 0, 0), Plane(ends, 1, 0))),
            )


def swap_pairs(even_block, odd_block):
    count = lax.axis_size("space")
    evens = [(i, i ^ 1) for i in range(count) if i ^ 1 < count]
    odds = [(i, ((i + 1) ^ 1) - 1) for i in range(count) if 0 <= ((i + 1) ^ 1) - 1 < count]
    return lax.ppermute(even_block, "space", evens), lax.ppermute(odd_block, "space", odds)


def across(block, mask):
    count = lax.axis_size("src")
    return lax.ppermute(block, "src", [(i, i ^ mask) for i in range(count)])


def block_step(fields, velocity, conductivity, labels):
    tile, ny, nz = velocity.shape
    groups = lax.axis_size("src")
    assert tile >= 4 and labels.shape[0] == 1 and groups >= 4 and groups & (groups - 1) == 0
    scale = 1.0 / (20.0 * math.sqrt(groups))

    def planes(*lead):
        return (*lead, ny, nz)

    ae, ao, be, bo, ce, co, coef, one, acc, w, fields, velocity, conductivity = call(
        isolated_kernel,
        [planes(4)] * 2 + [planes(2)] * 4 + [planes(tile), planes(2, tile), planes(tile)]
        + [(8, nz), fields.shape, velocity.shape, conductivity.shape],
        (labels, fields, velocity, conductivity),
        [planes(2, 2)],
        [pl.BlockSpec(memory_space=pltpu.HBM)] * 4,
        [pltpu.SMEM((1,), jnp.int32), pltpu.SemaphoreType.DMA((4,))],
    )
    ae, ao = swap_pairs(ae, ao)
    be, bo = swap_pairs(be, bo)
    ce, co = swap_pairs(ce, co)

    acc1, rim, ends, two, three, halo = call(
        inner_kernel,
        [((tile - 2) * ny + 8, nz), planes(2), planes(2, 2), planes(2, tile), planes(tile), planes(2, 2)],
        (w, fields, coef, one, acc, ae, ao),
        [planes(2)],
    )
    masks = [1 << k for k in reversed(range(groups.bit_length() - 1))]
    far1 = across(acc1, masks[0])
    acc2, wtwo, uthree, beyond = call(
        outer_kernel,
        [(2 * ny, nz), planes(2), planes(2), planes(2, 2)],
        (w, fields, coef, one, ends, two, halo, rim, be, bo),
        [planes(2)],
    )
    far2 = across(acc2, masks[0])
    pe, po, winner = call(
        early_kernel,
        [planes(6), planes(6), planes(tile - 2)],
        (w, coef, one, ends, two, wtwo, three, uthree),
    )
    pe, po = swap_pairs(pe, po)
    (other,) = call(pick_kernel, [planes(2)], (ce, co))
    other = across(other, 1)

    (part,) = call(weigh_kernel, [planes(2, tile)], (acc1, acc2, far1, far2))
    for mask in masks[1:-1]:
        part = part + across(part, mask)
    rest = across(part, masks[-1])
    pen, wthree, base, last = call(
        late_kernel,
        [planes(tile), planes(2), planes(2, 2), planes(2)],
        (w, velocity, conductivity, fields, coef, ends, two, wtwo, halo, beyond, ce, co, other),
        [planes(tile + 2), planes(2), planes(2)],
    )
    coef_next, e, o = call(
        lambda *refs: renew_kernel(scale, *refs),
        [planes(tile), planes(2), planes(2)],
        (w, part, rest, pen, velocity, conductivity),
    )
    e, o = swap_pairs(e, o)
    (models,) = call(
        lambda *refs: models_kernel(scale, *refs),
        [planes(2, tile)], (part, rest, pen, velocity, conductivity),
    )
    four, five, ring, lap, side = call(
        before_kernel,
        [planes(2, tile), planes(2, tile - 2), planes(2, 2, 2), planes(2, 2, 2), planes(2, 2)],
        (w, coef_next, two, wtwo, three, uthree, winner, wthree, base, halo, beyond, last, pe, po),
        [planes(tile + 6), planes(2)],
    )
    (final,) = call(
        after_kernel,
        [planes(1, 2, tile)],
        (w, coef_next, four, five, ring, lap, side, uthree, wthree, e, o),
        [planes(2, 2), planes(2, 2), planes(2, 2)],
    )
    return final, models


def solution(mesh):
    in_specs = (
        P(("parts", "src"), None, "space", None, None),
        P(("parts", "space"), None, None),
        P(("parts", "space"), None, None),
        P(("parts", "src")),
    )
    out_specs = (
        P(("parts", "src"), None, "space", None, None),
        P(None, ("parts", "space"), None, None),
    )
    return jax.shard_map(
        block_step, mesh=mesh, in_specs=in_specs, out_specs=out_specs, check_vma=False
    )
```

time: 107 us -> 47.5 us (0.44)
  waiting for transfers between devices: 36.2 us -> 10.1 us
  between operations: 15.1 us -> 1.44 us
  starting transfers between devices: 35 us -> 25 us
  other arithmetic: 9.47 us -> 0 us
  Pallas kernels: 0 us -> 6.81 us
  blocking collectives: 6.59 us -> 0 us
    ppermute x14, waiting for transfers between devices: 24.9 us -> 10.1 us  [the longest x4 5.73 us: across(): return lax.ppermute(block, 'src', [(i, i ^ mask) for i in range(count)])]
    reduce_scatter x1 -> x0, waiting for transfers between devices: 11.3 us -> none  [shards(): lax.psum_scatter(partial_sum, 'src', scatter_dimension=2, tiled=True)]
    ppermute x14, starting transfers between devices: 34.9 us -> 25 us  [the longest x5 18.4 us: swap_pairs(): lax.ppermute(even_block, 'space', evens)]
    pallas_call x0 -> x11, Pallas kernels: none -> 6.81 us  [call(): pl.pallas_call(kernel, out_shape=tuple((jax.ShapeDtypeStruct(o, F32) for...]
    all_gather x1 -> x0, blocking collectives: 6.59 us -> none  [shards(): updated = lax.all_gather(fresh, 'src', axis=2, tiled=True)]
    another operation x28 -> x0, other arithmetic: 5.28 us -> none  [the longest x21 2.26 us: advance_thin(): padded = extended_2(jnp.stack([upper, lower], 1), (('space', 2),), 1)]
    slice x4 -> x0, local copies, waits for them, and re-layouts: 2.1 us -> none  [the longest x1 1.07 us: shards(): state = (fields[:, 0], fields[:, 1], fields[:, 2], fields[:, 3])]
    sub x6 -> x0, other arithmetic: 1.97 us -> none  [neighbours(): return total - 6.0 * middle]
  transfers between devices with their start and end apart: 15 -> 14, of which waited for: 11 -> 5; matrix products, arithmetic and copies ran while one was open for 5% -> 0% of each run, Pallas kernels for 0% -> 8%
where the time goes in v3:
time: 47.5 us; the launch traced here: 46.5 us
  starting transfers between devices  25 us (53%)
  waiting for transfers between devices  10.1 us (21%)
  Pallas kernels  6.81 us (14%)
  local copies, waits for them, and re-layouts  3.12 us (7%)
  between operations  1.44 us (3%)
    ppermute x5, starting transfers between devices, swap_pairs(): lax.ppermute(even_block, 'space', evens)  18.4 us
    pallas_call x11, Pallas kernels, call(): pl.pallas_call(kernel, out_shape=tuple((jax.ShapeDtypeStruct(o, F32) for...  6.81 us
    ppermute x4, waiting for transfers between devices, across(): return lax.ppermute(block, 'src', [(i, i ^ mask) for i in range(count)])  5.73 us
    ppermute x5, waiting for transfers between devices, swap_pairs(): lax.ppermute(even_block, 'space', evens)  4.39 us
    ppermute x4, starting transfers between devices, across(): return lax.ppermute(block, 'src', [(i, i ^ mask) for i in range(count)])  3.32 us
    ppermute x5, starting transfers between devices, swap_pairs(): lax.ppermute(odd_block, 'space', odds)  3.31 us
    unnamed x6, local copies, waits for them, and re-layouts  3.12 us
  transfers between devices with their start and end apart: 14, of which 5 were waited for; matrix products, arithmetic and copies ran while one was open for 0% of the time, Pallas kernels for 8%

profile of v3, /device:TPU:0, one launch (start us, length us, event | category | flops | bytes accessed | tf_op | source)
XLA Modules:
  0.0 46.5 jit_solution(17359977818399178769)
XLA Ops:
  1.3 0.0 copy-start
  1.3 1.2 %copy-done = f32[1,4,4,128,128]{4,3,2,1,0:T(8,128)S(1)} copy-done((f32[1,4,4,128,128]{4,3,2,1,0:T(8,128)S(1)}, f32[1,4,4,128,128]{4,3,2,1,0:T(8,128)}, u32[]{:S(2)}) %copy-start) | copy-done | bytes 1048600
  2.5 0.0 copy-start.1
  2.5 0.9 %copy-done.1 = f32[4,128,128]{2,1,0:T(8,128)S(1)} copy-done((f32[4,128,128]{2,1,0:T(8,128)S(1)}, f32[4,128,128]{2,1,0:T(8,128)}, u32[]{:S(2)}) %copy-start.1) | copy-done | bytes 262168
  3.5 0.0 copy-start.2
  3.5 0.9 %copy-done.2 = f32[4,128,128]{2,1,0:T(8,128)S(1)} copy-done((f32[4,128,128]{2,1,0:T(8,128)S(1)}, f32[4,128,128]{2,1,0:T(8,128)}, u32[]{:S(2)}) %copy-start.2) | copy-done | bytes 262168
  4.4 1.2 %shard_map.59 = (f32[4,128,128]{2,1,0:T(8,128)S(1)}, f32[4,128,128]{2,1,0:T(8,128)S(1)}, f32[2,128,128]{2,1,0:T(8,128)S(1)}, f32[2,128,128]{2,1,0:T(8,128)S(1)},...) custom-call(s32[1]{0:T(128)S(6)} %copy.6.labels, ...), custom_call_target="tpu_custom_call" | custom-call | flops 26234900 | bytes 5246980 | tf_op jit(solution)/shard_map/pallas_call | solution.py:22
  5.6 3.1 %collective-permute-start = (f32[4,128,128]{2,1,0:T(8,128)S(1)}, f32[4,128,128]{2,1,0:T(8,128)S(1)}, u32[]{:S(2)}, u32[]{:S(2)}) collective-permute-start(f32[4,128,128]{2,1,0:T(8,128)S(1)} %get-tuple-element.45), channel_id=1, source_target_pairs={{0,1},{1,0},{2,3},{3,2},{4,5},{5,4},{6,7},{7,6},{8,9},{9,8},{10,11... | collective-permute-start | bytes 786440 | tf_op jit(solution)/shard_map/ppermute | solution.py:510
  8.8 0.7 %collective-permute-start.1 = (f32[4,128,128]{2,1,0:T(8,128)S(1)}, f32[4,128,128]{2,1,0:T(8,128)S(1)}, u32[]{:S(2)}, u32[]{:S(2)}) collective-permute-start(f32[4,128,128]{2,1,0:T(8,128)S(1)} %get-tuple-element.46), channel_id=1, source_target_pairs={{1,2},{2,1},{5,6},{6,5},{9,10},{10,9},{13,14},{14,13},{17,18},{18,... | collective-permute-start | bytes 786440 | tf_op jit(solution)/shard_map/ppermute | solution.py:510
  9.4 4.4 %collective-permute-start.2 = (f32[2,128,128]{2,1,0:T(8,128)S(1)}, f32[2,128,128]{2,1,0:T(8,128)S(1)}, u32[]{:S(2)}, u32[]{:S(2)}) collective-permute-start(f32[2,128,128]{2,1,0:T(8,128)S(1)} %get-tuple-element.52), channel_id=1, source_target_pairs={{0,1},{1,0},{2,3},{3,2},{4,5},{5,4},{6,7},{7,6},{8,9},{9,8},{10,11... | collective-permute-start | bytes 393224 | tf_op jit(solution)/shard_map/ppermute | solution.py:510
  13.9 0.7 %collective-permute-start.3 = (f32[2,128,128]{2,1,0:T(8,128)S(1)}, f32[2,128,128]{2,1,0:T(8,128)S(1)}, u32[]{:S(2)}, u32[]{:S(2)}) collective-permute-start(f32[2,128,128]{2,1,0:T(8,128)S(1)} %get-tuple-element.53), channel_id=1, source_target_pairs={{1,2},{2,1},{5,6},{6,5},{9,10},{10,9},{13,14},{14,13},{17,18},{18,... | collective-permute-start | bytes 393224 | tf_op jit(solution)/shard_map/ppermute | solution.py:510
  14.5 1.4 %collective-permute-done.ae = f32[4,128,128]{2,1,0:T(8,128)S(1)} collective-permute-done((f32[4,128,128]{2,1,0:T(8,128)S(1)}, f32[4,128,128]{2,1,0:T(8,128)S(1)}, u32[]{:S(2)}, u32[]{:S(2)}) %collective-permute-start) | collective-permute-done | bytes 262176 | tf_op jit(solution)/shard_map/ppermute | solution.py:510
  15.9 0.0 collective-permute-done.1.ao
  15.9 0.5 %shard_map.60 = (f32[264,128]{1,0:T(8,128)S(1)}, f32[2,128,128]{2,1,0:T(8,128)S(1)}, f32[2,2,128,128]{3,2,1,0:T(8,128)S(1)}, f32[2,4,128,128]{3,2,1,0:T(8,128)S(...) custom-call(f32[8,128]{1,0:T(8,128)S(1)} %get-tuple-element.40.w.refs_0_, ...), custom_call_target="tpu_custom_call" | custom-call | flops 21012480 | bytes 4202496 | tf_op jit(solution)/shard_map/pallas_call | solution.py:22
  16.4 2.0 %collective-permute-start.4 = (f32[264,128]{1,0:T(8,128)S(1)}, f32[264,128]{1,0:T(8,128)S(1)}, u32[]{:S(2)}, u32[]{:S(2)}) collective-permute-start(f32[264,128]{1,0:T(8,128)S(1)} %get-tuple-element.47.acc1), channel_id=1, source_target_pairs={{0,8},{4,12},{8,0},{12,4},{1,9},{5,13},{9,1},{13,5},{2,10},{6,14},... | collective-permute-start | bytes 405512 | tf_op jit(solution)/shard_map/ppermute | solution.py:515
  18.4 0.0 collective-permute-done.2.be
  18.4 0.0 collective-permute-done.3.bo
  18.4 0.3 shard_map.61
  18.7 1.2 %collective-permute-start.5 = (f32[256,128]{1,0:T(8,128)S(1)}, f32[256,128]{1,0:T(8,128)S(1)}, u32[]{:S(2)}, u32[]{:S(2)}) collective-permute-start(f32[256,128]{1,0:T(8,128)S(1)} %get-tuple-element.54.acc2), channel_id=1, source_target_pairs={{0,8},{4,12},{8,0},{12,4},{1,9},{5,13},{9,1},{13,5},{2,10},{6,14},... | collective-permute-start | bytes 393224 | tf_op jit(solution)/shard_map/ppermute | solution.py:515
  19.9 4.4 %collective-permute-done.5.far2 = f32[256,128]{1,0:T(8,128)S(1)} collective-permute-done((f32[256,128]{1,0:T(8,128)S(1)}, f32[256,128]{1,0:T(8,128)S(1)}, u32[]{:S(2)}, u32[]{:S(2)}) %collective-permute-start.5) | collective-permute-done | bytes 131104 | tf_op jit(solution)/shard_map/ppermute | solution.py:515
  24.3 0.0 collective-permute-done.4.far1
  24.3 0.1 shard_map.62.refs_1_.refs_0_
  24.4 0.1 collective-permute-start.6
  24.4 4.6 %collective-permute-start.7 = (f32[2,128,128]{2,1,0:T(8,128)S(1)}, f32[2,128,128]{2,1,0:T(8,128)S(1)}, u32[]{:S(2)}, u32[]{:S(2)}) collective-permute-start(f32[2,128,128]{2,1,0:T(8,128)S(1)} %get-tuple-element.59), channel_id=1, source_target_pairs={{0,1},{1,0},{2,3},{3,2},{4,5},{5,4},{6,7},{7,6},{8,9},{9,8},{10,11... | collective-permute-start | bytes 393224 | tf_op jit(solution)/shard_map/ppermute | solution.py:510
  29.0 0.7 %collective-permute-start.8 = (f32[2,128,128]{2,1,0:T(8,128)S(1)}, f32[2,128,128]{2,1,0:T(8,128)S(1)}, u32[]{:S(2)}, u32[]{:S(2)}) collective-permute-start(f32[2,128,128]{2,1,0:T(8,128)S(1)} %get-tuple-element.60), channel_id=1, source_target_pairs={{1,2},{2,1},{5,6},{6,5},{9,10},{10,9},{13,14},{14,13},{17,18},{18,... | collective-permute-start | bytes 393224 | tf_op jit(solution)/shard_map/ppermute | solution.py:510
  29.7 0.2 shard_map.66
  29.9 2.9 %collective-permute-start.10 = (f32[6,128,128]{2,1,0:T(8,128)S(1)}, f32[6,128,128]{2,1,0:T(8,128)S(1)}, u32[]{:S(2)}, u32[]{:S(2)}) collective-permute-start(f32[6,128,128]{2,1,0:T(8,128)S(1)} %get-tuple-element.69), channel_id=1, source_target_pairs={{0,1},{1,0},{2,3},{3,2},{4,5},{5,4},{6,7},{7,6},{8,9},{9,8},{10,11... | collective-permute-start | bytes 1179656 | tf_op jit(solution)/shard_map/ppermute | solution.py:510
  32.7 0.7 %collective-permute-start.11 = (f32[6,128,128]{2,1,0:T(8,128)S(1)}, f32[6,128,128]{2,1,0:T(8,128)S(1)}, u32[]{:S(2)}, u32[]{:S(2)}) collective-permute-start(f32[6,128,128]{2,1,0:T(8,128)S(1)} %get-tuple-element.70), channel_id=1, source_target_pairs={{1,2},{2,1},{5,6},{6,5},{9,10},{10,9},{13,14},{14,13},{17,18},{18,... | collective-permute-start | bytes 1179656 | tf_op jit(solution)/shard_map/ppermute | solution.py:510
  33.4 0.0 collective-permute-done.7.ce
  33.4 0.0 collective-permute-done.8.co
  33.5 0.1 collective-permute-start.9
  33.5 1.3 %collective-permute-done.9.other = f32[2,128,128]{2,1,0:T(8,128)S(1)} collective-permute-done((f32[2,128,128]{2,1,0:T(8,128)S(1)}, f32[2,128,128]{2,1,0:T(8,128)S(1)}, u32[]{:S(2)}, u32[]{:S(2)}) %collective-permute-start.9) | collective-permute-done | bytes 131104 | tf_op jit(solution)/shard_map/ppermute | solution.py:515
  34.9 0.8 %shard_map.64 = (f32[4,128,128]{2,1,0:T(8,128)S(1)}, f32[2,128,128]{2,1,0:T(8,128)S(1)}, f32[2,2,128,128]{3,2,1,0:T(8,128)S(1)}, f32[2,128,128]{2,1,0:T(8,128)S(1)}) custom-call(f32[8,128]{1,0:T(8,128)S(1)} %get-tuple-element.40.w.refs_0_, f32[4,128,128]{2,1,0:T(8,128)S(1)} %get-tuple-element.55.v.refs_4_.refs_3_, ...), custom_call_target="tpu_custom_call" | custom-call | flops 22302720 | bytes 4460544 | tf_op jit(solution)/shard_map/pallas_call | solution.py:22
  35.7 0.0 collective-permute-done.6.refs_2_.refs_1_
  35.7 0.2 shard_map.65
  35.9 3.4 %collective-permute-start.12 = (f32[2,128,128]{2,1,0:T(8,128)S(1)}, f32[2,128,128]{2,1,0:T(8,128)S(1)}, u32[]{:S(2)}, u32[]{:S(2)}) collective-permute-start(f32[2,128,128]{2,1,0:T(8,128)S(1)} %get-tuple-element.76), channel_id=1, source_target_pairs={{0,1},{1,0},{2,3},{3,2},{4,5},{5,4},{6,7},{7,6},{8,9},{9,8},{10,11... | collective-permute-start | bytes 393224 | tf_op jit(solution)/shard_map/ppermute | solution.py:510
  39.2 0.7 %collective-permute-start.13 = (f32[2,128,128]{2,1,0:T(8,128)S(1)}, f32[2,128,128]{2,1,0:T(8,128)S(1)}, u32[]{:S(2)}, u32[]{:S(2)}) collective-permute-start(f32[2,128,128]{2,1,0:T(8,128)S(1)} %get-tuple-element.77), channel_id=1, source_target_pairs={{1,2},{2,1},{5,6},{6,5},{9,10},{10,9},{13,14},{14,13},{17,18},{18,... | collective-permute-start | bytes 393224 | tf_op jit(solution)/shard_map/ppermute | solution.py:510
  39.9 0.9 %shard_map.69 = f32[2,4,128,128]{3,2,1,0:T(8,128)} custom-call(f32[2,4,128,128]{3,2,1,0:T(8,128)S(1)} %shard_map.62.refs_1_.refs_0_, f32[2,4,128,128]{3,2,1,0:T(8,128)S(1)} %collective-permute-done.6.refs_2_.refs_1_, f32[4,128,128]{2,1,0:T(8,128)S(1)} %get-tuple-element.61.refs_3_.refs_2_, f32[4,128,128]{2,1,0:T(8,128)S(1)} %get-tuple-element.55.v.refs_4_.refs_3_, ...), custom_call_target="tpu_custom_call" | custom-call | flops 11796480 | bytes 2359296 | tf_op jit(solution)/shard_map/pallas_call | solution.py:22
  40.8 1.9 %collective-permute-done.10.pe = f32[6,128,128]{2,1,0:T(8,128)S(1)} collective-permute-done((f32[6,128,128]{2,1,0:T(8,128)S(1)}, f32[6,128,128]{2,1,0:T(8,128)S(1)}, u32[]{:S(2)}, u32[]{:S(2)}) %collective-permute-start.10) | collective-permute-done | bytes 393248 | tf_op jit(solution)/shard_map/ppermute | solution.py:510
  42.7 0.0 collective-permute-done.11.po
  42.7 1.1 %shard_map.67 = (f32[2,4,128,128]{3,2,1,0:T(8,128)S(1)}, f32[2,2,128,128]{3,2,1,0:T(8,128)S(1)}, f32[2,2,2,128,128]{4,3,2,1,0:T(8,128)S(1)}, f32[2,2,2,128,128]{4,3,2,1,0:T(8,128)S(1)}, f32[2,2,128,128]{3,2,1,0:T(8,128)S(1)}) custom-call(f32[8,128]{1,0:T(8,128)S(1)} %get-tuple-element.40.w.refs_0_, f32[4,128,128]{2,1,0:T(8,128)S(1)} %get-tuple-element.62.coef, ...), custom_call_target="tpu_custom_call" | custom-call | flops 26890240 | bytes 5378048 | tf_op jit(solution)/shard_map/pallas_call | solution.py:22
  43.8 1.2 %collective-permute-done.12.e = f32[2,128,128]{2,1,0:T(8,128)S(1)} collective-permute-done((f32[2,128,128]{2,1,0:T(8,128)S(1)}, f32[2,128,128]{2,1,0:T(8,128)S(1)}, u32[]{:S(2)}, u32[]{:S(2)}) %collective-permute-start.12) | collective-permute-done | bytes 131104 | tf_op jit(solution)/shard_map/ppermute | solution.py:510
  45.0 0.0 collective-permute-done.13.o
  45.0 1.6 %shard_map.68 = f32[1,2,4,128,128]{4,3,2,1,0:T(8,128)} custom-call(f32[8,128]{1,0:T(8,128)S(1)} %get-tuple-element.40.w.refs_0_, f32[4,128,128]{2,1,0:T(8,128)S(1)} %get-tuple-element.62.coef, f32[2,4,128,128]{3,2,1,0:T(8,128)S(1)} %get-tuple-element.71.four, f32[2,2,128,128]{3,2,1,0:T(8,128)S(1)} %get-tuple-element.72.five, ...), custom_call_target="tpu_custom_call" | custom-call | flops 17059840 | bytes 3411968 | tf_op jit(solution)/shard_map/pallas_call | solution.py:22
  (1 shorter events, 0.0 us)
Async XLA Ops:
  1.3 1.2 %copy-start = (f32[1,4,4,128,128]{4,3,2,1,0:T(8,128)S(1)}, f32[1,4,4,128,128]{4,3,2,1,0:T(8,128)}, u32[]{:S(2)}) copy-start(f32[1,4,4,128,128]{4,3,2,1,0:T(8,128)} %f_in.1) | copy-start | bytes 3145732
  2.5 0.9 %copy-start.1 = (f32[4,128,128]{2,1,0:T(8,128)S(1)}, f32[4,128,128]{2,1,0:T(8,128)}, u32[]{:S(2)}) copy-start(f32[4,128,128]{2,1,0:T(8,128)} %v_in.1) | copy-start | bytes 786436
  3.5 0.9 %copy-start.2 = (f32[4,128,128]{2,1,0:T(8,128)S(1)}, f32[4,128,128]{2,1,0:T(8,128)}, u32[]{:S(2)}) copy-start(f32[4,128,128]{2,1,0:T(8,128)} %c_in.1) | copy-start | bytes 786436
  5.6 10.3 %collective-permute-start = (f32[4,128,128]{2,1,0:T(8,128)S(1)}, f32[4,128,128]{2,1,0:T(8,128)S(1)}, u32[]{:S(2)}, u32[]{:S(2)}) collective-permute-start(f32[4,128,128]{2,1,0:T(8,128)S(1)} %get-tuple-element.45), channel_id=1, source_target_pairs={{0,1},{1,0},{2,3},{3,2},{4,5},{5,4},{6,7},{7,6},{8,9},{9,8},{10,11... | collective-permute-start | bytes 786440 | tf_op jit(solution)/shard_map/ppermute | solution.py:510
  8.8 7.2 %collective-permute-start.1 = (f32[4,128,128]{2,1,0:T(8,128)S(1)}, f32[4,128,128]{2,1,0:T(8,128)S(1)}, u32[]{:S(2)}, u32[]{:S(2)}) collective-permute-start(f32[4,128,128]{2,1,0:T(8,128)S(1)} %get-tuple-element.46), channel_id=1, source_target_pairs={{1,2},{2,1},{5,6},{6,5},{9,10},{10,9},{13,14},{14,13},{17,18},{18,... | collective-permute-start | bytes 786440 | tf_op jit(solution)/shard_map/ppermute | solution.py:510
  9.4 9.0 %collective-permute-start.2 = (f32[2,128,128]{2,1,0:T(8,128)S(1)}, f32[2,128,128]{2,1,0:T(8,128)S(1)}, u32[]{:S(2)}, u32[]{:S(2)}) collective-permute-start(f32[2,128,128]{2,1,0:T(8,128)S(1)} %get-tuple-element.52), channel_id=1, source_target_pairs={{0,1},{1,0},{2,3},{3,2},{4,5},{5,4},{6,7},{7,6},{8,9},{9,8},{10,11... | collective-permute-start | bytes 393224 | tf_op jit(solution)/shard_map/ppermute | solution.py:510
  13.9 4.5 %collective-permute-start.3 = (f32[2,128,128]{2,1,0:T(8,128)S(1)}, f32[2,128,128]{2,1,0:T(8,128)S(1)}, u32[]{:S(2)}, u32[]{:S(2)}) collective-permute-start(f32[2,128,128]{2,1,0:T(8,128)S(1)} %get-tuple-element.53), channel_id=1, source_target_pairs={{1,2},{2,1},{5,6},{6,5},{9,10},{10,9},{13,14},{14,13},{17,18},{18,... | collective-permute-start | bytes 393224 | tf_op jit(solution)/shard_map/ppermute | solution.py:510
  16.4 7.9 %collective-permute-start.4 = (f32[264,128]{1,0:T(8,128)S(1)}, f32[264,128]{1,0:T(8,128)S(1)}, u32[]{:S(2)}, u32[]{:S(2)}) collective-permute-start(f32[264,128]{1,0:T(8,128)S(1)} %get-tuple-element.47.acc1), channel_id=1, source_target_pairs={{0,8},{4,12},{8,0},{12,4},{1,9},{5,13},{9,1},{13,5},{2,10},{6,14},... | collective-permute-start | bytes 405512 | tf_op jit(solution)/shard_map/ppermute | solution.py:515
  18.7 5.6 %collective-permute-start.5 = (f32[256,128]{1,0:T(8,128)S(1)}, f32[256,128]{1,0:T(8,128)S(1)}, u32[]{:S(2)}, u32[]{:S(2)}) collective-permute-start(f32[256,128]{1,0:T(8,128)S(1)} %get-tuple-element.54.acc2), channel_id=1, source_target_pairs={{0,8},{4,12},{8,0},{12,4},{1,9},{5,13},{9,1},{13,5},{2,10},{6,14},... | collective-permute-start | bytes 393224 | tf_op jit(solution)/shard_map/ppermute | solution.py:515
  24.4 11.3 %collective-permute-start.6 = (f32[2,4,128,128]{3,2,1,0:T(8,128)S(1)}, f32[2,4,128,128]{3,2,1,0:T(8,128)S(1)}, u32[]{:S(2)}, u32[]{:S(2)}) collective-permute-start(f32[2,4,128,128]{3,2,1,0:T(8,128)S(1)} %shard_map.62.refs_1_.refs_0_), channel_id=1, source_target_pairs={{0,4},{4,0},{8,12},{12,8},{1,5},{5,1},{9,13},{13,9},{2,6},{6,2},{1... | collective-permute-start | bytes 1572872 | tf_op jit(solution)/shard_map/ppermute | solution.py:515
  24.4 9.0 %collective-permute-start.7 = (f32[2,128,128]{2,1,0:T(8,128)S(1)}, f32[2,128,128]{2,1,0:T(8,128)S(1)}, u32[]{:S(2)}, u32[]{:S(2)}) collective-permute-start(f32[2,128,128]{2,1,0:T(8,128)S(1)} %get-tuple-element.59), channel_id=1, source_target_pairs={{0,1},{1,0},{2,3},{3,2},{4,5},{5,4},{6,7},{7,6},{8,9},{9,8},{10,11... | collective-permute-start | bytes 393224 | tf_op jit(solution)/shard_map/ppermute | solution.py:510
  29.0 4.4 %collective-permute-start.8 = (f32[2,128,128]{2,1,0:T(8,128)S(1)}, f32[2,128,128]{2,1,0:T(8,128)S(1)}, u32[]{:S(2)}, u32[]{:S(2)}) collective-permute-start(f32[2,128,128]{2,1,0:T(8,128)S(1)} %get-tuple-element.60), channel_id=1, source_target_pairs={{1,2},{2,1},{5,6},{6,5},{9,10},{10,9},{13,14},{14,13},{17,18},{18,... | collective-permute-start | bytes 393224 | tf_op jit(solution)/shard_map/ppermute | solution.py:510
  29.9 12.8 %collective-permute-start.10 = (f32[6,128,128]{2,1,0:T(8,128)S(1)}, f32[6,128,128]{2,1,0:T(8,128)S(1)}, u32[]{:S(2)}, u32[]{:S(2)}) collective-permute-start(f32[6,128,128]{2,1,0:T(8,128)S(1)} %get-tuple-element.69), channel_id=1, source_target_pairs={{0,1},{1,0},{2,3},{3,2},{4,5},{5,4},{6,7},{7,6},{8,9},{9,8},{10,11... | collective-permute-start | bytes 1179656 | tf_op jit(solution)/shard_map/ppermute | solution.py:510
  32.7 10.0 %collective-permute-start.11 = (f32[6,128,128]{2,1,0:T(8,128)S(1)}, f32[6,128,128]{2,1,0:T(8,128)S(1)}, u32[]{:S(2)}, u32[]{:S(2)}) collective-permute-start(f32[6,128,128]{2,1,0:T(8,128)S(1)} %get-tuple-element.70), channel_id=1, source_target_pairs={{1,2},{2,1},{5,6},{6,5},{9,10},{10,9},{13,14},{14,13},{17,18},{18,... | collective-permute-start | bytes 1179656 | tf_op jit(solution)/shard_map/ppermute | solution.py:510
  33.5 1.4 %collective-permute-start.9 = (f32[2,128,128]{2,1,0:T(8,128)S(1)}, f32[2,128,128]{2,1,0:T(8,128)S(1)}, u32[]{:S(2)}, u32[]{:S(2)}) collective-permute-start(f32[2,128,128]{2,1,0:T(8,128)S(1)} %shard_map.63), channel_id=1, source_target_pairs={{0,4},{4,0},{8,12},{12,8},{1,5},{5,1},{9,13},{13,9},{2,6},{6,2},{1... | collective-permute-start | bytes 393224 | tf_op jit(solution)/shard_map/ppermute | solution.py:515
  35.9 9.1 %collective-permute-start.12 = (f32[2,128,128]{2,1,0:T(8,128)S(1)}, f32[2,128,128]{2,1,0:T(8,128)S(1)}, u32[]{:S(2)}, u32[]{:S(2)}) collective-permute-start(f32[2,128,128]{2,1,0:T(8,128)S(1)} %get-tuple-element.76), channel_id=1, source_target_pairs={{0,1},{1,0},{2,3},{3,2},{4,5},{5,4},{6,7},{7,6},{8,9},{9,8},{10,11... | collective-permute-start | bytes 393224 | tf_op jit(solution)/shard_map/ppermute | solution.py:510
  39.2 5.7 %collective-permute-start.13 = (f32[2,128,128]{2,1,0:T(8,128)S(1)}, f32[2,128,128]{2,1,0:T(8,128)S(1)}, u32[]{:S(2)}, u32[]{:S(2)}) collective-permute-start(f32[2,128,128]{2,1,0:T(8,128)S(1)} %get-tuple-element.77), channel_id=1, source_target_pairs={{1,2},{2,1},{5,6},{6,5},{9,10},{10,9},{13,14},{14,13},{17,18},{18,... | collective-permute-start | bytes 393224 | tf_op jit(solution)/shard_map/ppermute | solution.py:510

commit v4 on v3

--- a/solution.py
+++ b/solution.py
@@ -17,13 +17,13 @@
 F32 = jnp.float32
 
 
-def call(kernel, outs, args, scratch=(), specs=None, extra=()):
+def call(kernel, outs, args, scratch=(), specs=None, extra=(), out_spec=VMEM):
     size = sum(math.prod(o) for o in outs) + sum(a.size for a in args)
     return pl.pallas_call(
         kernel,
         out_shape=tuple(jax.ShapeDtypeStruct(o, F32) for o in outs),
         in_specs=specs or [VMEM for _ in args],
-        out_specs=tuple(VMEM for _ in outs),
+        out_specs=tuple(out_spec for _ in outs),
         scratch_shapes=[pltpu.VMEM(s, F32) for s in scratch] + list(extra),
         compiler_params=pltpu.CompilerParams(vmem_limit_bytes=16 << 20),
         cost_estimate=pl.CostEstimate(flops=20 * size, bytes_accessed=4 * size, transcendentals=0),
@@ -125,26 +125,25 @@
 
 
 def isolated_kernel(
-    labels, f_in, v_in, c_in,
-    ae, ao, be, bo, ce, co, coef, one, acc, w, f, v, c, two, label, sems,
+    label, f_in, v_in, c_in,
+    ae, ao, be, bo, coef, one, acc, w, f, v, c, two, sems,
 ):
     copies = [
         pltpu.make_async_copy(src, dst, sems.at[n])
-        for n, (src, dst) in enumerate(((labels, label), (v_in, v), (c_in, c), (f_in, f)))
+        for n, (src, dst) in enumerate(((v_in, v), (c_in, c), (f_in, f)))
     ]
     for copy in copies:
         copy.start()
     tile, ny, nz = v.shape
-    copies[0].wait()
     w[...] = jnp.full(w.shape, label[0].astype(F32), F32)
     k = Work(w, ny, nz)
+    copies[0].wait()
     copies[1].wait()
-    copies[2].wait()
     edge = (0, tile - 1)
     for i in range(tile):
         for r in k.blocks():
             k.put(Plane(coef, i), r, k.coefficient(v[i, r:r + k.n], c[i, r:r + k.n]))
-    copies[3].wait()
+    copies[2].wait()
     for n in range(2):
         for i in range(tile):
 
@@ -155,23 +154,22 @@
                 Plane(one, n, i), Plane(f, 0, 2 * n, i), Plane(f, 0, 2 * n + 1, i), Plane(coef, i),
                 *near(lambda j: Plane(f, 0, 2 * n, j), i, tile), each if n == 0 else None,
             )
-        for s, i in enumerate(edge):
-            k.step(
-                Plane(two, n, s), Plane(one, n, i), Plane(f, 0, 2 * n, i), Plane(coef, i),
-                *near(lambda j: Plane(one, n, j), i, tile),
-            )
+    for s, i in enumerate(edge):
+        k.step(
+            Plane(two, s), Plane(one, 0, i), Plane(f, 0, 0, i), Plane(coef, i),
+            *near(lambda j: Plane(one, 0, j), i, tile),
+        )
     sides = [
         [Plane(coef, i), Plane(f, 0, 0, i), Plane(f, 0, 2, i), Plane(one, 0, i)] for i in edge
     ]
     k.pack(ae, ao, *sides)
-    k.pack(be, bo, *([Plane(two, 0, s), Plane(one, 1, i)] for s, i in enumerate(edge)))
+    k.pack(be, bo, *([Plane(two, s), Plane(one, 1, i)] for s, i in enumerate(edge)))
     for r in k.blocks():
         lo, hi = (
             jnp.where(k.first_core, v[i, r:r + k.n], c[i, r:r + k.n]) for i in edge
         )
-        k.put(Plane(ce, 0), r, jnp.where(k.even, hi, lo))
-        k.put(Plane(co, 0), r, jnp.where(k.even, lo, hi))
-    k.pack(ce.at[1:], co.at[1:], [Plane(two, 1, 0)], [Plane(two, 1, 1)])
+        k.put(Plane(be, 2), r, jnp.where(k.even, hi, lo))
+        k.put(Plane(bo, 2), r, jnp.where(k.even, lo, hi))
 
 
 def inner_kernel(w, f, coef, one, acc, ae, ao, acc1, rim, ends, two, three, halo, zero):
@@ -269,7 +267,17 @@
         )
 
 
-def early_kernel(w, coef, one, ends, two, wtwo, three, uthree, pe, po, wthree):
+def early_u_kernel(two, three, pe, po):
+    _, tile, ny, nz = two.shape
+    k = Work(None, ny, nz)
+
+    def planes(i, j):
+        return [Plane(two, 0, i), Plane(three, i), Plane(three, j), Plane(two, 1, i)]
+
+    k.pack(pe, po, planes(1, 2), planes(tile - 2, tile - 3))
+
+
+def early_w_kernel(w, coef, one, two, wtwo, pe, po, winner):
     tile, ny, nz = coef.shape
     k = Work(w, ny, nz)
     edge = (0, tile - 1)
@@ -279,37 +287,30 @@
 
     for i in range(1, tile - 1):
         k.step(
-            Plane(wthree, i - 1), second(i), Plane(one, 1, i), Plane(coef, i),
+            Plane(winner, i - 1), second(i), Plane(one, 1, i), Plane(coef, i),
             *near(second, i, tile),
         )
 
-    def planes(i, j):
-        return [
-            Plane(two, 0, i), Plane(three, i), Plane(three, j),
-            Plane(two, 1, i), Plane(wthree, i - 1), Plane(wthree, j - 1),
-        ]
-
-    k.pack(pe, po, planes(1, 2), planes(tile - 2, tile - 3))
-
-
-def pick_kernel(ce, co, out):
-    out[0], out[1] = ce[0], co[0]
-
-
-def late_kernel(
-    w, v, c, f, coef, ends, two, wtwo, halo, beyond, ce, co, other,
-    pen, wthree, base, last, logs, rims, d,
-):
-    tile, ny, nz = coef.shape
-    k = Work(w, ny, nz)
+    def planes(s, i, j):
+        return [Plane(wtwo, s), Plane(winner, i - 1), Plane(winner, j - 1)]
+
+    k.pack(pe, po, planes(0, 1, 2), planes(1, tile - 2, tile - 3))
+
+
+def pick_kernel(be, bo, out):
+    out[0], out[1] = be[2], bo[2]
+
+
+def penalty_kernel(v, c, be, bo, other, pen, logs, rims):
+    tile, ny, nz = v.shape
+    k = Work(None, ny, nz)
     edge = (0, tile - 1)
     for i in range(tile):
         for r in k.blocks():
             k.put(Plane(logs, i + 1), r, jnp.log(c[i, r:r + k.n]))
     for r in k.blocks():
-        mine = k.unpack(ce, co, 0, r)
+        mine = k.unpack(be, bo, 2, r)
         theirs = k.unpack(other.at[0:1], other.at[1:2], 0, r)
-        w2 = k.unpack(ce, co, 1, r)
         for s, i in enumerate(edge):
             vel = jnp.where(k.first_core, mine[s], theirs[s])
             con = jnp.where(k.first_core, theirs[s], mine[s])
@@ -319,33 +320,6 @@
                 Plane(logs, (0, tile + 1)[s]), r,
                 jnp.where(k.has[s], jnp.log(con), logs[i + 1, r:r + k.n]),
             )
-            k.put(Plane(d, s), r, halo[s, 0, r:r + k.n] * f[0, 2, i, r:r + k.n])
-            k.put(Plane(last, s), r, w2[s])
-    for s, i in enumerate(edge):
-        for r in k.blocks():
-            dv, total = k.flat(Plane(d, s), r)
-            total = total + ends[1, s, r:r + k.n]
-            k.put(
-                Plane(last, s), r,
-                last[s, r:r + k.n] + (1.0 + k.a) * dv + halo[s, 0, r:r + k.n] * total,
-            )
-
-    def second(i):
-        return Plane(wtwo, edge.index(i)) if i in edge else Plane(two, 1, i)
-
-    for s, i in enumerate(edge):
-        k.step(
-            Plane(wthree, s), second(i), Plane(ends, 1, s), Plane(coef, i),
-            *near(second, i, tile, (Plane(last, 0), Plane(last, 1))),
-        )
-        k.step(
-            Plane(base, s, 0), Plane(beyond, s, 0), Plane(halo, s, 1), Plane(halo, s, 0),
-            Plane(two, 0, i), None,
-        )
-        k.step(
-            Plane(base, s, 1), Plane(last, s), Plane(beyond, s, 1), Plane(halo, s, 0),
-            Plane(wtwo, s), None,
-        )
     for i in range(tile):
         below, above = near(lambda j: Plane(v, j), i, tile, (Plane(rims, 0), Plane(rims, 1)))
         for r in k.blocks():
@@ -414,25 +388,41 @@
 
 
 def before_kernel(
-    w, coef, two, wtwo, three, uthree, winner, wthree, base, halo, beyond, last, pe, po,
-    four, five, ring, lap, side, wide, prev,
+    w, coef, old, ends, two, wtwo, three, uthree, winner, halo, beyond, ue, uo, we, wo,
+    four, five, ring, lap, side, wthree, wide, prev, last,
 ):
     tile, ny, nz = coef.shape
     k = Work(w, ny, nz)
     edge = (0, tile - 1)
+    for r in k.blocks():
+        for s, value in enumerate(k.unpack(we, wo, 0, r)):
+            k.put(Plane(last, s), r, value)
     for n in range(2):
+        far = (((ue, uo, 0), (ue, uo, 1), (ue, uo, 2)), ((ue, uo, 3), (we, wo, 1), (we, wo, 2)))[n]
         for r in k.blocks():
             at = slice(r, r + k.n)
-            two_far = k.unpack(pe, po, 3 * n, r)
-            three_far = k.unpack(pe, po, 3 * n + 1, r)
-            three_end = k.unpack(pe, po, 3 * n + 2, r)
+            two_far, three_far, three_end = (k.unpack(*block, r) for block in far)
             for s in range(2):
-                third = base[s, n, at] + halo[s, 0, at] * two_far[s]
-                side[n, s, at] = third
-                wide[(2, tile + 3)[s], at] = third
                 wide[(1, tile + 4)[s], at] = three_far[s]
                 wide[(0, tile + 5)[s], at] = three_end[s]
                 prev[s, at] = two_far[s]
+
+        def second(i):
+            return Plane(wtwo, edge.index(i)) if n and i in edge else Plane(two, n, i)
+
+        for s, i in enumerate(edge):
+            known = Plane(last, s) if n else Plane(beyond, s, 0)
+            earlier = Plane(beyond, s, 1) if n else Plane(halo, s, 1)
+            k.step(
+                Plane(side, n, s), known, earlier, Plane(halo, s, 0), second(i), Plane(prev, s),
+            )
+            if n:
+                k.step(
+                    Plane(wthree, s), second(i), Plane(ends, 1, s), Plane(old, i),
+                    *near(second, i, tile, (Plane(last, 0), Plane(last, 1))),
+                )
+            for r in k.blocks():
+                k.put(Plane(wide, (2, tile + 3)[s]), r, side[n, s, r:r + k.n])
 
         def third_plane(i):
             if i in edge:
@@ -442,9 +432,6 @@
         for i in range(tile):
             for r in k.blocks():
                 k.put(Plane(wide, i + 3), r, k.get(third_plane(i), r))
-
-        def second(i):
-            return Plane(wtwo, edge.index(i)) if n and i in edge else Plane(two, n, i)
 
         for i in range(tile):
             k.step(
@@ -466,7 +453,10 @@
             )
 
 
-def after_kernel(w, coef, four, five, ring, lap, side, uthree, wthree, e, o, out, cn, far, ends):
+def after_kernel(
+    w, coef, four, five, ring, lap, side, uthree, wthree, e, o,
+    out, cn, far, ends, res, sems,
+):
     tile, ny, nz = coef.shape
     k = Work(w, ny, nz)
     edge = (0, tile - 1)
@@ -476,6 +466,7 @@
             order = (0, 1) if s == 0 else (1, 0)
             for m in range(2):
                 k.put(Plane(cn, s, m), r, parts[order[m]][s])
+    copies = []
     for n in range(2):
         for s in range(2):
             for m in range(2):
@@ -498,16 +489,22 @@
 
         for i in range(tile):
             k.step(
-                Plane(out, 0, n, i), fifth(i), Plane(four, n, i), Plane(coef, i),
+                Plane(res, n, i), fifth(i), Plane(four, n, i), Plane(coef, i),
                 *near(fifth, i, tile, (Plane(ends, 0, 0), Plane(ends, 1, 0))),
             )
+            copies.append(pltpu.make_async_copy(res.at[n, i], out.at[0, n, i], sems.at[n, i]))
+            copies[-1].start()
+    for copy in copies:
+        copy.wait()
 
 
 def swap_pairs(even_block, odd_block):
     count = lax.axis_size("space")
     evens = [(i, i ^ 1) for i in range(count) if i ^ 1 < count]
     odds = [(i, ((i + 1) ^ 1) - 1) for i in range(count) if 0 <= ((i + 1) ^ 1) - 1 < count]
-    return lax.ppermute(even_block, "space", evens), lax.ppermute(odd_block, "space", odds)
+    odd_block = lax.ppermute(odd_block, "space", odds)
+    even_block = lax.ppermute(even_block, "space", evens)
+    return even_block, odd_block
 
 
 def across(block, mask):
@@ -524,18 +521,20 @@
     def planes(*lead):
         return (*lead, ny, nz)
 
-    ae, ao, be, bo, ce, co, coef, one, acc, w, fields, velocity, conductivity = call(
+    ae, ao, be, bo, coef, one, acc, w, fields, velocity, conductivity = call(
         isolated_kernel,
-        [planes(4)] * 2 + [planes(2)] * 4 + [planes(tile), planes(2, tile), planes(tile)]
+        [planes(4)] * 2 + [planes(3)] * 2 + [planes(tile), planes(2, tile), planes(tile)]
         + [(8, nz), fields.shape, velocity.shape, conductivity.shape],
-        (labels, fields, velocity, conductivity),
-        [planes(2, 2)],
-        [pl.BlockSpec(memory_space=pltpu.HBM)] * 4,
-        [pltpu.SMEM((1,), jnp.int32), pltpu.SemaphoreType.DMA((4,))],
+        (
+            labels,
+            *(pltpu.with_memory_space_constraint(x, pltpu.HBM) for x in (fields, velocity, conductivity)),
+        ),
+        [planes(2)],
+        [pl.BlockSpec(memory_space=pltpu.SMEM)] + [pl.BlockSpec(memory_space=pltpu.HBM)] * 3,
+        [pltpu.SemaphoreType.DMA((3,))],
     )
     ae, ao = swap_pairs(ae, ao)
     be, bo = swap_pairs(be, bo)
-    ce, co = swap_pairs(ce, co)
 
     acc1, rim, ends, two, three, halo = call(
         inner_kernel,
@@ -545,6 +544,8 @@
     )
     masks = [1 << k for k in reversed(range(groups.bit_length() - 1))]
     far1 = across(acc1, masks[0])
+    ue, uo = call(early_u_kernel, [planes(4)] * 2, (two, three))
+    ue, uo = swap_pairs(ue, uo)
     acc2, wtwo, uthree, beyond = call(
         outer_kernel,
         [(2 * ny, nz), planes(2), planes(2), planes(2, 2)],
@@ -552,24 +553,22 @@
         [planes(2)],
     )
     far2 = across(acc2, masks[0])
-    pe, po, winner = call(
-        early_kernel,
-        [planes(6), planes(6), planes(tile - 2)],
-        (w, coef, one, ends, two, wtwo, three, uthree),
-    )
-    pe, po = swap_pairs(pe, po)
-    (other,) = call(pick_kernel, [planes(2)], (ce, co))
+    we, wo, winner = call(
+        early_w_kernel, [planes(3), planes(3), planes(tile - 2)], (w, coef, one, two, wtwo)
+    )
+    we, wo = swap_pairs(we, wo)
+    (other,) = call(pick_kernel, [planes(2)], (be, bo))
     other = across(other, 1)
 
     (part,) = call(weigh_kernel, [planes(2, tile)], (acc1, acc2, far1, far2))
     for mask in masks[1:-1]:
         part = part + across(part, mask)
     rest = across(part, masks[-1])
-    pen, wthree, base, last = call(
-        late_kernel,
-        [planes(tile), planes(2), planes(2, 2), planes(2)],
-        (w, velocity, conductivity, fields, coef, ends, two, wtwo, halo, beyond, ce, co, other),
-        [planes(tile + 2), planes(2), planes(2)],
+    (pen,) = call(
+        penalty_kernel,
+        [planes(tile)],
+        (velocity, conductivity, be, bo, other),
+        [planes(tile + 2), planes(2)],
     )
     coef_next, e, o = call(
         lambda *refs: renew_kernel(scale, *refs),
@@ -581,17 +580,20 @@
         lambda *refs: models_kernel(scale, *refs),
         [planes(2, tile)], (part, rest, pen, velocity, conductivity),
     )
-    four, five, ring, lap, side = call(
+    four, five, ring, lap, side, wthree = call(
         before_kernel,
-        [planes(2, tile), planes(2, tile - 2), planes(2, 2, 2), planes(2, 2, 2), planes(2, 2)],
-        (w, coef_next, two, wtwo, three, uthree, winner, wthree, base, halo, beyond, last, pe, po),
-        [planes(tile + 6), planes(2)],
+        [planes(2, tile), planes(2, tile - 2), planes(2, 2, 2), planes(2, 2, 2), planes(2, 2), planes(2)],
+        (w, coef_next, coef, ends, two, wtwo, three, uthree, winner, halo, beyond, ue, uo, we, wo),
+        [planes(tile + 6), planes(2), planes(2)],
     )
     (final,) = call(
         after_kernel,
         [planes(1, 2, tile)],
         (w, coef_next, four, five, ring, lap, side, uthree, wthree, e, o),
-        [planes(2, 2), planes(2, 2), planes(2, 2)],
+        [planes(2, 2), planes(2, 2), planes(2, 2), planes(2, tile)],
+        None,
+        [pltpu.SemaphoreType.DMA((2, tile))],
+        pl.BlockSpec(memory_space=pltpu.HBM),
     )
     return final, models
 

time: 47.5 us -> 45.7 us (0.962)
  the two profiles are of different devices: /device:TPU:0 before, /device:TPU:16 now
where the time goes in v4:
time: 45.7 us; the launch traced here: 45.5 us
  starting transfers between devices  21.2 us (46%)
  waiting for transfers between devices  15.3 us (33%)
  Pallas kernels  7.46 us (16%)
  between operations  1.45 us (3%)
    ppermute x5, starting transfers between devices, swap_pairs(): odd_block = lax.ppermute(odd_block, 'space', odds)  13.6 us
    ppermute x5, waiting for transfers between devices, swap_pairs(): odd_block = lax.ppermute(odd_block, 'space', odds)  9.87 us
    pallas_call x12, Pallas kernels, call(): pl.pallas_call(kernel, out_shape=tuple((jax.ShapeDtypeStruct(o, F32) for...  7.46 us
    ppermute x5, starting transfers between devices, swap_pairs(): even_block = lax.ppermute(even_block, 'space', evens)  3.92 us
    ppermute x4, waiting for transfers between devices, across(): return lax.ppermute(block, 'src', [(i, i ^ mask) for i in range(count)])  3.77 us
    ppermute x4, starting transfers between devices, across(): return lax.ppermute(block, 'src', [(i, i ^ mask) for i in range(count)])  3.74 us
    ppermute x5, waiting for transfers between devices, swap_pairs(): even_block = lax.ppermute(even_block, 'space', evens)  1.68 us
  transfers between devices with their start and end apart: 14, of which 5 were waited for; matrix products, arithmetic and copies ran while one was open for 0% of the time, Pallas kernels for 9%

profile of v4, /device:TPU:16, one launch (start us, length us, event | category | flops | bytes accessed | tf_op | source)
XLA Modules:
  0.0 45.5 jit_solution(4358710815142489009)
XLA Ops:
  1.3 1.9 %shard_map.59 = (f32[4,128,128]{2,1,0:T(8,128)S(1)}, f32[4,128,128]{2,1,0:T(8,128)S(1)}, f32[3,128,128]{2,1,0:T(8,128)S(1)}, f32[3,128,128]{2,1,0:T(8,128)S(1)},...) custom-call(s32[1]{0:T(128)S(6)} %copy.6.label, ...), custom_call_target="tpu_custom_call" | custom-call | flops 25579540 | bytes 5115908 | tf_op jit(solution)/shard_map/pallas_call | solution.py:22
  3.2 1.6 %collective-permute-start = (f32[4,128,128]{2,1,0:T(8,128)S(1)}, f32[4,128,128]{2,1,0:T(8,128)S(1)}, u32[]{:S(2)}, u32[]{:S(2)}) collective-permute-start(f32[4,128,128]{2,1,0:T(8,128)S(1)} %get-tuple-element.42), channel_id=1, source_target_pairs={{0,1},{1,0},{2,3},{3,2},{4,5},{5,4},{6,7},{7,6},{8,9},{9,8},{10,11... | collective-permute-start | bytes 786440 | tf_op jit(solution)/shard_map/ppermute | solution.py:506
  4.8 1.9 %collective-permute-start.1 = (f32[4,128,128]{2,1,0:T(8,128)S(1)}, f32[4,128,128]{2,1,0:T(8,128)S(1)}, u32[]{:S(2)}, u32[]{:S(2)}) collective-permute-start(f32[4,128,128]{2,1,0:T(8,128)S(1)} %get-tuple-element.43), channel_id=1, source_target_pairs={{1,2},{2,1},{5,6},{6,5},{9,10},{10,9},{13,14},{14,13},{17,18},{18,... | collective-permute-start | bytes 786440 | tf_op jit(solution)/shard_map/ppermute | solution.py:505
  6.7 0.1 collective-permute-start.2
  6.8 3.9 %collective-permute-start.3 = (f32[3,128,128]{2,1,0:T(8,128)S(1)}, f32[3,128,128]{2,1,0:T(8,128)S(1)}, u32[]{:S(2)}, u32[]{:S(2)}) collective-permute-start(f32[3,128,128]{2,1,0:T(8,128)S(1)} %get-tuple-element.50), channel_id=1, source_target_pairs={{1,2},{2,1},{5,6},{6,5},{9,10},{10,9},{13,14},{14,13},{17,18},{18,... | collective-permute-start | bytes 589832 | tf_op jit(solution)/shard_map/ppermute | solution.py:505
  10.8 1.7 %collective-permute-done.ae = f32[4,128,128]{2,1,0:T(8,128)S(1)} collective-permute-done((f32[4,128,128]{2,1,0:T(8,128)S(1)}, f32[4,128,128]{2,1,0:T(8,128)S(1)}, u32[]{:S(2)}, u32[]{:S(2)}) %collective-permute-start) | collective-permute-done | bytes 262176 | tf_op jit(solution)/shard_map/ppermute | solution.py:506
  12.4 3.5 %collective-permute-done.1.ao = f32[4,128,128]{2,1,0:T(8,128)S(1)} collective-permute-done((f32[4,128,128]{2,1,0:T(8,128)S(1)}, f32[4,128,128]{2,1,0:T(8,128)S(1)}, u32[]{:S(2)}, u32[]{:S(2)}) %collective-permute-start.1) | collective-permute-done | bytes 262176 | tf_op jit(solution)/shard_map/ppermute | solution.py:505
  15.9 0.5 %shard_map.60 = (f32[264,128]{1,0:T(8,128)S(1)}, f32[2,128,128]{2,1,0:T(8,128)S(1)}, f32[2,2,128,128]{3,2,1,0:T(8,128)S(1)}, f32[2,4,128,128]{3,2,1,0:T(8,128)S(...) custom-call(f32[8,128]{1,0:T(8,128)S(1)} %get-tuple-element.37.w.refs_0_, ...), custom_call_target="tpu_custom_call" | custom-call | flops 21012480 | bytes 4202496 | tf_op jit(solution)/shard_map/pallas_call | solution.py:22
  16.4 1.6 %collective-permute-start.4 = (f32[264,128]{1,0:T(8,128)S(1)}, f32[264,128]{1,0:T(8,128)S(1)}, u32[]{:S(2)}, u32[]{:S(2)}) collective-permute-start(f32[264,128]{1,0:T(8,128)S(1)} %get-tuple-element.44.acc1), channel_id=1, source_target_pairs={{0,8},{4,12},{8,0},{12,4},{1,9},{5,13},{9,1},{13,5},{2,10},{6,14},... | collective-permute-start | bytes 405512 | tf_op jit(solution)/shard_map/ppermute | solution.py:512
  18.0 0.0 collective-permute-done.2.be
  18.0 0.7 %collective-permute-done.3.bo = f32[3,128,128]{2,1,0:T(8,128)S(1)} collective-permute-done((f32[3,128,128]{2,1,0:T(8,128)S(1)}, f32[3,128,128]{2,1,0:T(8,128)S(1)}, u32[]{:S(2)}, u32[]{:S(2)}) %collective-permute-start.3) | collective-permute-done | bytes 196640 | tf_op jit(solution)/shard_map/ppermute | solution.py:505
  18.7 0.3 shard_map.61
  19.0 1.6 %collective-permute-start.5 = (f32[256,128]{1,0:T(8,128)S(1)}, f32[256,128]{1,0:T(8,128)S(1)}, u32[]{:S(2)}, u32[]{:S(2)}) collective-permute-start(f32[256,128]{1,0:T(8,128)S(1)} %get-tuple-element.51.acc2), channel_id=1, source_target_pairs={{0,8},{4,12},{8,0},{12,4},{1,9},{5,13},{9,1},{13,5},{2,10},{6,14},... | collective-permute-start | bytes 393224 | tf_op jit(solution)/shard_map/ppermute | solution.py:512
  20.6 3.8 %collective-permute-done.5.far2 = f32[256,128]{1,0:T(8,128)S(1)} collective-permute-done((f32[256,128]{1,0:T(8,128)S(1)}, f32[256,128]{1,0:T(8,128)S(1)}, u32[]{:S(2)}, u32[]{:S(2)}) %collective-permute-start.5) | collective-permute-done | bytes 131104 | tf_op jit(solution)/shard_map/ppermute | solution.py:512
  24.3 0.0 collective-permute-done.4.far1
  24.3 0.1 shard_map.62.refs_1_.refs_0_
  24.4 0.1 collective-permute-start.6
  24.5 0.6 %collective-permute-start.7 = (f32[2,128,128]{2,1,0:T(8,128)S(1)}, f32[2,128,128]{2,1,0:T(8,128)S(1)}, u32[]{:S(2)}, u32[]{:S(2)}) collective-permute-start(f32[2,128,128]{2,1,0:T(8,128)S(1)} %shard_map.63), channel_id=1, source_target_pairs={{0,4},{4,0},{8,12},{12,8},{1,5},{5,1},{9,13},{13,9},{2,6},{6,2},{1... | collective-permute-start | bytes 393224 | tf_op jit(solution)/shard_map/ppermute | solution.py:512
  25.0 0.2 shard_map.66
  25.2 0.1 collective-permute-start.10
  25.3 2.1 %collective-permute-start.8 = (f32[4,128,128]{2,1,0:T(8,128)S(1)}, f32[4,128,128]{2,1,0:T(8,128)S(1)}, u32[]{:S(2)}, u32[]{:S(2)}) collective-permute-start(f32[4,128,128]{2,1,0:T(8,128)S(1)} %get-tuple-element.60), channel_id=1, source_target_pairs={{0,1},{1,0},{2,3},{3,2},{4,5},{5,4},{6,7},{7,6},{8,9},{9,8},{10,11... | collective-permute-start | bytes 786440 | tf_op jit(solution)/shard_map/ppermute | solution.py:506
  27.4 1.9 %collective-permute-start.9 = (f32[4,128,128]{2,1,0:T(8,128)S(1)}, f32[4,128,128]{2,1,0:T(8,128)S(1)}, u32[]{:S(2)}, u32[]{:S(2)}) collective-permute-start(f32[4,128,128]{2,1,0:T(8,128)S(1)} %get-tuple-element.61), channel_id=1, source_target_pairs={{1,2},{2,1},{5,6},{6,5},{9,10},{10,9},{13,14},{14,13},{17,18},{18,... | collective-permute-start | bytes 786440 | tf_op jit(solution)/shard_map/ppermute | solution.py:505
  29.3 0.0 collective-permute-done.7.other
  29.3 3.9 %collective-permute-start.11 = (f32[3,128,128]{2,1,0:T(8,128)S(1)}, f32[3,128,128]{2,1,0:T(8,128)S(1)}, u32[]{:S(2)}, u32[]{:S(2)}) collective-permute-start(f32[3,128,128]{2,1,0:T(8,128)S(1)} %get-tuple-element.63), channel_id=1, source_target_pairs={{1,2},{2,1},{5,6},{6,5},{9,10},{10,9},{13,14},{14,13},{17,18},{18,... | collective-permute-start | bytes 589832 | tf_op jit(solution)/shard_map/ppermute | solution.py:505
  33.3 0.4 shard_map.64.refs_3_.refs_2_
  33.7 0.0 collective-permute-done.6.refs_2_.refs_1_
  33.7 0.2 shard_map.65
  33.9 0.1 collective-permute-start.12
  34.0 0.0 collective-permute-done.10.we
  34.0 1.9 %collective-permute-start.13 = (f32[2,128,128]{2,1,0:T(8,128)S(1)}, f32[2,128,128]{2,1,0:T(8,128)S(1)}, u32[]{:S(2)}, u32[]{:S(2)}) collective-permute-start(f32[2,128,128]{2,1,0:T(8,128)S(1)} %get-tuple-element.71), channel_id=1, source_target_pairs={{1,2},{2,1},{5,6},{6,5},{9,10},{10,9},{13,14},{14,13},{17,18},{18,... | collective-permute-start | bytes 393224 | tf_op jit(solution)/shard_map/ppermute | solution.py:505
  35.9 1.0 %shard_map.70 = f32[2,4,128,128]{3,2,1,0:T(8,128)} custom-call(f32[2,4,128,128]{3,2,1,0:T(8,128)S(1)} %shard_map.62.refs_1_.refs_0_, f32[2,4,128,128]{3,2,1,0:T(8,128)S(1)} %collective-permute-done.6.refs_2_.refs_1_, f32[4,128,128]{2,1,0:T(8,128)S(1)} %shard_map.64.refs_3_.refs_2_, f32[4,128,128]{2,1,0:T(8,128)S(1)} %get-tuple-element.52.v.refs_4_.refs_3_, ...), custom_call_target="tpu_custom_call" | custom-call | flops 11796480 | bytes 2359296 | tf_op jit(solution)/shard_map/pallas_call | solution.py:22
  36.9 5.7 %collective-permute-done.11.wo = f32[3,128,128]{2,1,0:T(8,128)S(1)} collective-permute-done((f32[3,128,128]{2,1,0:T(8,128)S(1)}, f32[3,128,128]{2,1,0:T(8,128)S(1)}, u32[]{:S(2)}, u32[]{:S(2)}) %collective-permute-start.11) | collective-permute-done | bytes 196640 | tf_op jit(solution)/shard_map/ppermute | solution.py:505
  42.6 0.0 collective-permute-done.8.ue
  42.6 0.0 collective-permute-done.9.uo
  42.6 1.3 %shard_map.68 = (f32[2,4,128,128]{3,2,1,0:T(8,128)S(1)}, f32[2,2,128,128]{3,2,1,0:T(8,128)S(1)}, f32[2,2,2,128,128]{4,3,2,1,0:T(8,128)S(1)}, f32[2,2,2,128,128]{...) custom-call(f32[8,128]{1,0:T(8,128)S(1)} %get-tuple-element.37.w.refs_0_, ...), custom_call_target="tpu_custom_call" | custom-call | flops 28200960 | bytes 5640192 | tf_op jit(solution)/shard_map/pallas_call | solution.py:22
  43.9 0.0 collective-permute-done.12.e
  43.9 0.0 collective-permute-done.13.o
  44.0 1.5 %shard_map.69 = f32[1,2,4,128,128]{4,3,2,1,0:T(8,128)} custom-call(f32[8,128]{1,0:T(8,128)S(1)} %get-tuple-element.37.w.refs_0_, f32[4,128,128]{2,1,0:T(8,128)S(1)} %get-tuple-element.54.coef, f32[2,4,128,128]{3,2,1,0:T(8,128)S(1)} %get-tuple-element.64.four, f32[2,2,128,128]{3,2,1,0:T(8,128)S(1)} %get-tuple-element.65.five, ...), custom_call_target="tpu_custom_call" | custom-call | flops 17059840 | bytes 3411968 | tf_op jit(solution)/shard_map/pallas_call | solution.py:22
  (2 shorter events, 0.1 us)
Async XLA Ops:
  3.2 9.2 %collective-permute-start = (f32[4,128,128]{2,1,0:T(8,128)S(1)}, f32[4,128,128]{2,1,0:T(8,128)S(1)}, u32[]{:S(2)}, u32[]{:S(2)}) collective-permute-start(f32[4,128,128]{2,1,0:T(8,128)S(1)} %get-tuple-element.42), channel_id=1, source_target_pairs={{0,1},{1,0},{2,3},{3,2},{4,5},{5,4},{6,7},{7,6},{8,9},{9,8},{10,11... | collective-permute-start | bytes 786440 | tf_op jit(solution)/shard_map/ppermute | solution.py:506
  4.8 11.1 %collective-permute-start.1 = (f32[4,128,128]{2,1,0:T(8,128)S(1)}, f32[4,128,128]{2,1,0:T(8,128)S(1)}, u32[]{:S(2)}, u32[]{:S(2)}) collective-permute-start(f32[4,128,128]{2,1,0:T(8,128)S(1)} %get-tuple-element.43), channel_id=1, source_target_pairs={{1,2},{2,1},{5,6},{6,5},{9,10},{10,9},{13,14},{14,13},{17,18},{18,... | collective-permute-start | bytes 786440 | tf_op jit(solution)/shard_map/ppermute | solution.py:505
  6.7 11.3 %collective-permute-start.2 = (f32[3,128,128]{2,1,0:T(8,128)S(1)}, f32[3,128,128]{2,1,0:T(8,128)S(1)}, u32[]{:S(2)}, u32[]{:S(2)}) collective-permute-start(f32[3,128,128]{2,1,0:T(8,128)S(1)} %get-tuple-element.49), channel_id=1, source_target_pairs={{0,1},{1,0},{2,3},{3,2},{4,5},{5,4},{6,7},{7,6},{8,9},{9,8},{10,11... | collective-permute-start | bytes 589832 | tf_op jit(solution)/shard_map/ppermute | solution.py:506
  6.8 11.9 %collective-permute-start.3 = (f32[3,128,128]{2,1,0:T(8,128)S(1)}, f32[3,128,128]{2,1,0:T(8,128)S(1)}, u32[]{:S(2)}, u32[]{:S(2)}) collective-permute-start(f32[3,128,128]{2,1,0:T(8,128)S(1)} %get-tuple-element.50), channel_id=1, source_target_pairs={{1,2},{2,1},{5,6},{6,5},{9,10},{10,9},{13,14},{14,13},{17,18},{18,... | collective-permute-start | bytes 589832 | tf_op jit(solution)/shard_map/ppermute | solution.py:505
  16.4 7.9 %collective-permute-start.4 = (f32[264,128]{1,0:T(8,128)S(1)}, f32[264,128]{1,0:T(8,128)S(1)}, u32[]{:S(2)}, u32[]{:S(2)}) collective-permute-start(f32[264,128]{1,0:T(8,128)S(1)} %get-tuple-element.44.acc1), channel_id=1, source_target_pairs={{0,8},{4,12},{8,0},{12,4},{1,9},{5,13},{9,1},{13,5},{2,10},{6,14},... | collective-permute-start | bytes 405512 | tf_op jit(solution)/shard_map/ppermute | solution.py:512
  19.0 5.3 %collective-permute-start.5 = (f32[256,128]{1,0:T(8,128)S(1)}, f32[256,128]{1,0:T(8,128)S(1)}, u32[]{:S(2)}, u32[]{:S(2)}) collective-permute-start(f32[256,128]{1,0:T(8,128)S(1)} %get-tuple-element.51.acc2), channel_id=1, source_target_pairs={{0,8},{4,12},{8,0},{12,4},{1,9},{5,13},{9,1},{13,5},{2,10},{6,14},... | collective-permute-start | bytes 393224 | tf_op jit(solution)/shard_map/ppermute | solution.py:512
  24.4 9.3 %collective-permute-start.6 = (f32[2,4,128,128]{3,2,1,0:T(8,128)S(1)}, f32[2,4,128,128]{3,2,1,0:T(8,128)S(1)}, u32[]{:S(2)}, u32[]{:S(2)}) collective-permute-start(f32[2,4,128,128]{3,2,1,0:T(8,128)S(1)} %shard_map.62.refs_1_.refs_0_), channel_id=1, source_target_pairs={{0,4},{4,0},{8,12},{12,8},{1,5},{5,1},{9,13},{13,9},{2,6},{6,2},{1... | collective-permute-start | bytes 1572872 | tf_op jit(solution)/shard_map/ppermute | solution.py:512
  24.5 4.8 %collective-permute-start.7 = (f32[2,128,128]{2,1,0:T(8,128)S(1)}, f32[2,128,128]{2,1,0:T(8,128)S(1)}, u32[]{:S(2)}, u32[]{:S(2)}) collective-permute-start(f32[2,128,128]{2,1,0:T(8,128)S(1)} %shard_map.63), channel_id=1, source_target_pairs={{0,4},{4,0},{8,12},{12,8},{1,5},{5,1},{9,13},{13,9},{2,6},{6,2},{1... | collective-permute-start | bytes 393224 | tf_op jit(solution)/shard_map/ppermute | solution.py:512
  25.2 8.8 %collective-permute-start.10 = (f32[3,128,128]{2,1,0:T(8,128)S(1)}, f32[3,128,128]{2,1,0:T(8,128)S(1)}, u32[]{:S(2)}, u32[]{:S(2)}) collective-permute-start(f32[3,128,128]{2,1,0:T(8,128)S(1)} %get-tuple-element.62), channel_id=1, source_target_pairs={{0,1},{1,0},{2,3},{3,2},{4,5},{5,4},{6,7},{7,6},{8,9},{9,8},{10,11... | collective-permute-start | bytes 589832 | tf_op jit(solution)/shard_map/ppermute | solution.py:506
  25.3 17.2 %collective-permute-start.8 = (f32[4,128,128]{2,1,0:T(8,128)S(1)}, f32[4,128,128]{2,1,0:T(8,128)S(1)}, u32[]{:S(2)}, u32[]{:S(2)}) collective-permute-start(f32[4,128,128]{2,1,0:T(8,128)S(1)} %get-tuple-element.60), channel_id=1, source_target_pairs={{0,1},{1,0},{2,3},{3,2},{4,5},{5,4},{6,7},{7,6},{8,9},{9,8},{10,11... | collective-permute-start | bytes 786440 | tf_op jit(solution)/shard_map/ppermute | solution.py:506
  27.4 15.2 %collective-permute-start.9 = (f32[4,128,128]{2,1,0:T(8,128)S(1)}, f32[4,128,128]{2,1,0:T(8,128)S(1)}, u32[]{:S(2)}, u32[]{:S(2)}) collective-permute-start(f32[4,128,128]{2,1,0:T(8,128)S(1)} %get-tuple-element.61), channel_id=1, source_target_pairs={{1,2},{2,1},{5,6},{6,5},{9,10},{10,9},{13,14},{14,13},{17,18},{18,... | collective-permute-start | bytes 786440 | tf_op jit(solution)/shard_map/ppermute | solution.py:505
  29.3 13.2 %collective-permute-start.11 = (f32[3,128,128]{2,1,0:T(8,128)S(1)}, f32[3,128,128]{2,1,0:T(8,128)S(1)}, u32[]{:S(2)}, u32[]{:S(2)}) collective-permute-start(f32[3,128,128]{2,1,0:T(8,128)S(1)} %get-tuple-element.63), channel_id=1, source_target_pairs={{1,2},{2,1},{5,6},{6,5},{9,10},{10,9},{13,14},{14,13},{17,18},{18,... | collective-permute-start | bytes 589832 | tf_op jit(solution)/shard_map/ppermute | solution.py:505
  33.9 10.0 %collective-permute-start.12 = (f32[2,128,128]{2,1,0:T(8,128)S(1)}, f32[2,128,128]{2,1,0:T(8,128)S(1)}, u32[]{:S(2)}, u32[]{:S(2)}) collective-permute-start(f32[2,128,128]{2,1,0:T(8,128)S(1)} %get-tuple-element.70), channel_id=1, source_target_pairs={{0,1},{1,0},{2,3},{3,2},{4,5},{5,4},{6,7},{7,6},{8,9},{9,8},{10,11... | collective-permute-start | bytes 393224 | tf_op jit(solution)/shard_map/ppermute | solution.py:506
  34.0 10.0 %collective-permute-start.13 = (f32[2,128,128]{2,1,0:T(8,128)S(1)}, f32[2,128,128]{2,1,0:T(8,128)S(1)}, u32[]{:S(2)}, u32[]{:S(2)}) collective-permute-start(f32[2,128,128]{2,1,0:T(8,128)S(1)} %get-tuple-element.71), channel_id=1, source_target_pairs={{1,2},{2,1},{5,6},{6,5},{9,10},{10,9},{13,14},{14,13},{17,18},{18,... | collective-permute-start | bytes 393224 | tf_op jit(solution)/shard_map/ppermute | solution.py:505

commit v5 on v4

--- a/solution.py
+++ b/solution.py
@@ -117,33 +117,47 @@
 
     def unpack(self, even_ref, odd_ref, k, r):
         e, o = self.get(Plane(even_ref, k), r), self.get(Plane(odd_ref, k), r)
-        return jnp.where(self.even, o, e), jnp.where(self.even, e, o)
+        low, high = jnp.where(self.even, o, e), jnp.where(self.even, e, o)
+        return jnp.where(self.has[0], low, 0.0), jnp.where(self.has[1], high, 0.0)
 
 
 def near(make, i, tile, ends=(None, None)):
     return (make(i - 1) if i > 0 else ends[0]), (make(i + 1) if i < tile - 1 else ends[1])
 
 
-def isolated_kernel(
-    label, f_in, v_in, c_in,
-    ae, ao, be, bo, coef, one, acc, w, f, v, c, two, sems,
-):
-    copies = [
-        pltpu.make_async_copy(src, dst, sems.at[n])
-        for n, (src, dst) in enumerate(((v_in, v), (c_in, c), (f_in, f)))
-    ]
+def lead_kernel(label, f_in, v_in, c_in, ae, ao, coef, w, f, v, c, one, sems):
+    parts = [(v_in, v), (c_in, c)] + [(f_in.at[0, n], f.at[0, n]) for n in (0, 1, 2, 3)]
+    copies = [pltpu.make_async_copy(src, dst, sems.at[n]) for n, (src, dst) in enumerate(parts)]
     for copy in copies:
         copy.start()
     tile, ny, nz = v.shape
     w[...] = jnp.full(w.shape, label[0].astype(F32), F32)
     k = Work(w, ny, nz)
+    edge = (0, tile - 1)
     copies[0].wait()
     copies[1].wait()
-    edge = (0, tile - 1)
     for i in range(tile):
         for r in k.blocks():
             k.put(Plane(coef, i), r, k.coefficient(v[i, r:r + k.n], c[i, r:r + k.n]))
     copies[2].wait()
+    copies[3].wait()
+    for s, i in enumerate(edge):
+        k.step(
+            Plane(one, s), Plane(f, 0, 0, i), Plane(f, 0, 1, i), Plane(coef, i),
+            *near(lambda j: Plane(f, 0, 0, j), i, tile),
+        )
+    copies[4].wait()
+    k.pack(ae, ao, *(
+        [Plane(coef, i), Plane(f, 0, 0, i), Plane(f, 0, 2, i), Plane(one, s)]
+        for s, i in enumerate(edge)
+    ))
+    copies[5].wait()
+
+
+def isolated_kernel(w, f, v, c, coef, be, bo, one, acc, two):
+    tile, ny, nz = v.shape
+    k = Work(w, ny, nz)
+    edge = (0, tile - 1)
     for n in range(2):
         for i in range(tile):
 
@@ -159,10 +173,6 @@
             Plane(two, s), Plane(one, 0, i), Plane(f, 0, 0, i), Plane(coef, i),
             *near(lambda j: Plane(one, 0, j), i, tile),
         )
-    sides = [
-        [Plane(coef, i), Plane(f, 0, 0, i), Plane(f, 0, 2, i), Plane(one, 0, i)] for i in edge
-    ]
-    k.pack(ae, ao, *sides)
     k.pack(be, bo, *([Plane(two, s), Plane(one, 1, i)] for s, i in enumerate(edge)))
     for r in k.blocks():
         lo, hi = (
@@ -499,11 +509,19 @@
 
 
 def swap_pairs(even_block, odd_block):
-    count = lax.axis_size("space")
-    evens = [(i, i ^ 1) for i in range(count) if i ^ 1 < count]
-    odds = [(i, ((i + 1) ^ 1) - 1) for i in range(count) if 0 <= ((i + 1) ^ 1) - 1 < count]
-    odd_block = lax.ppermute(odd_block, "space", odds)
-    even_block = lax.ppermute(even_block, "space", evens)
+    count, groups = lax.axis_size("space"), lax.axis_size("src")
+
+    def swap(block, partner):
+        pairs = []
+        for g in range(groups):
+            for i in range(count):
+                j = partner(i)
+                to = g * count + j if 0 <= j < count else (g ^ 1) * count + i
+                pairs.append((g * count + i, to))
+        return lax.ppermute(block, ("src", "space"), pairs)
+
+    odd_block = swap(odd_block, lambda i: ((i + 1) ^ 1) - 1)
+    even_block = swap(even_block, lambda i: i ^ 1)
     return even_block, odd_block
 
 
@@ -521,19 +539,24 @@
     def planes(*lead):
         return (*lead, ny, nz)
 
-    ae, ao, be, bo, coef, one, acc, w, fields, velocity, conductivity = call(
-        isolated_kernel,
-        [planes(4)] * 2 + [planes(3)] * 2 + [planes(tile), planes(2, tile), planes(tile)]
-        + [(8, nz), fields.shape, velocity.shape, conductivity.shape],
+    ae, ao, coef, w, fields, velocity, conductivity = call(
+        lead_kernel,
+        [planes(4)] * 2 + [planes(tile), (8, nz), fields.shape, velocity.shape, conductivity.shape],
         (
             labels,
             *(pltpu.with_memory_space_constraint(x, pltpu.HBM) for x in (fields, velocity, conductivity)),
         ),
         [planes(2)],
         [pl.BlockSpec(memory_space=pltpu.SMEM)] + [pl.BlockSpec(memory_space=pltpu.HBM)] * 3,
-        [pltpu.SemaphoreType.DMA((3,))],
+        [pltpu.SemaphoreType.DMA((6,))],
     )
     ae, ao = swap_pairs(ae, ao)
+    be, bo, one, acc = call(
+        isolated_kernel,
+        [planes(3), planes(3), planes(2, tile), planes(tile)],
+        (w, fields, velocity, conductivity, coef),
+        [planes(2)],
+    )
     be, bo = swap_pairs(be, bo)
 
     acc1, rim, ends, two, three, halo = call(

time: 45.7 us -> 41.4 us (0.906)
  starting transfers between devices: 21.2 us -> 11.8 us
  waiting for transfers between devices: 15.3 us -> 20.6 us
    ppermute x10, starting transfers between devices: 17.5 us -> 8.05 us  [swap(): return lax.ppermute(block, ('src', 'space'), pairs)]
    ppermute x10, waiting for transfers between devices: 11.6 us -> 16.8 us  [swap(): return lax.ppermute(block, ('src', 'space'), pairs)]
    pallas_call x12 -> x13, Pallas kernels: 7.46 us -> 7.49 us  [call(): pl.pallas_call(kernel, out_shape=tuple((jax.ShapeDtypeStruct(o, F32) for...]
  transfers between devices with their start and end apart: 14 -> 14, of which waited for: 5 -> 6; matrix products, arithmetic and copies ran while one was open for 0% -> 0% of each run, Pallas kernels for 9% -> 11%
where the time goes in v5:
time: 41.4 us; the launch traced here: 41.2 us
  waiting for transfers between devices  20.6 us (50%)
  starting transfers between devices  11.8 us (29%)
  Pallas kernels  7.49 us (18%)
  between operations  1.4 us (3%)
    ppermute x10, waiting for transfers between devices, swap(): return lax.ppermute(block, ('src', 'space'), pairs)  16.8 us
    ppermute x10, starting transfers between devices, swap(): return lax.ppermute(block, ('src', 'space'), pairs)  8.05 us
    pallas_call x13, Pallas kernels, call(): pl.pallas_call(kernel, out_shape=tuple((jax.ShapeDtypeStruct(o, F32) for...  7.49 us
    ppermute x4, waiting for transfers between devices, across(): return lax.ppermute(block, 'src', [(i, i ^ mask) for i in range(count)])  3.78 us
    ppermute x4, starting transfers between devices, across(): return lax.ppermute(block, 'src', [(i, i ^ mask) for i in range(count)])  3.74 us
  transfers between devices with their start and end apart: 14, of which 6 were waited for; matrix products, arithmetic and copies ran while one was open for 0% of the time, Pallas kernels for 11%

profile of v5, /device:TPU:16, one launch (start us, length us, event | category | flops | bytes accessed | tf_op | source)
XLA Modules:
  0.0 41.2 jit_solution(8081056346185095138)
XLA Ops:
  1.3 1.4 %shard_map.59 = (f32[4,128,128]{2,1,0:T(8,128)S(1)}, f32[4,128,128]{2,1,0:T(8,128)S(1)}, f32[4,128,128]{2,1,0:T(8,128)S(1)}, f32[8,128]{1,0:T(8,128)S(1)}, f32[1...) custom-call(s32[1]{0:T(128)S(6)} %copy.6.label, ...), custom_call_target="tpu_custom_call" | custom-call | flops 19681300 | bytes 3936260 | tf_op jit(solution)/shard_map/pallas_call | solution.py:22
  2.7 1.6 %collective-permute-start = (f32[4,128,128]{2,1,0:T(8,128)S(1)}, f32[4,128,128]{2,1,0:T(8,128)S(1)}, u32[]{:S(2)}, u32[]{:S(2)}) collective-permute-start(f32[4,128,128]{2,1,0:T(8,128)S(1)} %get-tuple-element.44), channel_id=1, source_target_pairs={{0,1},{1,0},{2,3},{3,2},{4,5},{5,4},{6,7},{7,6},{8,9},{9,8},{10,11... | collective-permute-start | bytes 786440 | tf_op jit(solution)/shard_map/ppermute | solution.py:521
  4.4 0.0 collective-permute-start.1
  4.4 0.5 %shard_map.60 = (f32[3,128,128]{2,1,0:T(8,128)S(1)}, f32[3,128,128]{2,1,0:T(8,128)S(1)}, f32[2,4,128,128]{3,2,1,0:T(8,128)S(1)}, f32[4,128,128]{2,1,0:T(8,128)S(1)}) custom-call(f32[8,128]{1,0:T(8,128)S(1)} %get-tuple-element.37.w.refs_0_, f32[1,4,4,128,128]{4,3,2,1,0:T(8,128)S(1)} %get-tuple-element.38.f, ...), custom_call_target="tpu_custom_call" | custom-call | flops 15093760 | bytes 3018752 | tf_op jit(solution)/shard_map/pallas_call | solution.py:22
  4.9 0.5 %collective-permute-start.2 = (f32[3,128,128]{2,1,0:T(8,128)S(1)}, f32[3,128,128]{2,1,0:T(8,128)S(1)}, u32[]{:S(2)}, u32[]{:S(2)}) collective-permute-start(f32[3,128,128]{2,1,0:T(8,128)S(1)} %get-tuple-element.51), channel_id=1, source_target_pairs={{0,1},{1,0},{2,3},{3,2},{4,5},{5,4},{6,7},{7,6},{8,9},{9,8},{10,11... | collective-permute-start | bytes 589832 | tf_op jit(solution)/shard_map/ppermute | solution.py:521
  5.4 1.7 %collective-permute-start.3 = (f32[3,128,128]{2,1,0:T(8,128)S(1)}, f32[3,128,128]{2,1,0:T(8,128)S(1)}, u32[]{:S(2)}, u32[]{:S(2)}) collective-permute-start(f32[3,128,128]{2,1,0:T(8,128)S(1)} %get-tuple-element.52), channel_id=1, source_target_pairs={{0,4},{1,2},{2,1},{3,7},{4,0},{5,6},{6,5},{7,3},{8,12},{9,10},{10,... | collective-permute-start | bytes 589832 | tf_op jit(solution)/shard_map/ppermute | solution.py:521
  7.0 4.9 %collective-permute-done.ae = f32[4,128,128]{2,1,0:T(8,128)S(1)} collective-permute-done((f32[4,128,128]{2,1,0:T(8,128)S(1)}, f32[4,128,128]{2,1,0:T(8,128)S(1)}, u32[]{:S(2)}, u32[]{:S(2)}) %collective-permute-start) | collective-permute-done | bytes 262176 | tf_op jit(solution)/shard_map/ppermute | solution.py:521
  12.0 1.6 %collective-permute-done.1.ao = f32[4,128,128]{2,1,0:T(8,128)S(1)} collective-permute-done((f32[4,128,128]{2,1,0:T(8,128)S(1)}, f32[4,128,128]{2,1,0:T(8,128)S(1)}, u32[]{:S(2)}, u32[]{:S(2)}) %collective-permute-start.1) | collective-permute-done | bytes 262176 | tf_op jit(solution)/shard_map/ppermute | solution.py:521
  13.5 0.6 %shard_map.61 = (f32[264,128]{1,0:T(8,128)S(1)}, f32[2,128,128]{2,1,0:T(8,128)S(1)}, f32[2,2,128,128]{3,2,1,0:T(8,128)S(1)}, f32[2,4,128,128]{3,2,1,0:T(8,128)S(...) custom-call(f32[8,128]{1,0:T(8,128)S(1)} %get-tuple-element.37.w.refs_0_, ...), custom_call_target="tpu_custom_call" | custom-call | flops 21012480 | bytes 4202496 | tf_op jit(solution)/shard_map/pallas_call | solution.py:22
  14.1 1.6 %collective-permute-start.4 = (f32[264,128]{1,0:T(8,128)S(1)}, f32[264,128]{1,0:T(8,128)S(1)}, u32[]{:S(2)}, u32[]{:S(2)}) collective-permute-start(f32[264,128]{1,0:T(8,128)S(1)} %get-tuple-element.46.acc1), channel_id=1, source_target_pairs={{0,8},{4,12},{8,0},{12,4},{1,9},{5,13},{9,1},{13,5},{2,10},{6,14},... | collective-permute-start | bytes 405512 | tf_op jit(solution)/shard_map/ppermute | solution.py:530
  15.7 0.0 collective-permute-done.2.be
  15.7 0.7 %collective-permute-done.3.bo = f32[3,128,128]{2,1,0:T(8,128)S(1)} collective-permute-done((f32[3,128,128]{2,1,0:T(8,128)S(1)}, f32[3,128,128]{2,1,0:T(8,128)S(1)}, u32[]{:S(2)}, u32[]{:S(2)}) %collective-permute-start.3) | collective-permute-done | bytes 196640 | tf_op jit(solution)/shard_map/ppermute | solution.py:521
  16.3 0.3 shard_map.62
  16.7 1.6 %collective-permute-start.5 = (f32[256,128]{1,0:T(8,128)S(1)}, f32[256,128]{1,0:T(8,128)S(1)}, u32[]{:S(2)}, u32[]{:S(2)}) collective-permute-start(f32[256,128]{1,0:T(8,128)S(1)} %get-tuple-element.53.acc2), channel_id=1, source_target_pairs={{0,8},{4,12},{8,0},{12,4},{1,9},{5,13},{9,1},{13,5},{2,10},{6,14},... | collective-permute-start | bytes 393224 | tf_op jit(solution)/shard_map/ppermute | solution.py:530
  18.2 3.8 %collective-permute-done.5.far2 = f32[256,128]{1,0:T(8,128)S(1)} collective-permute-done((f32[256,128]{1,0:T(8,128)S(1)}, f32[256,128]{1,0:T(8,128)S(1)}, u32[]{:S(2)}, u32[]{:S(2)}) %collective-permute-start.5) | collective-permute-done | bytes 131104 | tf_op jit(solution)/shard_map/ppermute | solution.py:530
  22.0 0.0 collective-permute-done.4.far1
  22.0 0.1 shard_map.63.refs_1_.refs_0_
  22.0 0.1 collective-permute-start.6
  22.1 0.6 %collective-permute-start.7 = (f32[2,128,128]{2,1,0:T(8,128)S(1)}, f32[2,128,128]{2,1,0:T(8,128)S(1)}, u32[]{:S(2)}, u32[]{:S(2)}) collective-permute-start(f32[2,128,128]{2,1,0:T(8,128)S(1)} %shard_map.64), channel_id=1, source_target_pairs={{0,4},{4,0},{8,12},{12,8},{1,5},{5,1},{9,13},{13,9},{2,6},{6,2},{1... | collective-permute-start | bytes 393224 | tf_op jit(solution)/shard_map/ppermute | solution.py:530
  22.7 0.2 shard_map.67
  22.9 0.1 collective-permute-start.10
  23.0 2.1 %collective-permute-start.8 = (f32[4,128,128]{2,1,0:T(8,128)S(1)}, f32[4,128,128]{2,1,0:T(8,128)S(1)}, u32[]{:S(2)}, u32[]{:S(2)}) collective-permute-start(f32[4,128,128]{2,1,0:T(8,128)S(1)} %get-tuple-element.60), channel_id=1, source_target_pairs={{0,1},{1,0},{2,3},{3,2},{4,5},{5,4},{6,7},{7,6},{8,9},{9,8},{10,11... | collective-permute-start | bytes 786440 | tf_op jit(solution)/shard_map/ppermute | solution.py:521
  25.1 0.0 collective-permute-start.9
  25.1 0.0 collective-permute-done.7.other
  25.1 2.0 %collective-permute-start.11 = (f32[3,128,128]{2,1,0:T(8,128)S(1)}, f32[3,128,128]{2,1,0:T(8,128)S(1)}, u32[]{:S(2)}, u32[]{:S(2)}) collective-permute-start(f32[3,128,128]{2,1,0:T(8,128)S(1)} %get-tuple-element.63), channel_id=1, source_target_pairs={{0,4},{1,2},{2,1},{3,7},{4,0},{5,6},{6,5},{7,3},{8,12},{9,10},{10,... | collective-permute-start | bytes 589832 | tf_op jit(solution)/shard_map/ppermute | solution.py:521
  27.1 0.4 %shard_map.65.refs_3_.refs_2_ = f32[4,128,128]{2,1,0:T(8,128)S(1)} custom-call(f32[4,128,128]{2,1,0:T(8,128)S(1)} %get-tuple-element.40.v.refs_4_.refs_3_, f32[4,128,128]{2,1,0:T(8,128)S(1)} %get-tuple-element.41.c.refs_5_.refs_4_, f32[3,128,128]{2,1,0:T(8,128)S(1)} %collective-permute-done.2.be, f32[3,128,128]{2,1,0:T(8,128)S(1)} %collective-permute-done.3.bo, ...), custom_call_target="tpu_custom_call" | custom-call | flops 6553600 | bytes 1310720 | tf_op jit(solution)/shard_map/pallas_call | solution.py:22
  27.5 0.0 collective-permute-done.6.refs_2_.refs_1_
  27.6 0.2 shard_map.66
  27.7 0.1 collective-permute-start.12
  27.8 2.9 %collective-permute-done.10.we = f32[3,128,128]{2,1,0:T(8,128)S(1)} collective-permute-done((f32[3,128,128]{2,1,0:T(8,128)S(1)}, f32[3,128,128]{2,1,0:T(8,128)S(1)}, u32[]{:S(2)}, u32[]{:S(2)}) %collective-permute-start.10) | collective-permute-done | bytes 196640 | tf_op jit(solution)/shard_map/ppermute | solution.py:521
  30.7 0.0 collective-permute-start.13
  30.7 1.0 %shard_map.71 = f32[2,4,128,128]{3,2,1,0:T(8,128)} custom-call(f32[2,4,128,128]{3,2,1,0:T(8,128)S(1)} %shard_map.63.refs_1_.refs_0_, f32[2,4,128,128]{3,2,1,0:T(8,128)S(1)} %collective-permute-done.6.refs_2_.refs_1_, f32[4,128,128]{2,1,0:T(8,128)S(1)} %shard_map.65.refs_3_.refs_2_, f32[4,128,128]{2,1,0:T(8,128)S(1)} %get-tuple-element.40.v.refs_4_.refs_3_, ...), custom_call_target="tpu_custom_call" | custom-call | flops 11796480 | bytes 2359296 | tf_op jit(solution)/shard_map/pallas_call | solution.py:22
  31.7 6.7 %collective-permute-done.11.wo = f32[3,128,128]{2,1,0:T(8,128)S(1)} collective-permute-done((f32[3,128,128]{2,1,0:T(8,128)S(1)}, f32[3,128,128]{2,1,0:T(8,128)S(1)}, u32[]{:S(2)}, u32[]{:S(2)}) %collective-permute-start.11) | collective-permute-done | bytes 196640 | tf_op jit(solution)/shard_map/ppermute | solution.py:521
  38.4 0.0 collective-permute-done.8.ue
  38.4 0.0 collective-permute-done.9.uo
  38.4 1.4 %shard_map.69 = (f32[2,4,128,128]{3,2,1,0:T(8,128)S(1)}, f32[2,2,128,128]{3,2,1,0:T(8,128)S(1)}, f32[2,2,2,128,128]{4,3,2,1,0:T(8,128)S(1)}, f32[2,2,2,128,128]{...) custom-call(f32[8,128]{1,0:T(8,128)S(1)} %get-tuple-element.37.w.refs_0_, ...), custom_call_target="tpu_custom_call" | custom-call | flops 28200960 | bytes 5640192 | tf_op jit(solution)/shard_map/pallas_call | solution.py:22
  39.7 0.0 collective-permute-done.12.e
  39.7 0.0 collective-permute-done.13.o
  39.8 1.5 %shard_map.70 = f32[1,2,4,128,128]{4,3,2,1,0:T(8,128)} custom-call(f32[8,128]{1,0:T(8,128)S(1)} %get-tuple-element.37.w.refs_0_, f32[4,128,128]{2,1,0:T(8,128)S(1)} %get-tuple-element.54.coef, f32[2,4,128,128]{3,2,1,0:T(8,128)S(1)} %get-tuple-element.64.four, f32[2,2,128,128]{3,2,1,0:T(8,128)S(1)} %get-tuple-element.65.five, ...), custom_call_target="tpu_custom_call" | custom-call | flops 17059840 | bytes 3411968 | tf_op jit(solution)/shard_map/pallas_call | solution.py:22
  (2 shorter events, 0.1 us)
Async XLA Ops:
  2.7 9.2 %collective-permute-start = (f32[4,128,128]{2,1,0:T(8,128)S(1)}, f32[4,128,128]{2,1,0:T(8,128)S(1)}, u32[]{:S(2)}, u32[]{:S(2)}) collective-permute-start(f32[4,128,128]{2,1,0:T(8,128)S(1)} %get-tuple-element.44), channel_id=1, source_target_pairs={{0,1},{1,0},{2,3},{3,2},{4,5},{5,4},{6,7},{7,6},{8,9},{9,8},{10,11... | collective-permute-start | bytes 786440 | tf_op jit(solution)/shard_map/ppermute | solution.py:521
  4.4 9.2 %collective-permute-start.1 = (f32[4,128,128]{2,1,0:T(8,128)S(1)}, f32[4,128,128]{2,1,0:T(8,128)S(1)}, u32[]{:S(2)}, u32[]{:S(2)}) collective-permute-start(f32[4,128,128]{2,1,0:T(8,128)S(1)} %get-tuple-element.45), channel_id=1, source_target_pairs={{0,4},{1,2},{2,1},{3,7},{4,0},{5,6},{6,5},{7,3},{8,12},{9,10},{10,... | collective-permute-start | bytes 786440 | tf_op jit(solution)/shard_map/ppermute | solution.py:521
  4.9 10.8 %collective-permute-start.2 = (f32[3,128,128]{2,1,0:T(8,128)S(1)}, f32[3,128,128]{2,1,0:T(8,128)S(1)}, u32[]{:S(2)}, u32[]{:S(2)}) collective-permute-start(f32[3,128,128]{2,1,0:T(8,128)S(1)} %get-tuple-element.51), channel_id=1, source_target_pairs={{0,1},{1,0},{2,3},{3,2},{4,5},{5,4},{6,7},{7,6},{8,9},{9,8},{10,11... | collective-permute-start | bytes 589832 | tf_op jit(solution)/shard_map/ppermute | solution.py:521
  5.4 11.0 %collective-permute-start.3 = (f32[3,128,128]{2,1,0:T(8,128)S(1)}, f32[3,128,128]{2,1,0:T(8,128)S(1)}, u32[]{:S(2)}, u32[]{:S(2)}) collective-permute-start(f32[3,128,128]{2,1,0:T(8,128)S(1)} %get-tuple-element.52), channel_id=1, source_target_pairs={{0,4},{1,2},{2,1},{3,7},{4,0},{5,6},{6,5},{7,3},{8,12},{9,10},{10,... | collective-permute-start | bytes 589832 | tf_op jit(solution)/shard_map/ppermute | solution.py:521
  14.1 7.9 %collective-permute-start.4 = (f32[264,128]{1,0:T(8,128)S(1)}, f32[264,128]{1,0:T(8,128)S(1)}, u32[]{:S(2)}, u32[]{:S(2)}) collective-permute-start(f32[264,128]{1,0:T(8,128)S(1)} %get-tuple-element.46.acc1), channel_id=1, source_target_pairs={{0,8},{4,12},{8,0},{12,4},{1,9},{5,13},{9,1},{13,5},{2,10},{6,14},... | collective-permute-start | bytes 405512 | tf_op jit(solution)/shard_map/ppermute | solution.py:530
  16.7 5.3 %collective-permute-start.5 = (f32[256,128]{1,0:T(8,128)S(1)}, f32[256,128]{1,0:T(8,128)S(1)}, u32[]{:S(2)}, u32[]{:S(2)}) collective-permute-start(f32[256,128]{1,0:T(8,128)S(1)} %get-tuple-element.53.acc2), channel_id=1, source_target_pairs={{0,8},{4,12},{8,0},{12,4},{1,9},{5,13},{9,1},{13,5},{2,10},{6,14},... | collective-permute-start | bytes 393224 | tf_op jit(solution)/shard_map/ppermute | solution.py:530
  22.0 5.5 %collective-permute-start.6 = (f32[2,4,128,128]{3,2,1,0:T(8,128)S(1)}, f32[2,4,128,128]{3,2,1,0:T(8,128)S(1)}, u32[]{:S(2)}, u32[]{:S(2)}) collective-permute-start(f32[2,4,128,128]{3,2,1,0:T(8,128)S(1)} %shard_map.63.refs_1_.refs_0_), channel_id=1, source_target_pairs={{0,4},{4,0},{8,12},{12,8},{1,5},{5,1},{9,13},{13,9},{2,6},{6,2},{1... | collective-permute-start | bytes 1572872 | tf_op jit(solution)/shard_map/ppermute | solution.py:530
  22.1 2.9 %collective-permute-start.7 = (f32[2,128,128]{2,1,0:T(8,128)S(1)}, f32[2,128,128]{2,1,0:T(8,128)S(1)}, u32[]{:S(2)}, u32[]{:S(2)}) collective-permute-start(f32[2,128,128]{2,1,0:T(8,128)S(1)} %shard_map.64), channel_id=1, source_target_pairs={{0,4},{4,0},{8,12},{12,8},{1,5},{5,1},{9,13},{13,9},{2,6},{6,2},{1... | collective-permute-start | bytes 393224 | tf_op jit(solution)/shard_map/ppermute | solution.py:530
  22.9 7.8 %collective-permute-start.10 = (f32[3,128,128]{2,1,0:T(8,128)S(1)}, f32[3,128,128]{2,1,0:T(8,128)S(1)}, u32[]{:S(2)}, u32[]{:S(2)}) collective-permute-start(f32[3,128,128]{2,1,0:T(8,128)S(1)} %get-tuple-element.62), channel_id=1, source_target_pairs={{0,1},{1,0},{2,3},{3,2},{4,5},{5,4},{6,7},{7,6},{8,9},{9,8},{10,11... | collective-permute-start | bytes 589832 | tf_op jit(solution)/shard_map/ppermute | solution.py:521
  23.0 15.4 %collective-permute-start.8 = (f32[4,128,128]{2,1,0:T(8,128)S(1)}, f32[4,128,128]{2,1,0:T(8,128)S(1)}, u32[]{:S(2)}, u32[]{:S(2)}) collective-permute-start(f32[4,128,128]{2,1,0:T(8,128)S(1)} %get-tuple-element.60), channel_id=1, source_target_pairs={{0,1},{1,0},{2,3},{3,2},{4,5},{5,4},{6,7},{7,6},{8,9},{9,8},{10,11... | collective-permute-start | bytes 786440 | tf_op jit(solution)/shard_map/ppermute | solution.py:521
  25.1 13.3 %collective-permute-start.9 = (f32[4,128,128]{2,1,0:T(8,128)S(1)}, f32[4,128,128]{2,1,0:T(8,128)S(1)}, u32[]{:S(2)}, u32[]{:S(2)}) collective-permute-start(f32[4,128,128]{2,1,0:T(8,128)S(1)} %get-tuple-element.61), channel_id=1, source_target_pairs={{0,4},{1,2},{2,1},{3,7},{4,0},{5,6},{6,5},{7,3},{8,12},{9,10},{10,... | collective-permute-start | bytes 786440 | tf_op jit(solution)/shard_map/ppermute | solution.py:521
  25.1 13.3 %collective-permute-start.11 = (f32[3,128,128]{2,1,0:T(8,128)S(1)}, f32[3,128,128]{2,1,0:T(8,128)S(1)}, u32[]{:S(2)}, u32[]{:S(2)}) collective-permute-start(f32[3,128,128]{2,1,0:T(8,128)S(1)} %get-tuple-element.63), channel_id=1, source_target_pairs={{0,4},{1,2},{2,1},{3,7},{4,0},{5,6},{6,5},{7,3},{8,12},{9,10},{10,... | collective-permute-start | bytes 589832 | tf_op jit(solution)/shard_map/ppermute | solution.py:521
  27.7 12.0 %collective-permute-start.12 = (f32[2,128,128]{2,1,0:T(8,128)S(1)}, f32[2,128,128]{2,1,0:T(8,128)S(1)}, u32[]{:S(2)}, u32[]{:S(2)}) collective-permute-start(f32[2,128,128]{2,1,0:T(8,128)S(1)} %get-tuple-element.70), channel_id=1, source_target_pairs={{0,1},{1,0},{2,3},{3,2},{4,5},{5,4},{6,7},{7,6},{8,9},{9,8},{10,11... | collective-permute-start | bytes 393224 | tf_op jit(solution)/shard_map/ppermute | solution.py:521
  30.7 9.1 %collective-permute-start.13 = (f32[2,128,128]{2,1,0:T(8,128)S(1)}, f32[2,128,128]{2,1,0:T(8,128)S(1)}, u32[]{:S(2)}, u32[]{:S(2)}) collective-permute-start(f32[2,128,128]{2,1,0:T(8,128)S(1)} %get-tuple-element.71), channel_id=1, source_target_pairs={{0,4},{1,2},{2,1},{3,7},{4,0},{5,6},{6,5},{7,3},{8,12},{9,10},{10,... | collective-permute-start | bytes 393224 | tf_op jit(solution)/shard_map/ppermute | solution.py:521

commit v6 on v5

--- a/solution.py
+++ b/solution.py
@@ -108,6 +108,16 @@
     def coefficient(self, v, c):
         return self.a * speed_gain * v**2 + (1.0 - self.a) * diffuse_gain / c
 
+    def models_beside(self, even_ref, odd_ref, other, r):
+        mine = self.unpack(even_ref, odd_ref, 0, r)
+        theirs = self.unpack(other.at[0:1], other.at[1:2], 0, r)
+        out = []
+        for s in range(2):
+            vel = jnp.where(self.first_core, mine[s], theirs[s])
+            con = jnp.where(self.first_core, theirs[s], mine[s])
+            out.append((jnp.where(self.has[s], vel, 1.0), jnp.where(self.has[s], con, 1.0)))
+        return out
+
     def pack(self, even_ref, odd_ref, lows, highs):
         for k, (low, high) in enumerate(zip(lows, highs)):
             for r in self.blocks():
@@ -125,37 +135,45 @@
     return (make(i - 1) if i > 0 else ends[0]), (make(i + 1) if i < tile - 1 else ends[1])
 
 
-def lead_kernel(label, f_in, v_in, c_in, ae, ao, coef, w, f, v, c, one, sems):
-    parts = [(v_in, v), (c_in, c)] + [(f_in.at[0, n], f.at[0, n]) for n in (0, 1, 2, 3)]
+def fetch_kernel(f_in, v_in, c_in, even, odd, f, v, c, sems):
+    parts = [(v_in, v), (c_in, c)] + [(f_in.at[0, n], f.at[0, n]) for n in range(4)]
     copies = [pltpu.make_async_copy(src, dst, sems.at[n]) for n, (src, dst) in enumerate(parts)]
     for copy in copies:
         copy.start()
     tile, ny, nz = v.shape
+    k = Work(None, ny, nz)
+    edge = (0, tile - 1)
+    for copy in copies[:3]:
+        copy.wait()
+    for r in k.blocks():
+        lo, hi = (
+            jnp.where(k.first_core, v[i, r:r + k.n], c[i, r:r + k.n]) for i in edge
+        )
+        k.put(Plane(even, 0), r, jnp.where(k.even, hi, lo))
+        k.put(Plane(odd, 0), r, jnp.where(k.even, lo, hi))
+    k.pack(even.at[1:], odd.at[1:], *([Plane(f, 0, 0, i)] for i in edge))
+    for copy in copies[3:]:
+        copy.wait()
+
+
+def lead_kernel(label, f, v, c, even, odd, coef, w, one):
+    tile, ny, nz = v.shape
     w[...] = jnp.full(w.shape, label[0].astype(F32), F32)
     k = Work(w, ny, nz)
     edge = (0, tile - 1)
-    copies[0].wait()
-    copies[1].wait()
     for i in range(tile):
         for r in k.blocks():
             k.put(Plane(coef, i), r, k.coefficient(v[i, r:r + k.n], c[i, r:r + k.n]))
-    copies[2].wait()
-    copies[3].wait()
     for s, i in enumerate(edge):
         k.step(
             Plane(one, s), Plane(f, 0, 0, i), Plane(f, 0, 1, i), Plane(coef, i),
             *near(lambda j: Plane(f, 0, 0, j), i, tile),
         )
-    copies[4].wait()
-    k.pack(ae, ao, *(
-        [Plane(coef, i), Plane(f, 0, 0, i), Plane(f, 0, 2, i), Plane(one, s)]
-        for s, i in enumerate(edge)
-    ))
-    copies[5].wait()
-
-
-def isolated_kernel(w, f, v, c, coef, be, bo, one, acc, two):
-    tile, ny, nz = v.shape
+    k.pack(even, odd, *([Plane(f, 0, 2, i), Plane(one, s)] for s, i in enumerate(edge)))
+
+
+def isolated_kernel(w, f, coef, be, bo, one, acc, two):
+    tile, ny, nz = coef.shape
     k = Work(w, ny, nz)
     edge = (0, tile - 1)
     for n in range(2):
@@ -174,22 +192,19 @@
             *near(lambda j: Plane(one, 0, j), i, tile),
         )
     k.pack(be, bo, *([Plane(two, s), Plane(one, 1, i)] for s, i in enumerate(edge)))
+
+
+def inner_kernel(
+    w, f, coef, one, acc, ae, ao, de, do, other, acc1, rim, ends, two, three, halo, zero,
+):
+    tile, ny, nz = coef.shape
+    k = Work(w, ny, nz)
+    edge = (0, tile - 1)
     for r in k.blocks():
-        lo, hi = (
-            jnp.where(k.first_core, v[i, r:r + k.n], c[i, r:r + k.n]) for i in edge
-        )
-        k.put(Plane(be, 2), r, jnp.where(k.even, hi, lo))
-        k.put(Plane(bo, 2), r, jnp.where(k.even, lo, hi))
-
-
-def inner_kernel(w, f, coef, one, acc, ae, ao, acc1, rim, ends, two, three, halo, zero):
-    tile, ny, nz = coef.shape
-    k = Work(w, ny, nz)
-    edge = (0, tile - 1)
-    for r in k.blocks():
-        parts = [k.unpack(ae, ao, m, r) for m in range(4)]
+        models = k.models_beside(ae, ao, other, r)
+        parts = [k.unpack(ae, ao, 1, r)] + [k.unpack(de, do, m, r) for m in range(2)]
         for s, i in enumerate(edge):
-            h = [p[s] for p in parts]
+            h = [jnp.where(k.has[s], k.coefficient(*models[s]), 0.0)] + [p[s] for p in parts]
             cf, w0, u0 = coef[i, r:r + k.n], f[0, 2, i, r:r + k.n], f[0, 0, i, r:r + k.n]
             k.put(Plane(halo, s, 0), r, h[0])
             k.put(Plane(halo, s, 1), r, h[3] + h[0] * u0)
@@ -307,11 +322,11 @@
     k.pack(pe, po, planes(0, 1, 2), planes(1, tile - 2, tile - 3))
 
 
-def pick_kernel(be, bo, out):
-    out[0], out[1] = be[2], bo[2]
-
-
-def penalty_kernel(v, c, be, bo, other, pen, logs, rims):
+def pick_kernel(even, odd, out):
+    out[0], out[1] = even[0], odd[0]
+
+
+def penalty_kernel(v, c, ae, ao, other, pen, logs, rims):
     tile, ny, nz = v.shape
     k = Work(None, ny, nz)
     edge = (0, tile - 1)
@@ -319,12 +334,9 @@
         for r in k.blocks():
             k.put(Plane(logs, i + 1), r, jnp.log(c[i, r:r + k.n]))
     for r in k.blocks():
-        mine = k.unpack(be, bo, 2, r)
-        theirs = k.unpack(other.at[0:1], other.at[1:2], 0, r)
+        models = k.models_beside(ae, ao, other, r)
         for s, i in enumerate(edge):
-            vel = jnp.where(k.first_core, mine[s], theirs[s])
-            con = jnp.where(k.first_core, theirs[s], mine[s])
-            con = jnp.where(k.has[s], con, 1.0)
+            vel, con = models[s]
             k.put(Plane(rims, s), r, jnp.where(k.has[s], vel, v[i, r:r + k.n]))
             k.put(
                 Plane(logs, (0, tile + 1)[s]), r,
@@ -345,30 +357,37 @@
             k.put(Plane(pen, i), r, penalty_gain * (ca * ca + cb * cb + cc * cc))
 
 
-def weigh_kernel(acc1, acc2, far1, far2, out):
-    _, tile, ny, nz = out.shape
+def weigh_kernel(labels, far_labels, mine, other, out):
+    _, planes, ny, nz = out.shape
     k = Work(None, ny, nz)
-    rows = (tile - 2) * ny
-    labels = [jnp.broadcast_to(ref[rows:rows + 1], (k.n, nz)) for ref in (acc1, far1)]
-    for i in range(tile):
-        for r in k.blocks():
-            if i in (0, tile - 1):
-                at = (0 if i == 0 else ny) + r
-                mine, other = acc2[at:at + k.n], far2[at:at + k.n]
-            else:
-                at = (i - 1) * ny + r
-                mine, other = acc1[at:at + k.n], far1[at:at + k.n]
-            k.put(Plane(out, 0, i), r, labels[0] * mine + labels[1] * other)
-            k.put(Plane(out, 1, i), r, (1.0 - labels[0]) * mine + (1.0 - labels[1]) * other)
-
-
-def renew(scale, value, part, rest, pen):
-    return value * jnp.exp(-step_size * jnp.tanh(scale * (part + rest) + pen))
-
-
-def renew_kernel(scale, w, part, rest, pen, v, c, coef, e, o):
+    last = labels.shape[0] - 8
+    one, two = (jnp.broadcast_to(ref[last:last + 1], (k.n, nz)) for ref in (labels, far_labels))
+    for i in range(planes):
+        for r in k.blocks():
+            at = slice(i * ny + r, i * ny + r + k.n)
+            k.put(Plane(out, 0, i), r, one * mine[at] + two * other[at])
+            k.put(Plane(out, 1, i), r, (1.0 - one) * mine[at] + (1.0 - two) * other[at])
+
+
+def renew(scale, value, gradient, pen):
+    return value * jnp.exp(-step_size * jnp.tanh(scale * gradient + pen))
+
+
+class Sums:
+    def __init__(self, part, rest, part_edge, rest_edge):
+        self.inner, self.edge = (part, rest), (part_edge, rest_edge)
+        self.tile = part.shape[1] + 2
+
+    def get(self, n, i, at):
+        edges = (0, self.tile - 1)
+        pair, j = (self.edge, edges.index(i)) if i in edges else (self.inner, i - 1)
+        return pair[0][n, j, at] + pair[1][n, j, at]
+
+
+def renew_kernel(scale, w, part, rest, part_edge, rest_edge, pen, v, c, coef, e, o):
     tile, ny, nz = v.shape
     k = Work(w, ny, nz)
+    sums = Sums(part, rest, part_edge, rest_edge)
     sound = k.a == 1.0
     for i in range(tile):
         for r in k.blocks():
@@ -376,8 +395,7 @@
             new = renew(
                 scale,
                 jnp.where(sound, v[i, at], c[i, at]),
-                jnp.where(sound, part[0, i, at], part[1, i, at]),
-                jnp.where(sound, rest[0, i, at], rest[1, i, at]),
+                jnp.where(sound, sums.get(0, i, at), sums.get(1, i, at)),
                 pen[i, at],
             )
             k.put(
@@ -387,19 +405,20 @@
     k.pack(e, o, [Plane(coef, 0), Plane(coef, 1)], [Plane(coef, tile - 2), Plane(coef, tile - 1)])
 
 
-def models_kernel(scale, part, rest, pen, v, c, out):
+def models_kernel(scale, part, rest, part_edge, rest_edge, pen, v, c, out):
     tile, ny, nz = v.shape
     k = Work(None, ny, nz)
+    sums = Sums(part, rest, part_edge, rest_edge)
     for n, ref in enumerate((v, c)):
         for i in range(tile):
             for r in k.blocks():
                 at = slice(r, r + k.n)
-                out[n, i, at] = renew(scale, ref[i, at], part[n, i, at], rest[n, i, at], pen[i, at])
+                out[n, i, at] = renew(scale, ref[i, at], sums.get(n, i, at), pen[i, at])
 
 
 def before_kernel(
     w, coef, old, ends, two, wtwo, three, uthree, winner, halo, beyond, ue, uo, we, wo,
-    four, five, ring, lap, side, wthree, wide, prev, last,
+    rim, six, ring, lap, side, wide, prev, last, wthree, four, five,
 ):
     tile, ny, nz = coef.shape
     k = Work(w, ny, nz)
@@ -445,7 +464,7 @@
 
         for i in range(tile):
             k.step(
-                Plane(four, n, i), Plane(wide, i + 3), second(i), Plane(coef, i),
+                Plane(four, i), Plane(wide, i + 3), second(i), Plane(coef, i),
                 Plane(wide, i + 2), Plane(wide, i + 4),
             )
         for s in range(2):
@@ -456,54 +475,62 @@
                     value, total = k.lap(Plane(wide, j + 3), Plane(wide, j + 2), Plane(wide, j + 4), r)
                     k.put(Plane(ring, n, s, m), r, k.ahead(value, k.get(earlier, r)))
                     k.put(Plane(lap, n, s, m), r, total)
-        for i in range(1, tile - 1):
-            k.step(
-                Plane(five, n, i - 1), Plane(four, n, i), third_plane(i), Plane(coef, i),
-                Plane(four, n, i - 1), Plane(four, n, i + 1),
-            )
-
-
-def after_kernel(
-    w, coef, four, five, ring, lap, side, uthree, wthree, e, o,
-    out, cn, far, ends, res, sems,
-):
-    tile, ny, nz = coef.shape
-    k = Work(w, ny, nz)
-    edge = (0, tile - 1)
-    for r in k.blocks():
-        parts = [k.unpack(e, o, m, r) for m in range(2)]
-        for s in range(2):
-            order = (0, 1) if s == 0 else (1, 0)
-            for m in range(2):
-                k.put(Plane(cn, s, m), r, parts[order[m]][s])
-    copies = []
-    for n in range(2):
-        for s in range(2):
-            for m in range(2):
-                for r in k.blocks():
-                    at = slice(r, r + k.n)
-                    far[s, m, at] = ring[n, s, m, at] + cn[s, m, at] * lap[n, s, m, at]
-        for s, i in enumerate(edge):
-            k.step(
-                Plane(ends, s, 0), Plane(far, s, 1), Plane(side, n, s), Plane(cn, s, 1),
-                Plane(far, s, 0), Plane(four, n, i),
-            )
-            k.step(
-                Plane(ends, s, 1), Plane(four, n, i), Plane(wthree if n else uthree, s),
-                Plane(coef, i),
-                *near(lambda j: Plane(four, n, j), i, tile, (Plane(far, 0, 1), Plane(far, 1, 1))),
-            )
-
-        def fifth(i):
-            return Plane(ends, edge.index(i), 1) if i in edge else Plane(five, n, i - 1)
-
         for i in range(tile):
             k.step(
-                Plane(res, n, i), fifth(i), Plane(four, n, i), Plane(coef, i),
-                *near(fifth, i, tile, (Plane(ends, 0, 0), Plane(ends, 1, 0))),
-            )
-            copies.append(pltpu.make_async_copy(res.at[n, i], out.at[0, n, i], sems.at[n, i]))
-            copies[-1].start()
+                Plane(five, i), Plane(four, i), third_plane(i), Plane(coef, i),
+                *near(lambda j: Plane(four, j), i, tile),
+            )
+        for i in range(tile):
+            k.step(
+                Plane(six, n, i), Plane(five, i), Plane(four, i), Plane(coef, i),
+                *near(lambda j: Plane(five, j), i, tile),
+            )
+        for s, i in enumerate(edge):
+            for r in k.blocks():
+                k.put(Plane(rim, n, s), r, k.get(Plane(four, i), r))
+
+
+def after_kernel(w, coef, rim, six, ring, lap, side, e, o, out, res, close, away, d, h5, sems):
+    _, tile, ny, nz = six.shape
+    k = Work(w, ny, nz)
+    edge, next_to = (0, tile - 1), (1, tile - 2)
+    copies = []
+
+    def send(n, i):
+        copies.append(pltpu.make_async_copy(res.at[n, i], out.at[0, n, i], sems.at[n, i]))
+        copies[-1].start()
+
+    for n in range(2):
+        for i in range(2, tile - 2):
+            for r in k.blocks():
+                k.put(Plane(res, n, i), r, k.get(Plane(six, n, i), r))
+            send(n, i)
+        for s, i in enumerate(edge):
+            for r in k.blocks():
+                at = slice(r, r + k.n)
+                outer, inner = (k.unpack(e, o, (m, 1 - m)[s], r)[s] for m in range(2))
+                near_plane = ring[n, s, 1, at] + inner * lap[n, s, 1, at]
+                close[n, s, at] = near_plane
+                away[n, s, at] = (
+                    k.ahead(near_plane, side[n, s, at])
+                    + inner * (ring[n, s, 0, at] + outer * lap[n, s, 0, at] + rim[n, s, at])
+                )
+                h5[n, s, at] = inner
+                delta = coef[i, at] * near_plane
+                d[n, s, at] = delta
+                j = next_to[s]
+                res[n, j, at] = six[n, j, at] + coef[j, at] * delta
+            send(n, next_to[s])
+        for s, i in enumerate(edge):
+            for r in k.blocks():
+                at = slice(r, r + k.n)
+                _, total = k.flat(Plane(close, n, s), r)
+                fifth = away[n, s, at] + h5[n, s, at] * total
+                delta, total = k.flat(Plane(d, n, s), r)
+                res[n, i, at] = (
+                    six[n, i, at] + (1.0 + k.a) * delta + coef[i, at] * (total + fifth)
+                )
+            send(n, i)
     for copy in copies:
         copy.wait()
 
@@ -539,30 +566,37 @@
     def planes(*lead):
         return (*lead, ny, nz)
 
-    ae, ao, coef, w, fields, velocity, conductivity = call(
+    ae, ao, fields, velocity, conductivity = call(
+        fetch_kernel,
+        [planes(2)] * 2 + [fields.shape, velocity.shape, conductivity.shape],
+        tuple(pltpu.with_memory_space_constraint(x, pltpu.HBM) for x in (fields, velocity, conductivity)),
+        (),
+        [pl.BlockSpec(memory_space=pltpu.HBM)] * 3,
+        [pltpu.SemaphoreType.DMA((6,))],
+    )
+    ae, ao = swap_pairs(ae, ao)
+    de, do, coef, w = call(
         lead_kernel,
-        [planes(4)] * 2 + [planes(tile), (8, nz), fields.shape, velocity.shape, conductivity.shape],
-        (
-            labels,
-            *(pltpu.with_memory_space_constraint(x, pltpu.HBM) for x in (fields, velocity, conductivity)),
-        ),
+        [planes(2)] * 2 + [planes(tile), (8, nz)],
+        (labels, fields, velocity, conductivity),
         [planes(2)],
-        [pl.BlockSpec(memory_space=pltpu.SMEM)] + [pl.BlockSpec(memory_space=pltpu.HBM)] * 3,
-        [pltpu.SemaphoreType.DMA((6,))],
-    )
-    ae, ao = swap_pairs(ae, ao)
+        [pl.BlockSpec(memory_space=pltpu.SMEM)] + [VMEM] * 3,
+    )
+    de, do = swap_pairs(de, do)
     be, bo, one, acc = call(
         isolated_kernel,
-        [planes(3), planes(3), planes(2, tile), planes(tile)],
-        (w, fields, velocity, conductivity, coef),
+        [planes(2)] * 2 + [planes(2, tile), planes(tile)],
+        (w, fields, coef),
         [planes(2)],
     )
     be, bo = swap_pairs(be, bo)
+    (other,) = call(pick_kernel, [planes(2)], (ae, ao))
+    other = across(other, 1)
 
     acc1, rim, ends, two, three, halo = call(
         inner_kernel,
         [((tile - 2) * ny + 8, nz), planes(2), planes(2, 2), planes(2, tile), planes(tile), planes(2, 2)],
-        (w, fields, coef, one, acc, ae, ao),
+        (w, fields, coef, one, acc, ae, ao, de, do, other),
         [planes(2)],
     )
     masks = [1 << k for k in reversed(range(groups.bit_length() - 1))]
@@ -580,40 +614,41 @@
         early_w_kernel, [planes(3), planes(3), planes(tile - 2)], (w, coef, one, two, wtwo)
     )
     we, wo = swap_pairs(we, wo)
-    (other,) = call(pick_kernel, [planes(2)], (be, bo))
-    other = across(other, 1)
-
-    (part,) = call(weigh_kernel, [planes(2, tile)], (acc1, acc2, far1, far2))
-    for mask in masks[1:-1]:
-        part = part + across(part, mask)
-    rest = across(part, masks[-1])
     (pen,) = call(
         penalty_kernel,
         [planes(tile)],
-        (velocity, conductivity, be, bo, other),
+        (velocity, conductivity, ae, ao, other),
         [planes(tile + 2), planes(2)],
     )
+
+    sums = []
+    for mine, far in ((acc1, far1), (acc2, far2)):
+        rows = mine.shape[0] // ny
+        (part,) = call(weigh_kernel, [planes(2, rows)], (acc1, far1, mine, far))
+        for mask in masks[1:-1]:
+            part = part + across(part, mask)
+        sums += [part, across(part, masks[-1])]
     coef_next, e, o = call(
         lambda *refs: renew_kernel(scale, *refs),
         [planes(tile), planes(2), planes(2)],
-        (w, part, rest, pen, velocity, conductivity),
+        (w, *sums, pen, velocity, conductivity),
     )
     e, o = swap_pairs(e, o)
     (models,) = call(
         lambda *refs: models_kernel(scale, *refs),
-        [planes(2, tile)], (part, rest, pen, velocity, conductivity),
-    )
-    four, five, ring, lap, side, wthree = call(
+        [planes(2, tile)], (*sums, pen, velocity, conductivity),
+    )
+    rim, six, ring, lap, side = call(
         before_kernel,
-        [planes(2, tile), planes(2, tile - 2), planes(2, 2, 2), planes(2, 2, 2), planes(2, 2), planes(2)],
+        [planes(2, 2), planes(2, tile), planes(2, 2, 2), planes(2, 2, 2), planes(2, 2)],
         (w, coef_next, coef, ends, two, wtwo, three, uthree, winner, halo, beyond, ue, uo, we, wo),
-        [planes(tile + 6), planes(2), planes(2)],
+        [planes(tile + 6), planes(2), planes(2), planes(2), planes(tile), planes(tile)],
     )
     (final,) = call(
         after_kernel,
         [planes(1, 2, tile)],
-        (w, coef_next, four, five, ring, lap, side, uthree, wthree, e, o),
-        [planes(2, 2), planes(2, 2), planes(2, 2), planes(2, tile)],
+        (w, coef_next, rim, six, ring, lap, side, e, o),
+        [planes(2, tile), planes(2, 2), planes(2, 2), planes(2, 2), planes(2, 2)],
         None,
         [pltpu.SemaphoreType.DMA((2, tile))],
         pl.BlockSpec(memory_space=pltpu.HBM),

time: 41.4 us -> 40.5 us (0.978)
  the two profiles are of different devices: /device:TPU:16 before, /device:TPU:0 now
where the time goes in v6:
time: 40.5 us; the launch traced here: 40 us
  starting transfers between devices  18.9 us (47%)
  waiting for transfers between devices  11.8 us (29%)
  Pallas kernels  7.86 us (19%)
  between operations  1.4 us (3%)
    ppermute x12, starting transfers between devices, swap(): return lax.ppermute(block, ('src', 'space'), pairs)  15.1 us
    ppermute x12, waiting for transfers between devices, swap(): return lax.ppermute(block, ('src', 'space'), pairs)  8.1 us
    pallas_call x15, Pallas kernels, call(): pl.pallas_call(kernel, out_shape=tuple((jax.ShapeDtypeStruct(o, F32) for...  7.86 us
    ppermute x5, starting transfers between devices, across(): return lax.ppermute(block, 'src', [(i, i ^ mask) for i in range(count)])  3.82 us
    ppermute x5, waiting for transfers between devices, across(): return lax.ppermute(block, 'src', [(i, i ^ mask) for i in range(count)])  3.72 us
  transfers between devices with their start and end apart: 17, of which 6 were waited for; matrix products, arithmetic and copies ran while one was open for 0% of the time, Pallas kernels for 13%

profile of v6, /device:TPU:0, one launch (start us, length us, event | category | flops | bytes accessed | tf_op | source)
XLA Modules:
  0.0 40.0 jit_solution(14599533578696403102)
XLA Ops:
  0.6 1.4 %shard_map.59 = (f32[2,128,128]{2,1,0:T(8,128)S(1)}, f32[2,128,128]{2,1,0:T(8,128)S(1)}, f32[1,4,4,128,128]{4,3,2,1,0:T(8,128)S(1)}, f32[4,128,128]{2,1,0:T(8,128)S(1)}, f32[4,128,128]{2,1,0:T(8,128)S(1)}) custom-call(f32[1,4,4,128,128]{4,3,2,1,0:T(8,128)} %f_in.1, f32[4,128,128]{2,1,0:T(8,128)} %v_in.1, f32[4,128,128]{2,1,0:T(8,128)} %c_in.1), custom_call_target="tpu_custom_call" | custom-call | flops 17039360 | bytes 3407872 | tf_op jit(solution)/shard_map/pallas_call | solution.py:22
  2.0 3.1 %collective-permute-start = (f32[2,128,128]{2,1,0:T(8,128)S(1)}, f32[2,128,128]{2,1,0:T(8,128)S(1)}, u32[]{:S(2)}, u32[]{:S(2)}) collective-permute-start(f32[2,128,128]{2,1,0:T(8,128)S(1)} %get-tuple-element.45), channel_id=1, source_target_pairs={{0,1},{1,0},{2,3},{3,2},{4,5},{5,4},{6,7},{7,6},{8,9},{9,8},{10,11... | collective-permute-start | bytes 393224 | tf_op jit(solution)/shard_map/ppermute | solution.py:548
  5.2 0.0 collective-permute-start.1
  5.8 0.2 shard_map.60
  6.0 3.2 %collective-permute-start.2 = (f32[2,128,128]{2,1,0:T(8,128)S(1)}, f32[2,128,128]{2,1,0:T(8,128)S(1)}, u32[]{:S(2)}, u32[]{:S(2)}) collective-permute-start(f32[2,128,128]{2,1,0:T(8,128)S(1)} %get-tuple-element.47), channel_id=1, source_target_pairs={{0,1},{1,0},{2,3},{3,2},{4,5},{5,4},{6,7},{7,6},{8,9},{9,8},{10,11... | collective-permute-start | bytes 393224 | tf_op jit(solution)/shard_map/ppermute | solution.py:548
  9.2 0.0 collective-permute-start.3
  9.2 0.0 collective-permute-done.even.ae
  9.2 0.0 collective-permute-done.1.odd.ao
  9.2 0.6 %collective-permute-start.4 = (f32[2,128,128]{2,1,0:T(8,128)S(1)}, f32[2,128,128]{2,1,0:T(8,128)S(1)}, u32[]{:S(2)}, u32[]{:S(2)}) collective-permute-start(f32[2,128,128]{2,1,0:T(8,128)S(1)} %shard_map.62), channel_id=1, source_target_pairs={{0,4},{4,0},{8,12},{12,8},{1,5},{5,1},{9,13},{13,9},{2,6},{6,2},{1... | collective-permute-start | bytes 393224 | tf_op jit(solution)/shard_map/ppermute | solution.py:557
  9.8 0.5 %shard_map.61 = (f32[2,128,128]{2,1,0:T(8,128)S(1)}, f32[2,128,128]{2,1,0:T(8,128)S(1)}, f32[2,4,128,128]{3,2,1,0:T(8,128)S(1)}, f32[4,128,128]{2,1,0:T(8,128)S(1)}) custom-call(f32[8,128]{1,0:T(8,128)S(1)} %get-tuple-element.41.w.refs_0_, f32[1,4,4,128,128]{4,3,2,1,0:T(8,128)S(1)} %get-tuple-element.38.f, f32[4,128,128]{2,1,0:T(8,128)S(1)} %get-tuple-element.42.coef.old), custom_call_target="tpu_custom_call" | custom-call | flops 11816960 | bytes 2363392 | tf_op jit(solution)/shard_map/pallas_call | solution.py:22
  10.3 2.2 %collective-permute-start.7 = (f32[2,128,128]{2,1,0:T(8,128)S(1)}, f32[2,128,128]{2,1,0:T(8,128)S(1)}, u32[]{:S(2)}, u32[]{:S(2)}) collective-permute-start(f32[2,128,128]{2,1,0:T(8,128)S(1)} %get-tuple-element.54), channel_id=1, source_target_pairs={{0,1},{1,0},{2,3},{3,2},{4,5},{5,4},{6,7},{7,6},{8,9},{9,8},{10,11... | collective-permute-start | bytes 393224 | tf_op jit(solution)/shard_map/ppermute | solution.py:548
  12.5 0.2 collective-permute-start.8
  12.7 0.0 collective-permute-done.2.de
  12.7 0.0 collective-permute-done.3.do
  12.7 0.0 collective-permute-done.4.other
  12.8 0.6 %shard_map.63 = (f32[264,128]{1,0:T(8,128)S(1)}, f32[2,128,128]{2,1,0:T(8,128)S(1)}, f32[2,2,128,128]{3,2,1,0:T(8,128)S(1)}, f32[2,4,128,128]{3,2,1,0:T(8,128)S(...) custom-call(f32[8,128]{1,0:T(8,128)S(1)} %get-tuple-element.41.w.refs_0_, ...), custom_call_target="tpu_custom_call" | custom-call | flops 21667840 | bytes 4333568 | tf_op jit(solution)/shard_map/pallas_call | solution.py:22
  13.4 1.6 %collective-permute-start.5 = (f32[264,128]{1,0:T(8,128)S(1)}, f32[264,128]{1,0:T(8,128)S(1)}, u32[]{:S(2)}, u32[]{:S(2)}) collective-permute-start(f32[264,128]{1,0:T(8,128)S(1)} %get-tuple-element.49.labels.mine), channel_id=1, source_target_pairs={{0,8},{4,12},{8,0},{12,4},{1,9},{5,13},{9,1},{13,5},{2,10},{6,14},... | collective-permute-start | bytes 405512 | tf_op jit(solution)/shard_map/ppermute | solution.py:557
  14.9 1.8 %collective-permute-done.7.be = f32[2,128,128]{2,1,0:T(8,128)S(1)} collective-permute-done((f32[2,128,128]{2,1,0:T(8,128)S(1)}, f32[2,128,128]{2,1,0:T(8,128)S(1)}, u32[]{:S(2)}, u32[]{:S(2)}) %collective-permute-start.7) | collective-permute-done | bytes 131104 | tf_op jit(solution)/shard_map/ppermute | solution.py:548
  16.7 0.0 collective-permute-done.8.bo
  16.7 0.3 shard_map.65
  17.0 1.6 %collective-permute-start.9 = (f32[256,128]{1,0:T(8,128)S(1)}, f32[256,128]{1,0:T(8,128)S(1)}, u32[]{:S(2)}, u32[]{:S(2)}) collective-permute-start(f32[256,128]{1,0:T(8,128)S(1)} %get-tuple-element.56.mine), channel_id=1, source_target_pairs={{0,8},{4,12},{8,0},{12,4},{1,9},{5,13},{9,1},{13,5},{2,10},{6,14},... | collective-permute-start | bytes 393224 | tf_op jit(solution)/shard_map/ppermute | solution.py:557
  18.6 0.7 %collective-permute-done.5.far_labels.other = f32[264,128]{1,0:T(8,128)S(1)} collective-permute-done((f32[264,128]{1,0:T(8,128)S(1)}, f32[264,128]{1,0:T(8,128)S(1)}, u32[]{:S(2)}, u32[]{:S(2)}) %collective-permute-start.5) | collective-permute-done | bytes 135200 | tf_op jit(solution)/shard_map/ppermute | solution.py:557
  19.3 0.1 collective-permute-start.6
  19.3 3.1 %collective-permute-done.9.other = f32[256,128]{1,0:T(8,128)S(1)} collective-permute-done((f32[256,128]{1,0:T(8,128)S(1)}, f32[256,128]{1,0:T(8,128)S(1)}, u32[]{:S(2)}, u32[]{:S(2)}) %collective-permute-start.9) | collective-permute-done | bytes 131104 | tf_op jit(solution)/shard_map/ppermute | solution.py:557
  22.4 0.1 collective-permute-start.10
  22.5 0.2 shard_map.69
  22.7 2.1 %collective-permute-start.13 = (f32[3,128,128]{2,1,0:T(8,128)S(1)}, f32[3,128,128]{2,1,0:T(8,128)S(1)}, u32[]{:S(2)}, u32[]{:S(2)}) collective-permute-start(f32[3,128,128]{2,1,0:T(8,128)S(1)} %get-tuple-element.65), channel_id=1, source_target_pairs={{0,1},{1,0},{2,3},{3,2},{4,5},{5,4},{6,7},{7,6},{8,9},{9,8},{10,11... | collective-permute-start | bytes 589832 | tf_op jit(solution)/shard_map/ppermute | solution.py:548
  24.9 0.1 collective-permute-start.11
  24.9 0.3 collective-permute-start.12
  25.2 0.0 collective-permute-done.6.refs_2_.refs_1_
  25.2 0.3 collective-permute-start.14
  25.5 0.4 %shard_map.67.refs_5_.refs_4_ = f32[4,128,128]{2,1,0:T(8,128)S(1)} custom-call(f32[4,128,128]{2,1,0:T(8,128)S(1)} %get-tuple-element.39.v.refs_6_.refs_5_, f32[4,128,128]{2,1,0:T(8,128)S(1)} %get-tuple-element.40.c.refs_7_.refs_6_, f32[2,128,128]{2,1,0:T(8,128)S(1)} %collective-permute-done.even.ae, f32[2,128,128]{2,1,0:T(8,128)S(1)} %collective-permute-done.1.odd.ao, ...), custom_call_target="tpu_custom_call" | custom-call | flops 5898240 | bytes 1179648 | tf_op jit(solution)/shard_map/pallas_call | solution.py:22
  26.0 0.0 collective-permute-done.10.refs_4_.refs_3_
  26.0 0.2 shard_map.68
  26.1 3.5 %collective-permute-start.15 = (f32[2,128,128]{2,1,0:T(8,128)S(1)}, f32[2,128,128]{2,1,0:T(8,128)S(1)}, u32[]{:S(2)}, u32[]{:S(2)}) collective-permute-start(f32[2,128,128]{2,1,0:T(8,128)S(1)} %get-tuple-element.72), channel_id=1, source_target_pairs={{0,1},{1,0},{2,3},{3,2},{4,5},{5,4},{6,7},{7,6},{8,9},{9,8},{10,11... | collective-permute-start | bytes 393224 | tf_op jit(solution)/shard_map/ppermute | solution.py:548
  29.7 0.9 %collective-permute-done.13.we = f32[3,128,128]{2,1,0:T(8,128)S(1)} collective-permute-done((f32[3,128,128]{2,1,0:T(8,128)S(1)}, f32[3,128,128]{2,1,0:T(8,128)S(1)}, u32[]{:S(2)}, u32[]{:S(2)}) %collective-permute-start.13) | collective-permute-done | bytes 196640 | tf_op jit(solution)/shard_map/ppermute | solution.py:548
  30.6 0.0 collective-permute-start.16
  30.6 1.0 %shard_map.73 = f32[2,4,128,128]{3,2,1,0:T(8,128)} custom-call(f32[2,2,128,128]{3,2,1,0:T(8,128)S(1)} %shard_map.64.refs_1_.refs_0_, f32[2,2,128,128]{3,2,1,0:T(8,128)S(1)} %collective-permute-done.6.refs_2_.refs_1_, f32[2,2,128,128]{3,2,1,0:T(8,128)S(1)} %shard_map.66.refs_3_.refs_2_, f32[2,2,128,128]{3,2,1,0:T(8,128)S(1)} %collective-permute-done.10.refs_4_.refs_3_, ...), custom_call_target="tpu_custom_call" | custom-call | flops 11796480 | bytes 2359296 | tf_op jit(solution)/shard_map/pallas_call | solution.py:22
  31.5 0.0 collective-permute-done.14.wo
  31.5 4.7 %collective-permute-done.11.ue = f32[4,128,128]{2,1,0:T(8,128)S(1)} collective-permute-done((f32[4,128,128]{2,1,0:T(8,128)S(1)}, f32[4,128,128]{2,1,0:T(8,128)S(1)}, u32[]{:S(2)}, u32[]{:S(2)}) %collective-permute-start.11) | collective-permute-done | bytes 262176 | tf_op jit(solution)/shard_map/ppermute | solution.py:548
  36.2 0.0 collective-permute-done.12.uo
  36.2 1.8 %shard_map.71 = (f32[2,2,128,128]{3,2,1,0:T(8,128)S(1)}, f32[2,4,128,128]{3,2,1,0:T(8,128)S(1)}, f32[2,2,2,128,128]{4,3,2,1,0:T(8,128)S(1)}, f32[2,2,2,128,128]{4,3,2,1,0:T(8,128)S(1)}, f32[2,2,128,128]{3,2,1,0:T(8,128)S(1)}) custom-call(f32[8,128]{1,0:T(8,128)S(1)} %get-tuple-element.41.w.refs_0_, f32[4,128,128]{2,1,0:T(8,128)S(1)} %get-tuple-element.57.coef, ...), custom_call_target="tpu_custom_call" | custom-call | flops 27545600 | bytes 5509120 | tf_op jit(solution)/shard_map/pallas_call | solution.py:22
  38.0 0.8 %collective-permute-done.15.e = f32[2,128,128]{2,1,0:T(8,128)S(1)} collective-permute-done((f32[2,128,128]{2,1,0:T(8,128)S(1)}, f32[2,128,128]{2,1,0:T(8,128)S(1)}, u32[]{:S(2)}, u32[]{:S(2)}) %collective-permute-start.15) | collective-permute-done | bytes 131104 | tf_op jit(solution)/shard_map/ppermute | solution.py:548
  38.8 0.0 collective-permute-done.16.o
  38.8 1.2 %shard_map.72 = f32[1,2,4,128,128]{4,3,2,1,0:T(8,128)} custom-call(f32[8,128]{1,0:T(8,128)S(1)} %get-tuple-element.41.w.refs_0_, f32[4,128,128]{2,1,0:T(8,128)S(1)} %get-tuple-element.57.coef, f32[2,2,128,128]{3,2,1,0:T(8,128)S(1)} %get-tuple-element.67.rim, f32[2,4,128,128]{3,2,1,0:T(8,128)S(1)} %get-tuple-element.68.six, ...), custom_call_target="tpu_custom_call" | custom-call | flops 15749120 | bytes 3149824 | tf_op jit(solution)/shard_map/pallas_call | solution.py:22
  (4 shorter events, 0.1 us)
Async XLA Ops:
  2.0 7.2 %collective-permute-start = (f32[2,128,128]{2,1,0:T(8,128)S(1)}, f32[2,128,128]{2,1,0:T(8,128)S(1)}, u32[]{:S(2)}, u32[]{:S(2)}) collective-permute-start(f32[2,128,128]{2,1,0:T(8,128)S(1)} %get-tuple-element.45), channel_id=1, source_target_pairs={{0,1},{1,0},{2,3},{3,2},{4,5},{5,4},{6,7},{7,6},{8,9},{9,8},{10,11... | collective-permute-start | bytes 393224 | tf_op jit(solution)/shard_map/ppermute | solution.py:548
  5.2 4.1 %collective-permute-start.1 = (f32[2,128,128]{2,1,0:T(8,128)S(1)}, f32[2,128,128]{2,1,0:T(8,128)S(1)}, u32[]{:S(2)}, u32[]{:S(2)}) collective-permute-start(f32[2,128,128]{2,1,0:T(8,128)S(1)} %get-tuple-element.46), channel_id=1, source_target_pairs={{0,4},{1,2},{2,1},{3,7},{4,0},{5,6},{6,5},{7,3},{8,12},{9,10},{10,... | collective-permute-start | bytes 393224 | tf_op jit(solution)/shard_map/ppermute | solution.py:548
  6.0 6.8 %collective-permute-start.2 = (f32[2,128,128]{2,1,0:T(8,128)S(1)}, f32[2,128,128]{2,1,0:T(8,128)S(1)}, u32[]{:S(2)}, u32[]{:S(2)}) collective-permute-start(f32[2,128,128]{2,1,0:T(8,128)S(1)} %get-tuple-element.47), channel_id=1, source_target_pairs={{0,1},{1,0},{2,3},{3,2},{4,5},{5,4},{6,7},{7,6},{8,9},{9,8},{10,11... | collective-permute-start | bytes 393224 | tf_op jit(solution)/shard_map/ppermute | solution.py:548
  9.2 3.5 %collective-permute-start.3 = (f32[2,128,128]{2,1,0:T(8,128)S(1)}, f32[2,128,128]{2,1,0:T(8,128)S(1)}, u32[]{:S(2)}, u32[]{:S(2)}) collective-permute-start(f32[2,128,128]{2,1,0:T(8,128)S(1)} %get-tuple-element.48), channel_id=1, source_target_pairs={{0,4},{1,2},{2,1},{3,7},{4,0},{5,6},{6,5},{7,3},{8,12},{9,10},{10,... | collective-permute-start | bytes 393224 | tf_op jit(solution)/shard_map/ppermute | solution.py:548
  9.2 3.5 %collective-permute-start.4 = (f32[2,128,128]{2,1,0:T(8,128)S(1)}, f32[2,128,128]{2,1,0:T(8,128)S(1)}, u32[]{:S(2)}, u32[]{:S(2)}) collective-permute-start(f32[2,128,128]{2,1,0:T(8,128)S(1)} %shard_map.62), channel_id=1, source_target_pairs={{0,4},{4,0},{8,12},{12,8},{1,5},{5,1},{9,13},{13,9},{2,6},{6,2},{1... | collective-permute-start | bytes 393224 | tf_op jit(solution)/shard_map/ppermute | solution.py:557
  10.3 6.4 %collective-permute-start.7 = (f32[2,128,128]{2,1,0:T(8,128)S(1)}, f32[2,128,128]{2,1,0:T(8,128)S(1)}, u32[]{:S(2)}, u32[]{:S(2)}) collective-permute-start(f32[2,128,128]{2,1,0:T(8,128)S(1)} %get-tuple-element.54), channel_id=1, source_target_pairs={{0,1},{1,0},{2,3},{3,2},{4,5},{5,4},{6,7},{7,6},{8,9},{9,8},{10,11... | collective-permute-start | bytes 393224 | tf_op jit(solution)/shard_map/ppermute | solution.py:548
  12.5 4.2 %collective-permute-start.8 = (f32[2,128,128]{2,1,0:T(8,128)S(1)}, f32[2,128,128]{2,1,0:T(8,128)S(1)}, u32[]{:S(2)}, u32[]{:S(2)}) collective-permute-start(f32[2,128,128]{2,1,0:T(8,128)S(1)} %get-tuple-element.55), channel_id=1, source_target_pairs={{0,4},{1,2},{2,1},{3,7},{4,0},{5,6},{6,5},{7,3},{8,12},{9,10},{10,... | collective-permute-start | bytes 393224 | tf_op jit(solution)/shard_map/ppermute | solution.py:548
  13.4 5.9 %collective-permute-start.5 = (f32[264,128]{1,0:T(8,128)S(1)}, f32[264,128]{1,0:T(8,128)S(1)}, u32[]{:S(2)}, u32[]{:S(2)}) collective-permute-start(f32[264,128]{1,0:T(8,128)S(1)} %get-tuple-element.49.labels.mine), channel_id=1, source_target_pairs={{0,8},{4,12},{8,0},{12,4},{1,9},{5,13},{9,1},{13,5},{2,10},{6,14},... | collective-permute-start | bytes 405512 | tf_op jit(solution)/shard_map/ppermute | solution.py:557
  17.0 5.4 %collective-permute-start.9 = (f32[256,128]{1,0:T(8,128)S(1)}, f32[256,128]{1,0:T(8,128)S(1)}, u32[]{:S(2)}, u32[]{:S(2)}) collective-permute-start(f32[256,128]{1,0:T(8,128)S(1)} %get-tuple-element.56.mine), channel_id=1, source_target_pairs={{0,8},{4,12},{8,0},{12,4},{1,9},{5,13},{9,1},{13,5},{2,10},{6,14},... | collective-permute-start | bytes 393224 | tf_op jit(solution)/shard_map/ppermute | solution.py:557
  19.3 6.0 %collective-permute-start.6 = (f32[2,2,128,128]{3,2,1,0:T(8,128)S(1)}, f32[2,2,128,128]{3,2,1,0:T(8,128)S(1)}, u32[]{:S(2)}, u32[]{:S(2)}) collective-permute-start(f32[2,2,128,128]{3,2,1,0:T(8,128)S(1)} %shard_map.64.refs_1_.refs_0_), channel_id=1, source_target_pairs={{0,4},{4,0},{8,12},{12,8},{1,5},{5,1},{9,13},{13,9},{2,6},{6,2},{1... | collective-permute-start | bytes 786440 | tf_op jit(solution)/shard_map/ppermute | solution.py:557
  22.4 3.5 %collective-permute-start.10 = (f32[2,2,128,128]{3,2,1,0:T(8,128)S(1)}, f32[2,2,128,128]{3,2,1,0:T(8,128)S(1)}, u32[]{:S(2)}, u32[]{:S(2)}) collective-permute-start(f32[2,2,128,128]{3,2,1,0:T(8,128)S(1)} %shard_map.66.refs_3_.refs_2_), channel_id=1, source_target_pairs={{0,4},{4,0},{8,12},{12,8},{1,5},{5,1},{9,13},{13,9},{2,6},{6,2},{1... | collective-permute-start | bytes 786440 | tf_op jit(solution)/shard_map/ppermute | solution.py:557
  22.7 7.9 %collective-permute-start.13 = (f32[3,128,128]{2,1,0:T(8,128)S(1)}, f32[3,128,128]{2,1,0:T(8,128)S(1)}, u32[]{:S(2)}, u32[]{:S(2)}) collective-permute-start(f32[3,128,128]{2,1,0:T(8,128)S(1)} %get-tuple-element.65), channel_id=1, source_target_pairs={{0,1},{1,0},{2,3},{3,2},{4,5},{5,4},{6,7},{7,6},{8,9},{9,8},{10,11... | collective-permute-start | bytes 589832 | tf_op jit(solution)/shard_map/ppermute | solution.py:548
  24.9 11.3 %collective-permute-start.11 = (f32[4,128,128]{2,1,0:T(8,128)S(1)}, f32[4,128,128]{2,1,0:T(8,128)S(1)}, u32[]{:S(2)}, u32[]{:S(2)}) collective-permute-start(f32[4,128,128]{2,1,0:T(8,128)S(1)} %get-tuple-element.63), channel_id=1, source_target_pairs={{0,1},{1,0},{2,3},{3,2},{4,5},{5,4},{6,7},{7,6},{8,9},{9,8},{10,11... | collective-permute-start | bytes 786440 | tf_op jit(solution)/shard_map/ppermute | solution.py:548
  24.9 11.2 %collective-permute-start.12 = (f32[4,128,128]{2,1,0:T(8,128)S(1)}, f32[4,128,128]{2,1,0:T(8,128)S(1)}, u32[]{:S(2)}, u32[]{:S(2)}) collective-permute-start(f32[4,128,128]{2,1,0:T(8,128)S(1)} %get-tuple-element.64), channel_id=1, source_target_pairs={{0,4},{1,2},{2,1},{3,7},{4,0},{5,6},{6,5},{7,3},{8,12},{9,10},{10,... | collective-permute-start | bytes 786440 | tf_op jit(solution)/shard_map/ppermute | solution.py:548
  25.2 6.3 %collective-permute-start.14 = (f32[3,128,128]{2,1,0:T(8,128)S(1)}, f32[3,128,128]{2,1,0:T(8,128)S(1)}, u32[]{:S(2)}, u32[]{:S(2)}) collective-permute-start(f32[3,128,128]{2,1,0:T(8,128)S(1)} %get-tuple-element.66), channel_id=1, source_target_pairs={{0,4},{1,2},{2,1},{3,7},{4,0},{5,6},{6,5},{7,3},{8,12},{9,10},{10,... | collective-permute-start | bytes 589832 | tf_op jit(solution)/shard_map/ppermute | solution.py:548
  26.1 12.7 %collective-permute-start.15 = (f32[2,128,128]{2,1,0:T(8,128)S(1)}, f32[2,128,128]{2,1,0:T(8,128)S(1)}, u32[]{:S(2)}, u32[]{:S(2)}) collective-permute-start(f32[2,128,128]{2,1,0:T(8,128)S(1)} %get-tuple-element.72), channel_id=1, source_target_pairs={{0,1},{1,0},{2,3},{3,2},{4,5},{5,4},{6,7},{7,6},{8,9},{9,8},{10,11... | collective-permute-start | bytes 393224 | tf_op jit(solution)/shard_map/ppermute | solution.py:548
  30.6 8.2 %collective-permute-start.16 = (f32[2,128,128]{2,1,0:T(8,128)S(1)}, f32[2,128,128]{2,1,0:T(8,128)S(1)}, u32[]{:S(2)}, u32[]{:S(2)}) collective-permute-start(f32[2,128,128]{2,1,0:T(8,128)S(1)} %get-tuple-element.73), channel_id=1, source_target_pairs={{0,4},{1,2},{2,1},{3,7},{4,0},{5,6},{6,5},{7,3},{8,12},{9,10},{10,... | collective-permute-start | bytes 393224 | tf_op jit(solution)/shard_map/ppermute | solution.py:548

commit v7 on v6

--- a/solution.py
+++ b/solution.py
@@ -135,25 +135,22 @@
     return (make(i - 1) if i > 0 else ends[0]), (make(i + 1) if i < tile - 1 else ends[1])
 
 
-def fetch_kernel(f_in, v_in, c_in, even, odd, f, v, c, sems):
-    parts = [(v_in, v), (c_in, c)] + [(f_in.at[0, n], f.at[0, n]) for n in range(4)]
-    copies = [pltpu.make_async_copy(src, dst, sems.at[n]) for n, (src, dst) in enumerate(parts)]
+def fetch_kernel(f_in, v_in, c_in, even, odd, buf, sems):
+    tile, ny, nz = v_in.shape
+    k = Work(None, ny, nz)
+    copies = []
+    for n, src in enumerate((v_in, c_in, f_in.at[0, 0])):
+        for s, i in enumerate((0, tile - 1)):
+            copies.append(pltpu.make_async_copy(src.at[i], buf.at[n, s], sems.at[n, s]))
+            copies[-1].start()
     for copy in copies:
-        copy.start()
-    tile, ny, nz = v.shape
-    k = Work(None, ny, nz)
-    edge = (0, tile - 1)
-    for copy in copies[:3]:
         copy.wait()
     for r in k.blocks():
-        lo, hi = (
-            jnp.where(k.first_core, v[i, r:r + k.n], c[i, r:r + k.n]) for i in edge
-        )
+        at = slice(r, r + k.n)
+        lo, hi = (jnp.where(k.first_core, buf[0, s, at], buf[1, s, at]) for s in range(2))
         k.put(Plane(even, 0), r, jnp.where(k.even, hi, lo))
         k.put(Plane(odd, 0), r, jnp.where(k.even, lo, hi))
-    k.pack(even.at[1:], odd.at[1:], *([Plane(f, 0, 0, i)] for i in edge))
-    for copy in copies[3:]:
-        copy.wait()
+    k.pack(even.at[1:], odd.at[1:], [Plane(buf, 2, 0)], [Plane(buf, 2, 1)])
 
 
 def lead_kernel(label, f, v, c, even, odd, coef, w, one):
@@ -566,13 +563,13 @@
     def planes(*lead):
         return (*lead, ny, nz)
 
-    ae, ao, fields, velocity, conductivity = call(
+    ae, ao = call(
         fetch_kernel,
-        [planes(2)] * 2 + [fields.shape, velocity.shape, conductivity.shape],
+        [planes(2)] * 2,
         tuple(pltpu.with_memory_space_constraint(x, pltpu.HBM) for x in (fields, velocity, conductivity)),
-        (),
+        [planes(3, 2)],
         [pl.BlockSpec(memory_space=pltpu.HBM)] * 3,
-        [pltpu.SemaphoreType.DMA((6,))],
+        [pltpu.SemaphoreType.DMA((3, 2))],
     )
     ae, ao = swap_pairs(ae, ao)
     de, do, coef, w = call(

time: 40.5 us -> 40.8 us (level)
  the two profiles are of different devices: /device:TPU:0 before, /device:TPU:10 now
where the time goes in v7:
time: 40.8 us; the launch traced here: 40.7 us
  waiting for transfers between devices  17.6 us (43%)
  starting transfers between devices  13.9 us (34%)
  Pallas kernels  7.66 us (19%)
  between operations  1.49 us (4%)
    ppermute x12, waiting for transfers between devices, swap(): return lax.ppermute(block, ('src', 'space'), pairs)  12.9 us
    ppermute x12, starting transfers between devices, swap(): return lax.ppermute(block, ('src', 'space'), pairs)  12 us
    pallas_call x15, Pallas kernels, call(): pl.pallas_call(kernel, out_shape=tuple((jax.ShapeDtypeStruct(o, F32) for...  7.66 us
    ppermute x5, waiting for transfers between devices, across(): return lax.ppermute(block, 'src', [(i, i ^ mask) for i in range(count)])  4.61 us
    ppermute x5, starting transfers between devices, across(): return lax.ppermute(block, 'src', [(i, i ^ mask) for i in range(count)])  1.9 us
  transfers between devices with their start and end apart: 17, of which 7 were waited for; matrix products, arithmetic and copies ran while one was open for 0% of the time, Pallas kernels for 13%

profile of v7, /device:TPU:10, one launch (start us, length us, event | category | flops | bytes accessed | tf_op | source)
XLA Modules:
  0.0 40.7 jit_solution(7026703310275037293)
XLA Ops:
  0.6 0.0 copy-start.2
  0.6 0.0 copy-start.1
  0.6 0.0 copy-start
  0.7 1.2 %shard_map.61 = (f32[2,128,128]{2,1,0:T(8,128)S(1)}, f32[2,128,128]{2,1,0:T(8,128)S(1)}) custom-call(f32[1,4,4,128,128]{4,3,2,1,0:T(8,128)} %f.7, f32[4,128,128]{2,1,0:T(8,128)} %refs_5_.1, f32[4,128,128]{2,1,0:T(8,128)} %refs_6_.3), custom_call_target="tpu_custom_call" | custom-call | flops 9175040 | bytes 1835008 | tf_op jit(solution)/shard_map/pallas_call | solution.py:22
  1.9 0.5 %collective-permute-start = (f32[2,128,128]{2,1,0:T(8,128)S(1)}, f32[2,128,128]{2,1,0:T(8,128)S(1)}, u32[]{:S(2)}, u32[]{:S(2)}) collective-permute-start(f32[2,128,128]{2,1,0:T(8,128)S(1)} %get-tuple-element.39), channel_id=1, source_target_pairs={{0,1},{1,0},{2,3},{3,2},{4,5},{5,4},{6,7},{7,6},{8,9},{9,8},{10,11... | collective-permute-start | bytes 393224 | tf_op jit(solution)/shard_map/ppermute | solution.py:545
  2.4 2.7 %collective-permute-start.1 = (f32[2,128,128]{2,1,0:T(8,128)S(1)}, f32[2,128,128]{2,1,0:T(8,128)S(1)}, u32[]{:S(2)}, u32[]{:S(2)}) collective-permute-start(f32[2,128,128]{2,1,0:T(8,128)S(1)} %get-tuple-element.40), channel_id=1, source_target_pairs={{0,4},{1,2},{2,1},{3,7},{4,0},{5,6},{6,5},{7,3},{8,12},{9,10},{10,... | collective-permute-start | bytes 393224 | tf_op jit(solution)/shard_map/ppermute | solution.py:545
  5.8 0.2 shard_map.59
  5.9 0.1 collective-permute-start.2
  6.0 0.4 %collective-permute-start.3 = (f32[2,128,128]{2,1,0:T(8,128)S(1)}, f32[2,128,128]{2,1,0:T(8,128)S(1)}, u32[]{:S(2)}, u32[]{:S(2)}) collective-permute-start(f32[2,128,128]{2,1,0:T(8,128)S(1)} %get-tuple-element.42), channel_id=1, source_target_pairs={{0,4},{1,2},{2,1},{3,7},{4,0},{5,6},{6,5},{7,3},{8,12},{9,10},{10,... | collective-permute-start | bytes 393224 | tf_op jit(solution)/shard_map/ppermute | solution.py:545
  6.5 0.7 %collective-permute-done.even.ae = f32[2,128,128]{2,1,0:T(8,128)S(1)} collective-permute-done((f32[2,128,128]{2,1,0:T(8,128)S(1)}, f32[2,128,128]{2,1,0:T(8,128)S(1)}, u32[]{:S(2)}, u32[]{:S(2)}) %collective-permute-start) | collective-permute-done | bytes 131104 | tf_op jit(solution)/shard_map/ppermute | solution.py:545
  7.2 1.5 %collective-permute-done.1.odd.ao = f32[2,128,128]{2,1,0:T(8,128)S(1)} collective-permute-done((f32[2,128,128]{2,1,0:T(8,128)S(1)}, f32[2,128,128]{2,1,0:T(8,128)S(1)}, u32[]{:S(2)}, u32[]{:S(2)}) %collective-permute-start.1) | collective-permute-done | bytes 131104 | tf_op jit(solution)/shard_map/ppermute | solution.py:545
  8.6 0.1 collective-permute-start.4
  8.7 0.5 %shard_map.60 = (f32[2,128,128]{2,1,0:T(8,128)S(1)}, f32[2,128,128]{2,1,0:T(8,128)S(1)}, f32[2,4,128,128]{3,2,1,0:T(8,128)S(1)}, f32[4,128,128]{2,1,0:T(8,128)S(1)}) custom-call(f32[8,128]{1,0:T(8,128)S(1)} %get-tuple-element.35.w.refs_0_, f32[1,4,4,128,128]{4,3,2,1,0:T(8,128)S(1)} %copy-done, f32[4,128,128]{2,1,0:T(8,128)S(1)} %get-tuple-element.36.coef.old), custom_call_target="tpu_custom_call" | custom-call | flops 11816960 | bytes 2363392 | tf_op jit(solution)/shard_map/pallas_call | solution.py:22
  9.2 0.1 collective-permute-start.7
  9.3 2.4 %collective-permute-start.8 = (f32[2,128,128]{2,1,0:T(8,128)S(1)}, f32[2,128,128]{2,1,0:T(8,128)S(1)}, u32[]{:S(2)}, u32[]{:S(2)}) collective-permute-start(f32[2,128,128]{2,1,0:T(8,128)S(1)} %get-tuple-element.49), channel_id=1, source_target_pairs={{0,4},{1,2},{2,1},{3,7},{4,0},{5,6},{6,5},{7,3},{8,12},{9,10},{10,... | collective-permute-start | bytes 393224 | tf_op jit(solution)/shard_map/ppermute | solution.py:545
  11.7 0.0 collective-permute-done.2.de
  11.7 0.0 collective-permute-done.3.do
  11.7 0.0 collective-permute-done.4.other
  11.7 0.6 %shard_map.63 = (f32[264,128]{1,0:T(8,128)S(1)}, f32[2,128,128]{2,1,0:T(8,128)S(1)}, f32[2,2,128,128]{3,2,1,0:T(8,128)S(1)}, f32[2,4,128,128]{3,2,1,0:T(8,128)S(...) custom-call(f32[8,128]{1,0:T(8,128)S(1)} %get-tuple-element.35.w.refs_0_, ...), custom_call_target="tpu_custom_call" | custom-call | flops 21667840 | bytes 4333568 | tf_op jit(solution)/shard_map/pallas_call | solution.py:22
  12.3 0.6 %collective-permute-start.5 = (f32[264,128]{1,0:T(8,128)S(1)}, f32[264,128]{1,0:T(8,128)S(1)}, u32[]{:S(2)}, u32[]{:S(2)}) collective-permute-start(f32[264,128]{1,0:T(8,128)S(1)} %get-tuple-element.43.labels.mine), channel_id=1, source_target_pairs={{0,8},{4,12},{8,0},{12,4},{1,9},{5,13},{9,1},{13,5},{2,10},{6,14},... | collective-permute-start | bytes 405512 | tf_op jit(solution)/shard_map/ppermute | solution.py:554
  12.9 2.2 %collective-permute-done.7.be = f32[2,128,128]{2,1,0:T(8,128)S(1)} collective-permute-done((f32[2,128,128]{2,1,0:T(8,128)S(1)}, f32[2,128,128]{2,1,0:T(8,128)S(1)}, u32[]{:S(2)}, u32[]{:S(2)}) %collective-permute-start.7) | collective-permute-done | bytes 131104 | tf_op jit(solution)/shard_map/ppermute | solution.py:545
  15.2 0.5 %collective-permute-done.8.bo = f32[2,128,128]{2,1,0:T(8,128)S(1)} collective-permute-done((f32[2,128,128]{2,1,0:T(8,128)S(1)}, f32[2,128,128]{2,1,0:T(8,128)S(1)}, u32[]{:S(2)}, u32[]{:S(2)}) %collective-permute-start.8) | collective-permute-done | bytes 131104 | tf_op jit(solution)/shard_map/ppermute | solution.py:545
  15.7 0.3 shard_map.65
  16.0 0.6 %collective-permute-start.9 = (f32[256,128]{1,0:T(8,128)S(1)}, f32[256,128]{1,0:T(8,128)S(1)}, u32[]{:S(2)}, u32[]{:S(2)}) collective-permute-start(f32[256,128]{1,0:T(8,128)S(1)} %get-tuple-element.50.mine), channel_id=1, source_target_pairs={{0,8},{4,12},{8,0},{12,4},{1,9},{5,13},{9,1},{13,5},{2,10},{6,14},... | collective-permute-start | bytes 393224 | tf_op jit(solution)/shard_map/ppermute | solution.py:554
  16.6 4.6 %collective-permute-done.9.other = f32[256,128]{1,0:T(8,128)S(1)} collective-permute-done((f32[256,128]{1,0:T(8,128)S(1)}, f32[256,128]{1,0:T(8,128)S(1)}, u32[]{:S(2)}, u32[]{:S(2)}) %collective-permute-start.9) | collective-permute-done | bytes 131104 | tf_op jit(solution)/shard_map/ppermute | solution.py:554
  21.2 0.0 collective-permute-done.5.far_labels.other
  21.2 0.1 collective-permute-start.10
  21.4 0.6 %collective-permute-start.6 = (f32[2,2,128,128]{3,2,1,0:T(8,128)S(1)}, f32[2,2,128,128]{3,2,1,0:T(8,128)S(1)}, u32[]{:S(2)}, u32[]{:S(2)}) collective-permute-start(f32[2,2,128,128]{3,2,1,0:T(8,128)S(1)} %shard_map.64.refs_1_.refs_0_), channel_id=1, source_target_pairs={{0,4},{4,0},{8,12},{12,8},{1,5},{5,1},{9,13},{13,9},{2,6},{6,2},{1... | collective-permute-start | bytes 786440 | tf_op jit(solution)/shard_map/ppermute | solution.py:554
  21.9 0.2 shard_map.69
  22.1 0.1 collective-permute-start.13
  22.2 2.1 %collective-permute-start.11 = (f32[4,128,128]{2,1,0:T(8,128)S(1)}, f32[4,128,128]{2,1,0:T(8,128)S(1)}, u32[]{:S(2)}, u32[]{:S(2)}) collective-permute-start(f32[4,128,128]{2,1,0:T(8,128)S(1)} %get-tuple-element.57), channel_id=1, source_target_pairs={{0,1},{1,0},{2,3},{3,2},{4,5},{5,4},{6,7},{7,6},{8,9},{9,8},{10,11... | collective-permute-start | bytes 786440 | tf_op jit(solution)/shard_map/ppermute | solution.py:545
  24.3 1.6 %collective-permute-start.12 = (f32[4,128,128]{2,1,0:T(8,128)S(1)}, f32[4,128,128]{2,1,0:T(8,128)S(1)}, u32[]{:S(2)}, u32[]{:S(2)}) collective-permute-start(f32[4,128,128]{2,1,0:T(8,128)S(1)} %get-tuple-element.58), channel_id=1, source_target_pairs={{0,4},{1,2},{2,1},{3,7},{4,0},{5,6},{6,5},{7,3},{8,12},{9,10},{10,... | collective-permute-start | bytes 786440 | tf_op jit(solution)/shard_map/ppermute | solution.py:545
  25.9 0.0 collective-permute-done.10.refs_4_.refs_3_
  25.9 0.5 %collective-permute-start.14 = (f32[3,128,128]{2,1,0:T(8,128)S(1)}, f32[3,128,128]{2,1,0:T(8,128)S(1)}, u32[]{:S(2)}, u32[]{:S(2)}) collective-permute-start(f32[3,128,128]{2,1,0:T(8,128)S(1)} %get-tuple-element.60), channel_id=1, source_target_pairs={{0,4},{1,2},{2,1},{3,7},{4,0},{5,6},{6,5},{7,3},{8,12},{9,10},{10,... | collective-permute-start | bytes 589832 | tf_op jit(solution)/shard_map/ppermute | solution.py:545
  26.3 0.4 %shard_map.67.refs_5_.refs_4_ = f32[4,128,128]{2,1,0:T(8,128)S(1)} custom-call(f32[4,128,128]{2,1,0:T(8,128)S(1)} %copy-done.1, f32[4,128,128]{2,1,0:T(8,128)S(1)} %copy-done.2, f32[2,128,128]{2,1,0:T(8,128)S(1)} %collective-permute-done.even.ae, f32[2,128,128]{2,1,0:T(8,128)S(1)} %collective-permute-done.1.odd.ao, ...), custom_call_target="tpu_custom_call" | custom-call | flops 5898240 | bytes 1179648 | tf_op jit(solution)/shard_map/pallas_call | solution.py:22
  26.8 0.0 collective-permute-done.6.refs_2_.refs_1_
  26.8 0.2 shard_map.68
  26.9 0.1 collective-permute-start.15
  27.0 2.9 %collective-permute-done.13.we = f32[3,128,128]{2,1,0:T(8,128)S(1)} collective-permute-done((f32[3,128,128]{2,1,0:T(8,128)S(1)}, f32[3,128,128]{2,1,0:T(8,128)S(1)}, u32[]{:S(2)}, u32[]{:S(2)}) %collective-permute-start.13) | collective-permute-done | bytes 196640 | tf_op jit(solution)/shard_map/ppermute | solution.py:545
  29.9 1.6 %collective-permute-start.16 = (f32[2,128,128]{2,1,0:T(8,128)S(1)}, f32[2,128,128]{2,1,0:T(8,128)S(1)}, u32[]{:S(2)}, u32[]{:S(2)}) collective-permute-start(f32[2,128,128]{2,1,0:T(8,128)S(1)} %get-tuple-element.67), channel_id=1, source_target_pairs={{0,4},{1,2},{2,1},{3,7},{4,0},{5,6},{6,5},{7,3},{8,12},{9,10},{10,... | collective-permute-start | bytes 393224 | tf_op jit(solution)/shard_map/ppermute | solution.py:545
  31.5 1.0 %shard_map.73 = f32[2,4,128,128]{3,2,1,0:T(8,128)} custom-call(f32[2,2,128,128]{3,2,1,0:T(8,128)S(1)} %shard_map.64.refs_1_.refs_0_, f32[2,2,128,128]{3,2,1,0:T(8,128)S(1)} %collective-permute-done.6.refs_2_.refs_1_, f32[2,2,128,128]{3,2,1,0:T(8,128)S(1)} %shard_map.66.refs_3_.refs_2_, f32[2,2,128,128]{3,2,1,0:T(8,128)S(1)} %collective-permute-done.10.refs_4_.refs_3_, ...), custom_call_target="tpu_custom_call" | custom-call | flops 11796480 | bytes 2359296 | tf_op jit(solution)/shard_map/pallas_call | solution.py:22
  32.4 5.1 %collective-permute-done.14.wo = f32[3,128,128]{2,1,0:T(8,128)S(1)} collective-permute-done((f32[3,128,128]{2,1,0:T(8,128)S(1)}, f32[3,128,128]{2,1,0:T(8,128)S(1)}, u32[]{:S(2)}, u32[]{:S(2)}) %collective-permute-start.14) | collective-permute-done | bytes 196640 | tf_op jit(solution)/shard_map/ppermute | solution.py:545
  37.6 0.0 collective-permute-done.11.ue
  37.6 0.0 collective-permute-done.12.uo
  37.6 1.8 %shard_map.71 = (f32[2,2,128,128]{3,2,1,0:T(8,128)S(1)}, f32[2,4,128,128]{3,2,1,0:T(8,128)S(1)}, f32[2,2,2,128,128]{4,3,2,1,0:T(8,128)S(1)}, f32[2,2,2,128,128]{4,3,2,1,0:T(8,128)S(1)}, f32[2,2,128,128]{3,2,1,0:T(8,128)S(1)}) custom-call(f32[8,128]{1,0:T(8,128)S(1)} %get-tuple-element.35.w.refs_0_, f32[4,128,128]{2,1,0:T(8,128)S(1)} %get-tuple-element.51.coef, ...), custom_call_target="tpu_custom_call" | custom-call | flops 27545600 | bytes 5509120 | tf_op jit(solution)/shard_map/pallas_call | solution.py:22
  39.4 0.0 collective-permute-done.15.e
  39.4 0.0 collective-permute-done.16.o
  39.4 1.2 %shard_map.72 = f32[1,2,4,128,128]{4,3,2,1,0:T(8,128)} custom-call(f32[8,128]{1,0:T(8,128)S(1)} %get-tuple-element.35.w.refs_0_, f32[4,128,128]{2,1,0:T(8,128)S(1)} %get-tuple-element.51.coef, f32[2,2,128,128]{3,2,1,0:T(8,128)S(1)} %get-tuple-element.61.rim, f32[2,4,128,128]{3,2,1,0:T(8,128)S(1)} %get-tuple-element.62.six, ...), custom_call_target="tpu_custom_call" | custom-call | flops 15749120 | bytes 3149824 | tf_op jit(solution)/shard_map/pallas_call | solution.py:22
  (7 shorter events, 0.1 us)
Async XLA Ops:
  0.6 5.1 %copy-start.2 = (f32[4,128,128]{2,1,0:T(8,128)S(1)}, f32[4,128,128]{2,1,0:T(8,128)}, u32[]{:S(2)}) copy-start(f32[4,128,128]{2,1,0:T(8,128)} %refs_6_.3) | copy-start | bytes 786436
  0.6 5.1 %copy-start.1 = (f32[4,128,128]{2,1,0:T(8,128)S(1)}, f32[4,128,128]{2,1,0:T(8,128)}, u32[]{:S(2)}) copy-start(f32[4,128,128]{2,1,0:T(8,128)} %refs_5_.1) | copy-start | bytes 786436
  0.6 5.1 %copy-start = (f32[1,4,4,128,128]{4,3,2,1,0:T(8,128)S(1)}, f32[1,4,4,128,128]{4,3,2,1,0:T(8,128)}, u32[]{:S(2)}) copy-start(f32[1,4,4,128,128]{4,3,2,1,0:T(8,128)} %f.7) | copy-start | bytes 3145732
  1.9 5.3 %collective-permute-start = (f32[2,128,128]{2,1,0:T(8,128)S(1)}, f32[2,128,128]{2,1,0:T(8,128)S(1)}, u32[]{:S(2)}, u32[]{:S(2)}) collective-permute-start(f32[2,128,128]{2,1,0:T(8,128)S(1)} %get-tuple-element.39), channel_id=1, source_target_pairs={{0,1},{1,0},{2,3},{3,2},{4,5},{5,4},{6,7},{7,6},{8,9},{9,8},{10,11... | collective-permute-start | bytes 393224 | tf_op jit(solution)/shard_map/ppermute | solution.py:545
  2.4 6.3 %collective-permute-start.1 = (f32[2,128,128]{2,1,0:T(8,128)S(1)}, f32[2,128,128]{2,1,0:T(8,128)S(1)}, u32[]{:S(2)}, u32[]{:S(2)}) collective-permute-start(f32[2,128,128]{2,1,0:T(8,128)S(1)} %get-tuple-element.40), channel_id=1, source_target_pairs={{0,4},{1,2},{2,1},{3,7},{4,0},{5,6},{6,5},{7,3},{8,12},{9,10},{10,... | collective-permute-start | bytes 393224 | tf_op jit(solution)/shard_map/ppermute | solution.py:545
  5.9 5.8 %collective-permute-start.2 = (f32[2,128,128]{2,1,0:T(8,128)S(1)}, f32[2,128,128]{2,1,0:T(8,128)S(1)}, u32[]{:S(2)}, u32[]{:S(2)}) collective-permute-start(f32[2,128,128]{2,1,0:T(8,128)S(1)} %get-tuple-element.41), channel_id=1, source_target_pairs={{0,1},{1,0},{2,3},{3,2},{4,5},{5,4},{6,7},{7,6},{8,9},{9,8},{10,11... | collective-permute-start | bytes 393224 | tf_op jit(solution)/shard_map/ppermute | solution.py:545
  6.0 5.7 %collective-permute-start.3 = (f32[2,128,128]{2,1,0:T(8,128)S(1)}, f32[2,128,128]{2,1,0:T(8,128)S(1)}, u32[]{:S(2)}, u32[]{:S(2)}) collective-permute-start(f32[2,128,128]{2,1,0:T(8,128)S(1)} %get-tuple-element.42), channel_id=1, source_target_pairs={{0,4},{1,2},{2,1},{3,7},{4,0},{5,6},{6,5},{7,3},{8,12},{9,10},{10,... | collective-permute-start | bytes 393224 | tf_op jit(solution)/shard_map/ppermute | solution.py:545
  8.6 3.1 %collective-permute-start.4 = (f32[2,128,128]{2,1,0:T(8,128)S(1)}, f32[2,128,128]{2,1,0:T(8,128)S(1)}, u32[]{:S(2)}, u32[]{:S(2)}) collective-permute-start(f32[2,128,128]{2,1,0:T(8,128)S(1)} %shard_map.62), channel_id=1, source_target_pairs={{0,4},{4,0},{8,12},{12,8},{1,5},{5,1},{9,13},{13,9},{2,6},{6,2},{1... | collective-permute-start | bytes 393224 | tf_op jit(solution)/shard_map/ppermute | solution.py:554
  9.2 6.0 %collective-permute-start.7 = (f32[2,128,128]{2,1,0:T(8,128)S(1)}, f32[2,128,128]{2,1,0:T(8,128)S(1)}, u32[]{:S(2)}, u32[]{:S(2)}) collective-permute-start(f32[2,128,128]{2,1,0:T(8,128)S(1)} %get-tuple-element.48), channel_id=1, source_target_pairs={{0,1},{1,0},{2,3},{3,2},{4,5},{5,4},{6,7},{7,6},{8,9},{9,8},{10,11... | collective-permute-start | bytes 393224 | tf_op jit(solution)/shard_map/ppermute | solution.py:545
  9.3 6.4 %collective-permute-start.8 = (f32[2,128,128]{2,1,0:T(8,128)S(1)}, f32[2,128,128]{2,1,0:T(8,128)S(1)}, u32[]{:S(2)}, u32[]{:S(2)}) collective-permute-start(f32[2,128,128]{2,1,0:T(8,128)S(1)} %get-tuple-element.49), channel_id=1, source_target_pairs={{0,4},{1,2},{2,1},{3,7},{4,0},{5,6},{6,5},{7,3},{8,12},{9,10},{10,... | collective-permute-start | bytes 393224 | tf_op jit(solution)/shard_map/ppermute | solution.py:545
  12.3 8.9 %collective-permute-start.5 = (f32[264,128]{1,0:T(8,128)S(1)}, f32[264,128]{1,0:T(8,128)S(1)}, u32[]{:S(2)}, u32[]{:S(2)}) collective-permute-start(f32[264,128]{1,0:T(8,128)S(1)} %get-tuple-element.43.labels.mine), channel_id=1, source_target_pairs={{0,8},{4,12},{8,0},{12,4},{1,9},{5,13},{9,1},{13,5},{2,10},{6,14},... | collective-permute-start | bytes 405512 | tf_op jit(solution)/shard_map/ppermute | solution.py:554
  16.0 5.2 %collective-permute-start.9 = (f32[256,128]{1,0:T(8,128)S(1)}, f32[256,128]{1,0:T(8,128)S(1)}, u32[]{:S(2)}, u32[]{:S(2)}) collective-permute-start(f32[256,128]{1,0:T(8,128)S(1)} %get-tuple-element.50.mine), channel_id=1, source_target_pairs={{0,8},{4,12},{8,0},{12,4},{1,9},{5,13},{9,1},{13,5},{2,10},{6,14},... | collective-permute-start | bytes 393224 | tf_op jit(solution)/shard_map/ppermute | solution.py:554
  21.2 4.6 %collective-permute-start.10 = (f32[2,2,128,128]{3,2,1,0:T(8,128)S(1)}, f32[2,2,128,128]{3,2,1,0:T(8,128)S(1)}, u32[]{:S(2)}, u32[]{:S(2)}) collective-permute-start(f32[2,2,128,128]{3,2,1,0:T(8,128)S(1)} %shard_map.66.refs_3_.refs_2_), channel_id=1, source_target_pairs={{0,4},{4,0},{8,12},{12,8},{1,5},{5,1},{9,13},{13,9},{2,6},{6,2},{1... | collective-permute-start | bytes 786440 | tf_op jit(solution)/shard_map/ppermute | solution.py:554
  21.4 5.4 %collective-permute-start.6 = (f32[2,2,128,128]{3,2,1,0:T(8,128)S(1)}, f32[2,2,128,128]{3,2,1,0:T(8,128)S(1)}, u32[]{:S(2)}, u32[]{:S(2)}) collective-permute-start(f32[2,2,128,128]{3,2,1,0:T(8,128)S(1)} %shard_map.64.refs_1_.refs_0_), channel_id=1, source_target_pairs={{0,4},{4,0},{8,12},{12,8},{1,5},{5,1},{9,13},{13,9},{2,6},{6,2},{1... | collective-permute-start | bytes 786440 | tf_op jit(solution)/shard_map/ppermute | solution.py:554
  22.1 7.8 %collective-permute-start.13 = (f32[3,128,128]{2,1,0:T(8,128)S(1)}, f32[3,128,128]{2,1,0:T(8,128)S(1)}, u32[]{:S(2)}, u32[]{:S(2)}) collective-permute-start(f32[3,128,128]{2,1,0:T(8,128)S(1)} %get-tuple-element.59), channel_id=1, source_target_pairs={{0,1},{1,0},{2,3},{3,2},{4,5},{5,4},{6,7},{7,6},{8,9},{9,8},{10,11... | collective-permute-start | bytes 589832 | tf_op jit(solution)/shard_map/ppermute | solution.py:545
  22.2 15.4 %collective-permute-start.11 = (f32[4,128,128]{2,1,0:T(8,128)S(1)}, f32[4,128,128]{2,1,0:T(8,128)S(1)}, u32[]{:S(2)}, u32[]{:S(2)}) collective-permute-start(f32[4,128,128]{2,1,0:T(8,128)S(1)} %get-tuple-element.57), channel_id=1, source_target_pairs={{0,1},{1,0},{2,3},{3,2},{4,5},{5,4},{6,7},{7,6},{8,9},{9,8},{10,11... | collective-permute-start | bytes 786440 | tf_op jit(solution)/shard_map/ppermute | solution.py:545
  24.3 13.3 %collective-permute-start.12 = (f32[4,128,128]{2,1,0:T(8,128)S(1)}, f32[4,128,128]{2,1,0:T(8,128)S(1)}, u32[]{:S(2)}, u32[]{:S(2)}) collective-permute-start(f32[4,128,128]{2,1,0:T(8,128)S(1)} %get-tuple-element.58), channel_id=1, source_target_pairs={{0,4},{1,2},{2,1},{3,7},{4,0},{5,6},{6,5},{7,3},{8,12},{9,10},{10,... | collective-permute-start | bytes 786440 | tf_op jit(solution)/shard_map/ppermute | solution.py:545
  25.9 11.7 %collective-permute-start.14 = (f32[3,128,128]{2,1,0:T(8,128)S(1)}, f32[3,128,128]{2,1,0:T(8,128)S(1)}, u32[]{:S(2)}, u32[]{:S(2)}) collective-permute-start(f32[3,128,128]{2,1,0:T(8,128)S(1)} %get-tuple-element.60), channel_id=1, source_target_pairs={{0,4},{1,2},{2,1},{3,7},{4,0},{5,6},{6,5},{7,3},{8,12},{9,10},{10,... | collective-permute-start | bytes 589832 | tf_op jit(solution)/shard_map/ppermute | solution.py:545
  26.9 12.5 %collective-permute-start.15 = (f32[2,128,128]{2,1,0:T(8,128)S(1)}, f32[2,128,128]{2,1,0:T(8,128)S(1)}, u32[]{:S(2)}, u32[]{:S(2)}) collective-permute-start(f32[2,128,128]{2,1,0:T(8,128)S(1)} %get-tuple-element.66), channel_id=1, source_target_pairs={{0,1},{1,0},{2,3},{3,2},{4,5},{5,4},{6,7},{7,6},{8,9},{9,8},{10,11... | collective-permute-start | bytes 393224 | tf_op jit(solution)/shard_map/ppermute | solution.py:545
  29.9 9.5 %collective-permute-start.16 = (f32[2,128,128]{2,1,0:T(8,128)S(1)}, f32[2,128,128]{2,1,0:T(8,128)S(1)}, u32[]{:S(2)}, u32[]{:S(2)}) collective-permute-start(f32[2,128,128]{2,1,0:T(8,128)S(1)} %get-tuple-element.67), channel_id=1, source_target_pairs={{0,4},{1,2},{2,1},{3,7},{4,0},{5,6},{6,5},{7,3},{8,12},{9,10},{10,... | collective-permute-start | bytes 393224 | tf_op jit(solution)/shard_map/ppermute | solution.py:545

commit v8 on v7

--- a/solution.py
+++ b/solution.py
@@ -135,22 +135,23 @@
     return (make(i - 1) if i > 0 else ends[0]), (make(i + 1) if i < tile - 1 else ends[1])
 
 
-def fetch_kernel(f_in, v_in, c_in, even, odd, buf, sems):
+def fetch_kernel(f_in, v_in, c_in, even, odd, sems):
     tile, ny, nz = v_in.shape
     k = Work(None, ny, nz)
-    copies = []
-    for n, src in enumerate((v_in, c_in, f_in.at[0, 0])):
-        for s, i in enumerate((0, tile - 1)):
-            copies.append(pltpu.make_async_copy(src.at[i], buf.at[n, s], sems.at[n, s]))
-            copies[-1].start()
-    for copy in copies:
-        copy.wait()
-    for r in k.blocks():
-        at = slice(r, r + k.n)
-        lo, hi = (jnp.where(k.first_core, buf[0, s, at], buf[1, s, at]) for s in range(2))
-        k.put(Plane(even, 0), r, jnp.where(k.even, hi, lo))
-        k.put(Plane(odd, 0), r, jnp.where(k.even, lo, hi))
-    k.pack(even.at[1:], odd.at[1:], [Plane(buf, 2, 0)], [Plane(buf, 2, 1)])
+    high = (tile - 1) * k.even.astype(jnp.int32)
+    places = ((even, high), (odd, tile - 1 - high))
+
+    def model(src):
+        for n, (out, at) in enumerate(places):
+            pltpu.make_async_copy(src.at[at], out.at[0], sems.at[0, n]).start()
+
+    pl.when(k.first_core)(lambda: model(v_in))
+    pl.when(jnp.logical_not(k.first_core))(lambda: model(c_in))
+    for n, (out, at) in enumerate(places):
+        pltpu.make_async_copy(f_in.at[0, 0, at], out.at[1], sems.at[1, n]).start()
+    for n, (out, at) in enumerate(places):
+        pltpu.make_async_copy(v_in.at[at], out.at[0], sems.at[0, n]).wait()
+        pltpu.make_async_copy(f_in.at[0, 0, at], out.at[1], sems.at[1, n]).wait()
 
 
 def lead_kernel(label, f, v, c, even, odd, coef, w, one):
@@ -502,27 +503,29 @@
             for r in k.blocks():
                 k.put(Plane(res, n, i), r, k.get(Plane(six, n, i), r))
             send(n, i)
-        for s, i in enumerate(edge):
-            for r in k.blocks():
-                at = slice(r, r + k.n)
-                outer, inner = (k.unpack(e, o, (m, 1 - m)[s], r)[s] for m in range(2))
+    for s, i in enumerate(edge):
+        j = next_to[s]
+        for r in k.blocks():
+            at = slice(r, r + k.n)
+            outer, inner = (k.unpack(e, o, (m, 1 - m)[s], r)[s] for m in range(2))
+            h5[s, at] = inner
+            for n in range(2):
                 near_plane = ring[n, s, 1, at] + inner * lap[n, s, 1, at]
                 close[n, s, at] = near_plane
                 away[n, s, at] = (
                     k.ahead(near_plane, side[n, s, at])
                     + inner * (ring[n, s, 0, at] + outer * lap[n, s, 0, at] + rim[n, s, at])
                 )
-                h5[n, s, at] = inner
                 delta = coef[i, at] * near_plane
                 d[n, s, at] = delta
-                j = next_to[s]
                 res[n, j, at] = six[n, j, at] + coef[j, at] * delta
-            send(n, next_to[s])
-        for s, i in enumerate(edge):
+        for n in range(2):
+            send(n, j)
+        for n in range(2):
             for r in k.blocks():
                 at = slice(r, r + k.n)
                 _, total = k.flat(Plane(close, n, s), r)
-                fifth = away[n, s, at] + h5[n, s, at] * total
+                fifth = away[n, s, at] + h5[s, at] * total
                 delta, total = k.flat(Plane(d, n, s), r)
                 res[n, i, at] = (
                     six[n, i, at] + (1.0 + k.a) * delta + coef[i, at] * (total + fifth)
@@ -567,9 +570,9 @@
         fetch_kernel,
         [planes(2)] * 2,
         tuple(pltpu.with_memory_space_constraint(x, pltpu.HBM) for x in (fields, velocity, conductivity)),
-        [planes(3, 2)],
+        (),
         [pl.BlockSpec(memory_space=pltpu.HBM)] * 3,
-        [pltpu.SemaphoreType.DMA((3, 2))],
+        [pltpu.SemaphoreType.DMA((2, 2))],
     )
     ae, ao = swap_pairs(ae, ao)
     de, do, coef, w = call(
@@ -645,7 +648,7 @@
         after_kernel,
         [planes(1, 2, tile)],
         (w, coef_next, rim, six, ring, lap, side, e, o),
-        [planes(2, tile), planes(2, 2), planes(2, 2), planes(2, 2), planes(2, 2)],
+        [planes(2, tile), planes(2, 2), planes(2, 2), planes(2, 2), planes(2)],
         None,
         [pltpu.SemaphoreType.DMA((2, tile))],
         pl.BlockSpec(memory_space=pltpu.HBM),

time: 40.8 us -> 40.7 us (level)
  no operation moved by 1% of the time
where the time goes in v8:
time: 40.7 us; the launch traced here: 40.6 us
  waiting for transfers between devices  17.6 us (43%)
  starting transfers between devices  13.9 us (34%)
  Pallas kernels  7.55 us (19%)
  between operations  1.49 us (4%)
    ppermute x12, waiting for transfers between devices, swap(): return lax.ppermute(block, ('src', 'space'), pairs)  12.9 us
    ppermute x12, starting transfers between devices, swap(): return lax.ppermute(block, ('src', 'space'), pairs)  12 us
    pallas_call x15, Pallas kernels, call(): pl.pallas_call(kernel, out_shape=tuple((jax.ShapeDtypeStruct(o, F32) for...  7.55 us
    ppermute x5, waiting for transfers between devices, across(): return lax.ppermute(block, 'src', [(i, i ^ mask) for i in range(count)])  4.61 us
    ppermute x5, starting transfers between devices, across(): return lax.ppermute(block, 'src', [(i, i ^ mask) for i in range(count)])  1.9 us
  transfers between devices with their start and end apart: 17, of which 7 were waited for; matrix products, arithmetic and copies ran while one was open for 0% of the time, Pallas kernels for 13%

profile of v8, /device:TPU:10, one launch (start us, length us, event | category | flops | bytes accessed | tf_op | source)
XLA Modules:
  0.0 40.6 jit_solution(7997106862828722080)
XLA Ops:
  0.6 0.0 copy-start.2
  0.6 0.0 copy-start.1
  0.6 0.0 copy-start
  0.7 1.1 %shard_map.61 = (f32[2,128,128]{2,1,0:T(8,128)S(1)}, f32[2,128,128]{2,1,0:T(8,128)S(1)}) custom-call(f32[1,4,4,128,128]{4,3,2,1,0:T(8,128)} %f.7, f32[4,128,128]{2,1,0:T(8,128)} %refs_5_.1, f32[4,128,128]{2,1,0:T(8,128)} %refs_6_.3), custom_call_target="tpu_custom_call" | custom-call | flops 9175040 | bytes 1835008 | tf_op jit(solution)/shard_map/pallas_call | solution.py:22
  1.8 0.5 %collective-permute-start = (f32[2,128,128]{2,1,0:T(8,128)S(1)}, f32[2,128,128]{2,1,0:T(8,128)S(1)}, u32[]{:S(2)}, u32[]{:S(2)}) collective-permute-start(f32[2,128,128]{2,1,0:T(8,128)S(1)} %get-tuple-element.39), channel_id=1, source_target_pairs={{0,1},{1,0},{2,3},{3,2},{4,5},{5,4},{6,7},{7,6},{8,9},{9,8},{10,11... | collective-permute-start | bytes 393224 | tf_op jit(solution)/shard_map/ppermute | solution.py:548
  2.3 2.7 %collective-permute-start.1 = (f32[2,128,128]{2,1,0:T(8,128)S(1)}, f32[2,128,128]{2,1,0:T(8,128)S(1)}, u32[]{:S(2)}, u32[]{:S(2)}) collective-permute-start(f32[2,128,128]{2,1,0:T(8,128)S(1)} %get-tuple-element.40), channel_id=1, source_target_pairs={{0,4},{1,2},{2,1},{3,7},{4,0},{5,6},{6,5},{7,3},{8,12},{9,10},{10,... | collective-permute-start | bytes 393224 | tf_op jit(solution)/shard_map/ppermute | solution.py:548
  5.7 0.2 shard_map.59
  5.8 0.1 collective-permute-start.2
  5.9 0.4 %collective-permute-start.3 = (f32[2,128,128]{2,1,0:T(8,128)S(1)}, f32[2,128,128]{2,1,0:T(8,128)S(1)}, u32[]{:S(2)}, u32[]{:S(2)}) collective-permute-start(f32[2,128,128]{2,1,0:T(8,128)S(1)} %get-tuple-element.42), channel_id=1, source_target_pairs={{0,4},{1,2},{2,1},{3,7},{4,0},{5,6},{6,5},{7,3},{8,12},{9,10},{10,... | collective-permute-start | bytes 393224 | tf_op jit(solution)/shard_map/ppermute | solution.py:548
  6.4 0.7 %collective-permute-done.even.ae = f32[2,128,128]{2,1,0:T(8,128)S(1)} collective-permute-done((f32[2,128,128]{2,1,0:T(8,128)S(1)}, f32[2,128,128]{2,1,0:T(8,128)S(1)}, u32[]{:S(2)}, u32[]{:S(2)}) %collective-permute-start) | collective-permute-done | bytes 131104 | tf_op jit(solution)/shard_map/ppermute | solution.py:548
  7.1 1.5 %collective-permute-done.1.odd.ao = f32[2,128,128]{2,1,0:T(8,128)S(1)} collective-permute-done((f32[2,128,128]{2,1,0:T(8,128)S(1)}, f32[2,128,128]{2,1,0:T(8,128)S(1)}, u32[]{:S(2)}, u32[]{:S(2)}) %collective-permute-start.1) | collective-permute-done | bytes 131104 | tf_op jit(solution)/shard_map/ppermute | solution.py:548
  8.5 0.1 collective-permute-start.4
  8.6 0.5 %shard_map.60 = (f32[2,128,128]{2,1,0:T(8,128)S(1)}, f32[2,128,128]{2,1,0:T(8,128)S(1)}, f32[2,4,128,128]{3,2,1,0:T(8,128)S(1)}, f32[4,128,128]{2,1,0:T(8,128)S(1)}) custom-call(f32[8,128]{1,0:T(8,128)S(1)} %get-tuple-element.35.w.refs_0_, f32[1,4,4,128,128]{4,3,2,1,0:T(8,128)S(1)} %copy-done, f32[4,128,128]{2,1,0:T(8,128)S(1)} %get-tuple-element.36.coef.old), custom_call_target="tpu_custom_call" | custom-call | flops 11816960 | bytes 2363392 | tf_op jit(solution)/shard_map/pallas_call | solution.py:22
  9.1 0.1 collective-permute-start.7
  9.2 2.4 %collective-permute-start.8 = (f32[2,128,128]{2,1,0:T(8,128)S(1)}, f32[2,128,128]{2,1,0:T(8,128)S(1)}, u32[]{:S(2)}, u32[]{:S(2)}) collective-permute-start(f32[2,128,128]{2,1,0:T(8,128)S(1)} %get-tuple-element.49), channel_id=1, source_target_pairs={{0,4},{1,2},{2,1},{3,7},{4,0},{5,6},{6,5},{7,3},{8,12},{9,10},{10,... | collective-permute-start | bytes 393224 | tf_op jit(solution)/shard_map/ppermute | solution.py:548
  11.6 0.0 collective-permute-done.2.de
  11.6 0.0 collective-permute-done.3.do
  11.6 0.0 collective-permute-done.4.other
  11.6 0.6 %shard_map.63 = (f32[264,128]{1,0:T(8,128)S(1)}, f32[2,128,128]{2,1,0:T(8,128)S(1)}, f32[2,2,128,128]{3,2,1,0:T(8,128)S(1)}, f32[2,4,128,128]{3,2,1,0:T(8,128)S(...) custom-call(f32[8,128]{1,0:T(8,128)S(1)} %get-tuple-element.35.w.refs_0_, ...), custom_call_target="tpu_custom_call" | custom-call | flops 21667840 | bytes 4333568 | tf_op jit(solution)/shard_map/pallas_call | solution.py:22
  12.2 0.6 %collective-permute-start.5 = (f32[264,128]{1,0:T(8,128)S(1)}, f32[264,128]{1,0:T(8,128)S(1)}, u32[]{:S(2)}, u32[]{:S(2)}) collective-permute-start(f32[264,128]{1,0:T(8,128)S(1)} %get-tuple-element.43.labels.mine), channel_id=1, source_target_pairs={{0,8},{4,12},{8,0},{12,4},{1,9},{5,13},{9,1},{13,5},{2,10},{6,14},... | collective-permute-start | bytes 405512 | tf_op jit(solution)/shard_map/ppermute | solution.py:557
  12.8 2.2 %collective-permute-done.7.be = f32[2,128,128]{2,1,0:T(8,128)S(1)} collective-permute-done((f32[2,128,128]{2,1,0:T(8,128)S(1)}, f32[2,128,128]{2,1,0:T(8,128)S(1)}, u32[]{:S(2)}, u32[]{:S(2)}) %collective-permute-start.7) | collective-permute-done | bytes 131104 | tf_op jit(solution)/shard_map/ppermute | solution.py:548
  15.1 0.5 %collective-permute-done.8.bo = f32[2,128,128]{2,1,0:T(8,128)S(1)} collective-permute-done((f32[2,128,128]{2,1,0:T(8,128)S(1)}, f32[2,128,128]{2,1,0:T(8,128)S(1)}, u32[]{:S(2)}, u32[]{:S(2)}) %collective-permute-start.8) | collective-permute-done | bytes 131104 | tf_op jit(solution)/shard_map/ppermute | solution.py:548
  15.6 0.3 shard_map.65
  15.9 0.6 %collective-permute-start.9 = (f32[256,128]{1,0:T(8,128)S(1)}, f32[256,128]{1,0:T(8,128)S(1)}, u32[]{:S(2)}, u32[]{:S(2)}) collective-permute-start(f32[256,128]{1,0:T(8,128)S(1)} %get-tuple-element.50.mine), channel_id=1, source_target_pairs={{0,8},{4,12},{8,0},{12,4},{1,9},{5,13},{9,1},{13,5},{2,10},{6,14},... | collective-permute-start | bytes 393224 | tf_op jit(solution)/shard_map/ppermute | solution.py:557
  16.5 4.6 %collective-permute-done.9.other = f32[256,128]{1,0:T(8,128)S(1)} collective-permute-done((f32[256,128]{1,0:T(8,128)S(1)}, f32[256,128]{1,0:T(8,128)S(1)}, u32[]{:S(2)}, u32[]{:S(2)}) %collective-permute-start.9) | collective-permute-done | bytes 131104 | tf_op jit(solution)/shard_map/ppermute | solution.py:557
  21.1 0.0 collective-permute-done.5.far_labels.other
  21.1 0.1 collective-permute-start.10
  21.3 0.6 %collective-permute-start.6 = (f32[2,2,128,128]{3,2,1,0:T(8,128)S(1)}, f32[2,2,128,128]{3,2,1,0:T(8,128)S(1)}, u32[]{:S(2)}, u32[]{:S(2)}) collective-permute-start(f32[2,2,128,128]{3,2,1,0:T(8,128)S(1)} %shard_map.64.refs_1_.refs_0_), channel_id=1, source_target_pairs={{0,4},{4,0},{8,12},{12,8},{1,5},{5,1},{9,13},{13,9},{2,6},{6,2},{1... | collective-permute-start | bytes 786440 | tf_op jit(solution)/shard_map/ppermute | solution.py:557
  21.8 0.2 shard_map.69
  22.0 0.1 collective-permute-start.13
  22.1 2.1 %collective-permute-start.11 = (f32[4,128,128]{2,1,0:T(8,128)S(1)}, f32[4,128,128]{2,1,0:T(8,128)S(1)}, u32[]{:S(2)}, u32[]{:S(2)}) collective-permute-start(f32[4,128,128]{2,1,0:T(8,128)S(1)} %get-tuple-element.57), channel_id=1, source_target_pairs={{0,1},{1,0},{2,3},{3,2},{4,5},{5,4},{6,7},{7,6},{8,9},{9,8},{10,11... | collective-permute-start | bytes 786440 | tf_op jit(solution)/shard_map/ppermute | solution.py:548
  24.2 1.6 %collective-permute-start.12 = (f32[4,128,128]{2,1,0:T(8,128)S(1)}, f32[4,128,128]{2,1,0:T(8,128)S(1)}, u32[]{:S(2)}, u32[]{:S(2)}) collective-permute-start(f32[4,128,128]{2,1,0:T(8,128)S(1)} %get-tuple-element.58), channel_id=1, source_target_pairs={{0,4},{1,2},{2,1},{3,7},{4,0},{5,6},{6,5},{7,3},{8,12},{9,10},{10,... | collective-permute-start | bytes 786440 | tf_op jit(solution)/shard_map/ppermute | solution.py:548
  25.8 0.0 collective-permute-done.10.refs_4_.refs_3_
  25.8 0.5 %collective-permute-start.14 = (f32[3,128,128]{2,1,0:T(8,128)S(1)}, f32[3,128,128]{2,1,0:T(8,128)S(1)}, u32[]{:S(2)}, u32[]{:S(2)}) collective-permute-start(f32[3,128,128]{2,1,0:T(8,128)S(1)} %get-tuple-element.60), channel_id=1, source_target_pairs={{0,4},{1,2},{2,1},{3,7},{4,0},{5,6},{6,5},{7,3},{8,12},{9,10},{10,... | collective-permute-start | bytes 589832 | tf_op jit(solution)/shard_map/ppermute | solution.py:548
  26.2 0.4 %shard_map.67.refs_5_.refs_4_ = f32[4,128,128]{2,1,0:T(8,128)S(1)} custom-call(f32[4,128,128]{2,1,0:T(8,128)S(1)} %copy-done.1, f32[4,128,128]{2,1,0:T(8,128)S(1)} %copy-done.2, f32[2,128,128]{2,1,0:T(8,128)S(1)} %collective-permute-done.even.ae, f32[2,128,128]{2,1,0:T(8,128)S(1)} %collective-permute-done.1.odd.ao, ...), custom_call_target="tpu_custom_call" | custom-call | flops 5898240 | bytes 1179648 | tf_op jit(solution)/shard_map/pallas_call | solution.py:22
  26.7 0.0 collective-permute-done.6.refs_2_.refs_1_
  26.7 0.2 shard_map.68
  26.8 0.1 collective-permute-start.15
  26.9 2.9 %collective-permute-done.13.we = f32[3,128,128]{2,1,0:T(8,128)S(1)} collective-permute-done((f32[3,128,128]{2,1,0:T(8,128)S(1)}, f32[3,128,128]{2,1,0:T(8,128)S(1)}, u32[]{:S(2)}, u32[]{:S(2)}) %collective-permute-start.13) | collective-permute-done | bytes 196640 | tf_op jit(solution)/shard_map/ppermute | solution.py:548
  29.8 1.6 %collective-permute-start.16 = (f32[2,128,128]{2,1,0:T(8,128)S(1)}, f32[2,128,128]{2,1,0:T(8,128)S(1)}, u32[]{:S(2)}, u32[]{:S(2)}) collective-permute-start(f32[2,128,128]{2,1,0:T(8,128)S(1)} %get-tuple-element.67), channel_id=1, source_target_pairs={{0,4},{1,2},{2,1},{3,7},{4,0},{5,6},{6,5},{7,3},{8,12},{9,10},{10,... | collective-permute-start | bytes 393224 | tf_op jit(solution)/shard_map/ppermute | solution.py:548
  31.4 1.0 %shard_map.73 = f32[2,4,128,128]{3,2,1,0:T(8,128)} custom-call(f32[2,2,128,128]{3,2,1,0:T(8,128)S(1)} %shard_map.64.refs_1_.refs_0_, f32[2,2,128,128]{3,2,1,0:T(8,128)S(1)} %collective-permute-done.6.refs_2_.refs_1_, f32[2,2,128,128]{3,2,1,0:T(8,128)S(1)} %shard_map.66.refs_3_.refs_2_, f32[2,2,128,128]{3,2,1,0:T(8,128)S(1)} %collective-permute-done.10.refs_4_.refs_3_, ...), custom_call_target="tpu_custom_call" | custom-call | flops 11796480 | bytes 2359296 | tf_op jit(solution)/shard_map/pallas_call | solution.py:22
  32.4 5.1 %collective-permute-done.14.wo = f32[3,128,128]{2,1,0:T(8,128)S(1)} collective-permute-done((f32[3,128,128]{2,1,0:T(8,128)S(1)}, f32[3,128,128]{2,1,0:T(8,128)S(1)}, u32[]{:S(2)}, u32[]{:S(2)}) %collective-permute-start.14) | collective-permute-done | bytes 196640 | tf_op jit(solution)/shard_map/ppermute | solution.py:548
  37.5 0.0 collective-permute-done.11.ue
  37.5 0.0 collective-permute-done.12.uo
  37.5 1.8 %shard_map.71 = (f32[2,2,128,128]{3,2,1,0:T(8,128)S(1)}, f32[2,4,128,128]{3,2,1,0:T(8,128)S(1)}, f32[2,2,2,128,128]{4,3,2,1,0:T(8,128)S(1)}, f32[2,2,2,128,128]{4,3,2,1,0:T(8,128)S(1)}, f32[2,2,128,128]{3,2,1,0:T(8,128)S(1)}) custom-call(f32[8,128]{1,0:T(8,128)S(1)} %get-tuple-element.35.w.refs_0_, f32[4,128,128]{2,1,0:T(8,128)S(1)} %get-tuple-element.51.coef, ...), custom_call_target="tpu_custom_call" | custom-call | flops 27545600 | bytes 5509120 | tf_op jit(solution)/shard_map/pallas_call | solution.py:22
  39.3 0.0 collective-permute-done.15.e
  39.3 0.0 collective-permute-done.16.o
  39.3 1.2 %shard_map.72 = f32[1,2,4,128,128]{4,3,2,1,0:T(8,128)} custom-call(f32[8,128]{1,0:T(8,128)S(1)} %get-tuple-element.35.w.refs_0_, f32[4,128,128]{2,1,0:T(8,128)S(1)} %get-tuple-element.51.coef, f32[2,2,128,128]{3,2,1,0:T(8,128)S(1)} %get-tuple-element.61.rim, f32[2,4,128,128]{3,2,1,0:T(8,128)S(1)} %get-tuple-element.62.six, ...), custom_call_target="tpu_custom_call" | custom-call | flops 15749120 | bytes 3149824 | tf_op jit(solution)/shard_map/pallas_call | solution.py:22
  (7 shorter events, 0.1 us)
Async XLA Ops:
  0.6 5.0 %copy-start.2 = (f32[4,128,128]{2,1,0:T(8,128)S(1)}, f32[4,128,128]{2,1,0:T(8,128)}, u32[]{:S(2)}) copy-start(f32[4,128,128]{2,1,0:T(8,128)} %refs_6_.3) | copy-start | bytes 786436
  0.6 5.0 %copy-start.1 = (f32[4,128,128]{2,1,0:T(8,128)S(1)}, f32[4,128,128]{2,1,0:T(8,128)}, u32[]{:S(2)}) copy-start(f32[4,128,128]{2,1,0:T(8,128)} %refs_5_.1) | copy-start | bytes 786436
  0.6 5.0 %copy-start = (f32[1,4,4,128,128]{4,3,2,1,0:T(8,128)S(1)}, f32[1,4,4,128,128]{4,3,2,1,0:T(8,128)}, u32[]{:S(2)}) copy-start(f32[1,4,4,128,128]{4,3,2,1,0:T(8,128)} %f.7) | copy-start | bytes 3145732
  1.8 5.3 %collective-permute-start = (f32[2,128,128]{2,1,0:T(8,128)S(1)}, f32[2,128,128]{2,1,0:T(8,128)S(1)}, u32[]{:S(2)}, u32[]{:S(2)}) collective-permute-start(f32[2,128,128]{2,1,0:T(8,128)S(1)} %get-tuple-element.39), channel_id=1, source_target_pairs={{0,1},{1,0},{2,3},{3,2},{4,5},{5,4},{6,7},{7,6},{8,9},{9,8},{10,11... | collective-permute-start | bytes 393224 | tf_op jit(solution)/shard_map/ppermute | solution.py:548
  2.3 6.3 %collective-permute-start.1 = (f32[2,128,128]{2,1,0:T(8,128)S(1)}, f32[2,128,128]{2,1,0:T(8,128)S(1)}, u32[]{:S(2)}, u32[]{:S(2)}) collective-permute-start(f32[2,128,128]{2,1,0:T(8,128)S(1)} %get-tuple-element.40), channel_id=1, source_target_pairs={{0,4},{1,2},{2,1},{3,7},{4,0},{5,6},{6,5},{7,3},{8,12},{9,10},{10,... | collective-permute-start | bytes 393224 | tf_op jit(solution)/shard_map/ppermute | solution.py:548
  5.8 5.8 %collective-permute-start.2 = (f32[2,128,128]{2,1,0:T(8,128)S(1)}, f32[2,128,128]{2,1,0:T(8,128)S(1)}, u32[]{:S(2)}, u32[]{:S(2)}) collective-permute-start(f32[2,128,128]{2,1,0:T(8,128)S(1)} %get-tuple-element.41), channel_id=1, source_target_pairs={{0,1},{1,0},{2,3},{3,2},{4,5},{5,4},{6,7},{7,6},{8,9},{9,8},{10,11... | collective-permute-start | bytes 393224 | tf_op jit(solution)/shard_map/ppermute | solution.py:548
  5.9 5.7 %collective-permute-start.3 = (f32[2,128,128]{2,1,0:T(8,128)S(1)}, f32[2,128,128]{2,1,0:T(8,128)S(1)}, u32[]{:S(2)}, u32[]{:S(2)}) collective-permute-start(f32[2,128,128]{2,1,0:T(8,128)S(1)} %get-tuple-element.42), channel_id=1, source_target_pairs={{0,4},{1,2},{2,1},{3,7},{4,0},{5,6},{6,5},{7,3},{8,12},{9,10},{10,... | collective-permute-start | bytes 393224 | tf_op jit(solution)/shard_map/ppermute | solution.py:548
  8.5 3.1 %collective-permute-start.4 = (f32[2,128,128]{2,1,0:T(8,128)S(1)}, f32[2,128,128]{2,1,0:T(8,128)S(1)}, u32[]{:S(2)}, u32[]{:S(2)}) collective-permute-start(f32[2,128,128]{2,1,0:T(8,128)S(1)} %shard_map.62), channel_id=1, source_target_pairs={{0,4},{4,0},{8,12},{12,8},{1,5},{5,1},{9,13},{13,9},{2,6},{6,2},{1... | collective-permute-start | bytes 393224 | tf_op jit(solution)/shard_map/ppermute | solution.py:557
  9.1 6.0 %collective-permute-start.7 = (f32[2,128,128]{2,1,0:T(8,128)S(1)}, f32[2,128,128]{2,1,0:T(8,128)S(1)}, u32[]{:S(2)}, u32[]{:S(2)}) collective-permute-start(f32[2,128,128]{2,1,0:T(8,128)S(1)} %get-tuple-element.48), channel_id=1, source_target_pairs={{0,1},{1,0},{2,3},{3,2},{4,5},{5,4},{6,7},{7,6},{8,9},{9,8},{10,11... | collective-permute-start | bytes 393224 | tf_op jit(solution)/shard_map/ppermute | solution.py:548
  9.2 6.4 %collective-permute-start.8 = (f32[2,128,128]{2,1,0:T(8,128)S(1)}, f32[2,128,128]{2,1,0:T(8,128)S(1)}, u32[]{:S(2)}, u32[]{:S(2)}) collective-permute-start(f32[2,128,128]{2,1,0:T(8,128)S(1)} %get-tuple-element.49), channel_id=1, source_target_pairs={{0,4},{1,2},{2,1},{3,7},{4,0},{5,6},{6,5},{7,3},{8,12},{9,10},{10,... | collective-permute-start | bytes 393224 | tf_op jit(solution)/shard_map/ppermute | solution.py:548
  12.2 8.9 %collective-permute-start.5 = (f32[264,128]{1,0:T(8,128)S(1)}, f32[264,128]{1,0:T(8,128)S(1)}, u32[]{:S(2)}, u32[]{:S(2)}) collective-permute-start(f32[264,128]{1,0:T(8,128)S(1)} %get-tuple-element.43.labels.mine), channel_id=1, source_target_pairs={{0,8},{4,12},{8,0},{12,4},{1,9},{5,13},{9,1},{13,5},{2,10},{6,14},... | collective-permute-start | bytes 405512 | tf_op jit(solution)/shard_map/ppermute | solution.py:557
  15.9 5.2 %collective-permute-start.9 = (f32[256,128]{1,0:T(8,128)S(1)}, f32[256,128]{1,0:T(8,128)S(1)}, u32[]{:S(2)}, u32[]{:S(2)}) collective-permute-start(f32[256,128]{1,0:T(8,128)S(1)} %get-tuple-element.50.mine), channel_id=1, source_target_pairs={{0,8},{4,12},{8,0},{12,4},{1,9},{5,13},{9,1},{13,5},{2,10},{6,14},... | collective-permute-start | bytes 393224 | tf_op jit(solution)/shard_map/ppermute | solution.py:557
  21.1 4.6 %collective-permute-start.10 = (f32[2,2,128,128]{3,2,1,0:T(8,128)S(1)}, f32[2,2,128,128]{3,2,1,0:T(8,128)S(1)}, u32[]{:S(2)}, u32[]{:S(2)}) collective-permute-start(f32[2,2,128,128]{3,2,1,0:T(8,128)S(1)} %shard_map.66.refs_3_.refs_2_), channel_id=1, source_target_pairs={{0,4},{4,0},{8,12},{12,8},{1,5},{5,1},{9,13},{13,9},{2,6},{6,2},{1... | collective-permute-start | bytes 786440 | tf_op jit(solution)/shard_map/ppermute | solution.py:557
  21.3 5.4 %collective-permute-start.6 = (f32[2,2,128,128]{3,2,1,0:T(8,128)S(1)}, f32[2,2,128,128]{3,2,1,0:T(8,128)S(1)}, u32[]{:S(2)}, u32[]{:S(2)}) collective-permute-start(f32[2,2,128,128]{3,2,1,0:T(8,128)S(1)} %shard_map.64.refs_1_.refs_0_), channel_id=1, source_target_pairs={{0,4},{4,0},{8,12},{12,8},{1,5},{5,1},{9,13},{13,9},{2,6},{6,2},{1... | collective-permute-start | bytes 786440 | tf_op jit(solution)/shard_map/ppermute | solution.py:557
  22.0 7.8 %collective-permute-start.13 = (f32[3,128,128]{2,1,0:T(8,128)S(1)}, f32[3,128,128]{2,1,0:T(8,128)S(1)}, u32[]{:S(2)}, u32[]{:S(2)}) collective-permute-start(f32[3,128,128]{2,1,0:T(8,128)S(1)} %get-tuple-element.59), channel_id=1, source_target_pairs={{0,1},{1,0},{2,3},{3,2},{4,5},{5,4},{6,7},{7,6},{8,9},{9,8},{10,11... | collective-permute-start | bytes 589832 | tf_op jit(solution)/shard_map/ppermute | solution.py:548
  22.1 15.4 %collective-permute-start.11 = (f32[4,128,128]{2,1,0:T(8,128)S(1)}, f32[4,128,128]{2,1,0:T(8,128)S(1)}, u32[]{:S(2)}, u32[]{:S(2)}) collective-permute-start(f32[4,128,128]{2,1,0:T(8,128)S(1)} %get-tuple-element.57), channel_id=1, source_target_pairs={{0,1},{1,0},{2,3},{3,2},{4,5},{5,4},{6,7},{7,6},{8,9},{9,8},{10,11... | collective-permute-start | bytes 786440 | tf_op jit(solution)/shard_map/ppermute | solution.py:548
  24.2 13.3 %collective-permute-start.12 = (f32[4,128,128]{2,1,0:T(8,128)S(1)}, f32[4,128,128]{2,1,0:T(8,128)S(1)}, u32[]{:S(2)}, u32[]{:S(2)}) collective-permute-start(f32[4,128,128]{2,1,0:T(8,128)S(1)} %get-tuple-element.58), channel_id=1, source_target_pairs={{0,4},{1,2},{2,1},{3,7},{4,0},{5,6},{6,5},{7,3},{8,12},{9,10},{10,... | collective-permute-start | bytes 786440 | tf_op jit(solution)/shard_map/ppermute | solution.py:548
  25.8 11.7 %collective-permute-start.14 = (f32[3,128,128]{2,1,0:T(8,128)S(1)}, f32[3,128,128]{2,1,0:T(8,128)S(1)}, u32[]{:S(2)}, u32[]{:S(2)}) collective-permute-start(f32[3,128,128]{2,1,0:T(8,128)S(1)} %get-tuple-element.60), channel_id=1, source_target_pairs={{0,4},{1,2},{2,1},{3,7},{4,0},{5,6},{6,5},{7,3},{8,12},{9,10},{10,... | collective-permute-start | bytes 589832 | tf_op jit(solution)/shard_map/ppermute | solution.py:548
  26.8 12.5 %collective-permute-start.15 = (f32[2,128,128]{2,1,0:T(8,128)S(1)}, f32[2,128,128]{2,1,0:T(8,128)S(1)}, u32[]{:S(2)}, u32[]{:S(2)}) collective-permute-start(f32[2,128,128]{2,1,0:T(8,128)S(1)} %get-tuple-element.66), channel_id=1, source_target_pairs={{0,1},{1,0},{2,3},{3,2},{4,5},{5,4},{6,7},{7,6},{8,9},{9,8},{10,11... | collective-permute-start | bytes 393224 | tf_op jit(solution)/shard_map/ppermute | solution.py:548
  29.8 9.5 %collective-permute-start.16 = (f32[2,128,128]{2,1,0:T(8,128)S(1)}, f32[2,128,128]{2,1,0:T(8,128)S(1)}, u32[]{:S(2)}, u32[]{:S(2)}) collective-permute-start(f32[2,128,128]{2,1,0:T(8,128)S(1)} %get-tuple-element.67), channel_id=1, source_target_pairs={{0,4},{1,2},{2,1},{3,7},{4,0},{5,6},{6,5},{7,3},{8,12},{9,10},{10,... | collective-permute-start | bytes 393224 | tf_op jit(solution)/shard_map/ppermute | solution.py:548
